TPU v7x, 256 devices: a whole 4x4x8 slice. The times are simulated.
256 devices in a mesh: req: 64 (over x, z, y_lo), kv: 4 (over y_hi, core).
Axes of the slice: x: 4, y: 4 (y_hi: 2, y_lo: 2; y = y_hi * 2 + y_lo), z: 8, core: 2. Of those that a mesh axis runs over, the one named last changes fastest.
Arguments:
- hidden: bfloat16 [64, 1024, 1536], P('req', 'kv'), may hold values from -6 to 6
- lengths: int32 [64], P('req'), may hold values from 1 to 2048, as said below
- key_cache: bfloat16 [64, 2048, 768], P('req', 'kv'), may hold values from -180 to 180
- value_cache: bfloat16 [64, 2048, 768], P('req', 'kv'), may hold values from -6 to 6
- norm_gain: bfloat16 [1536], replicated, may hold values from 0.099609375 to 1.8984375
- w_query: bfloat16 [1536, 1536], P('req', 'kv'), may hold values from -0.15625 to 0.15625
- w_key: bfloat16 [1536, 768], P('req', 'kv'), may hold values from -0.15625 to 0.15625
- w_value: bfloat16 [1536, 768], P('req', 'kv'), may hold values from -0.15625 to 0.15625
- w_out: bfloat16 [1536, 1536], P('req', 'kv'), may hold values from -0.15625 to 0.15625
Outputs:
- attended: bfloat16 [64, 1024, 1536], P('req', 'kv')
- new_keys: bfloat16 [64, 1024, 768], P('req', 'kv')
- new_values: bfloat16 [64, 1024, 768], P('req', 'kv')
Inputs may be any that keep to these rules, and one draw needn't show every extreme that they name: `lengths`: at least a quarter of the requests (one or more) hold more than 1792 tokens, one of them exactly 2048; the others hold fewer than 512.
All inputs are finite; a program needn't handle non-finite values.
Results may differ from a plain program's by a relative error of at most 0.011.
Values may be sent and summed in bfloat16 or wider, within the bound.
A program may use at most 192 MiB of HBM per device.

v0:
```python
import jax
import jax.numpy as jnp
from jax import lax
from jax.sharding import PartitionSpec as P

H = 16
KVH = 8
HD = 96


rope_base = 100000.0
masked_score = -1e30


def rms_norm(states, gain):
    mean_square = jnp.mean(states * states, axis=-1, keepdims=True)
    scaled = states * lax.rsqrt(mean_square + 1e-05) * gain.astype(jnp.float32)
    return scaled.astype(jnp.bfloat16)


def rotate(values, positions):
    count = values.shape[0]
    heads = values.shape[1] // HD
    half = HD // 2
    frequency = rope_base ** (-(jnp.arange(half, dtype=jnp.float32) * 2.0 / HD))
    angle = positions[:, None] * frequency[None, :]
    cosine = jnp.cos(angle)[:, None, :]
    sine = jnp.sin(angle)[:, None, :]
    shaped = values.reshape(count, heads, HD)
    first = shaped[..., :half]
    second = shaped[..., half:]
    turned = jnp.concatenate(
        [first * cosine - second * sine, second * cosine + first * sine], axis=-1
    )
    return turned.reshape(count, heads * HD)


def fold_three(inputs, pieces):
    return tuple((jnp.dot(inputs, piece, preferred_element_type=jnp.float32) for piece in pieces))


def fold_single(inputs, piece):
    return jnp.dot(inputs, piece, preferred_element_type=jnp.float32)


def combine_blocks(blocks, share):
    block_count = blocks.shape[0]
    count = blocks.shape[1]
    numerator = jnp.zeros((count, H, HD), jnp.float32)
    for block in range(block_count):
        weight_rows = jnp.transpose(share[block])[:, :, None]
        numerator = (
            numerator + blocks[block].reshape(count, H, HD).astype(jnp.float32) * weight_rows
        )
    denominator = jnp.transpose(jnp.sum(share, axis=0))[:, :, None]
    return (numerator / denominator).reshape(count, H * HD).astype(jnp.bfloat16)


def body(hidden, lengths, key_cache, value_cache, norm_gain, w_query, w_key, w_value, w_out):
    rows_here = hidden.shape[1]
    width = hidden.shape[2]
    kv_count = lax.axis_size("kv")
    kv_index = lax.axis_index("kv")
    appended = rows_here * kv_count
    slots = key_cache.shape[1]
    groups = H // KVH
    scale = HD ** (-0.5)
    length = lengths[0]
    normed = rms_norm(hidden[0].astype(jnp.float32), norm_gain)
    query_cols, key_cols, value_cols = (
        lax.all_gather(w_query, "kv", axis=1, tiled=True),
        lax.all_gather(w_key, "kv", axis=1, tiled=True),
        lax.all_gather(w_value, "kv", axis=1, tiled=True),
    )
    proj_query, proj_key, proj_value = fold_three(
        normed,
        (
            lax.all_gather(query_cols, "req", axis=0, tiled=True),
            lax.all_gather(key_cols, "req", axis=0, tiled=True),
            lax.all_gather(value_cols, "req", axis=0, tiled=True),
        ),
    )
    positions = (length + kv_index * rows_here + jnp.arange(rows_here, dtype=jnp.int32)).astype(
        jnp.float32
    )
    queries_here = rotate(proj_query, positions).astype(jnp.bfloat16)
    new_keys = rotate(proj_key, positions).astype(jnp.bfloat16)
    new_values = proj_value.astype(jnp.bfloat16)
    queries = lax.all_gather(queries_here, "kv", axis=0, tiled=True)
    keys_all = jnp.concatenate([key_cache[0], new_keys], axis=0)
    values_all = jnp.concatenate([value_cache[0], new_values], axis=0)
    key_count = keys_all.shape[0]
    query_index = jnp.arange(appended, dtype=jnp.int32)
    cache_live = kv_index * slots + jnp.arange(slots, dtype=jnp.int32) < length
    own_index = kv_index * rows_here + jnp.arange(rows_here, dtype=jnp.int32)
    visible = jnp.concatenate(
        [
            jnp.broadcast_to(cache_live[None, :], (appended, slots)),
            own_index[None, :] <= query_index[:, None],
        ],
        axis=1,
    )
    query_heads = jnp.transpose(queries.reshape(appended, KVH, groups, HD), (1, 0, 2, 3))
    key_heads = jnp.transpose(keys_all.reshape(key_count, KVH, HD), (1, 0, 2))
    value_heads = jnp.transpose(values_all.reshape(key_count, KVH, HD), (1, 0, 2))

    def attend(operands):
        query_block, key_block, value_block = operands
        score = (
            jnp.einsum("qgd,kd->gqk", query_block, key_block, preferred_element_type=jnp.float32)
            * scale
        )
        score = jnp.where(visible[None], score, masked_score)
        peak = jnp.max(score, axis=-1)
        weights = jnp.where(visible[None], jnp.exp(score - peak[..., None]), 0.0)
        total = jnp.sum(weights, axis=-1)
        context = jnp.einsum(
            "gqk,kd->qgd",
            weights.astype(jnp.bfloat16),
            value_block,
            preferred_element_type=jnp.float32,
        )
        divisor = jnp.transpose(jnp.maximum(total, 1.0))[:, :, None]
        return ((context / divisor).astype(jnp.bfloat16), peak, total)

    outputs, peaks, totals = lax.map(attend, (query_heads, key_heads, value_heads))
    block_output = jnp.transpose(outputs, (1, 0, 2, 3)).reshape(appended, width)
    peaks = peaks.reshape(H, appended)
    totals = totals.reshape(H, appended)
    peak_blocks, total_blocks = (
        lax.all_gather(peaks[None], "kv", axis=0, tiled=True),
        lax.all_gather(totals[None], "kv", axis=0, tiled=True),
    )
    peak_all = jnp.max(peak_blocks, axis=0)
    share = jnp.exp(peak_blocks - peak_all[None]) * total_blocks
    received = lax.all_to_all(block_output, "kv", split_axis=0, concat_axis=0, tiled=True)
    blocks_here = received.reshape(kv_count, rows_here, width)
    share_here = lax.dynamic_slice_in_dim(share, kv_index * rows_here, rows_here, 2)
    context_here = combine_blocks(blocks_here, share_here)
    out_cols = lax.all_gather(w_out, "kv", axis=1, tiled=True)
    result = fold_single(context_here, lax.all_gather(out_cols, "req", axis=0, tiled=True))
    return (result.astype(jnp.bfloat16)[None], new_keys[None], new_values[None])


def solution(mesh):
    return jax.shard_map(
        body,
        mesh=mesh,
        in_specs=(
            P("req", "kv", None),
            P("req"),
            P("req", "kv", None),
            P("req", "kv", None),
            P(),
            P("req", "kv"),
            P("req", "kv"),
            P("req", "kv"),
            P("req", "kv"),
        ),
        out_specs=(P("req", "kv", None), P("req", "kv", None), P("req", "kv", None)),
        check_vma=False,
    )
```

profile of v0, /device:TPU:16, one launch (start us, length us, event | category | flops | bytes accessed | tf_op | source)
XLA Modules:
  0.0 1278.3 jit_solution(5281821043887652498)
XLA Ops:
  7.2 7.5 all_gather.37
  14.8 7.0 all-gather.1
  22.6 6.9 all-gather
  31.7 1.4 fusion.36
  33.4 290.6 %all-gather.12.cloned.1.call-done = bf16[1536,1536]{1,0:T(8,128)(2,1)} async-done(((bf16[24,1536]{1,0:T(8,128)(2,1)}), bf16[1536,1536]{1,0:T(8,128)(2,1)}) %all-gather.12.cloned.1.call-update) | async-done | bytes 4718608 | tf_op jit(solution)/shard_map/all_gather | solution.py:78
  323.9 6.8 copy.49
  330.7 3.9 fusion.50
  335.9 7.5 all_gather.42
  344.7 279.0 %all-gather.10.cloned.1.call-done = bf16[1536,768]{1,0:T(8,128)(2,1)} async-done(((bf16[24,768]{1,0:T(8,128)(2,1)}), bf16[1536,768]{1,0:T(8,128)(2,1)}) %all-gather.10.cloned.1.call-update) | async-done | bytes 2359312 | tf_op jit(solution)/shard_map/all_gather | solution.py:79
  623.6 4.4 copy.48
  628.0 2.6 fusion.52
  631.5 292.6 %all-gather.8.cloned.1.call-done = bf16[1536,768]{1,0:T(8,128)(2,1)} async-done(((bf16[24,768]{1,0:T(8,128)(2,1)}), bf16[1536,768]{1,0:T(8,128)(2,1)}) %all-gather.8.cloned.1.call-update) | async-done | bytes 2359312 | tf_op jit(solution)/shard_map/all_gather | solution.py:80
  924.0 2.5 convolution_convert_fusion.1
  928.3 1.7 maximum_bitcast_fusion.1
  930.0 26.4 %all-gather.14.cloned.1.call-done = bf16[1024,1536]{0,1:T(8,128)(2,1)} async-done(((bf16[256,1536]{0,1:T(8,128)(2,1)}), bf16[1024,1536]{0,1:T(8,128)(2,1)}) %all-gather.14.cloned.1.call-update) | async-done | bytes 3145744 | tf_op jit(solution)/shard_map/all_gather | solution.py:89
  956.4 69.6 %while.14 = (s32[]{:T(128)}, bf16[8,1024,2,96]{1,3,2,0:T(8,128)(2,1)}, f32[8,2,1024]{2,1,0:T(2,128)}, f32[8,2,1024]{2,1,0:T(2,128)}, bf16[8,768,96]{1,2,0:T(8,12...) while((s32[]{:T(128)}, ...), condition=%wide.region_4.5_spmd, body=%wide.region_1.4_spmd.sunk | while | flops 624818176 | bytes 22407772 | solution.py:126
  956.4 2.5 fusion.68
  959.0 1.7 fusion.69
  961.2 3.9 fusion.70
  965.1 2.6 fusion.68
  967.7 1.7 fusion.69
  970.0 3.9 fusion.70
  973.8 2.5 fusion.68
  976.4 1.7 fusion.69
  978.7 3.9 fusion.70
  982.6 2.6 fusion.68
  985.1 1.7 fusion.69
  987.4 3.9 fusion.70
  991.3 2.6 fusion.68
  993.9 1.7 fusion.69
  996.1 3.9 fusion.70
  1000.0 2.6 fusion.68
  1002.6 1.7 fusion.69
  1004.8 3.9 fusion.70
  1008.7 2.5 fusion.68
  1011.2 1.7 fusion.69
  1013.5 3.9 fusion.70
  1017.4 2.6 fusion.68
  1019.9 1.7 fusion.69
  1022.2 3.9 fusion.70
  1026.1 4.8 all_to_all.6
  1030.9 2.0 copy.50
  1032.9 6.9 all-to-all-start
  1042.6 55.7 %all_gather.40 = f32[4,16,1024]{2,1,0:T(8,128)S(1)} all-gather(f32[1,16,1024]{2,1,0:T(8,128)S(1)} %broadcast_in_dim_reshape.6), channel_id=1, replica_groups=mesh['req'=64,'kv'=4] {'kv'}, dimensions={0}, use_global_device_ids=true | all-gather | bytes 327680 | tf_op jit(solution)/shard_map/all_gather | solution.py:131
  1098.2 8.7 all_gather.41
  1107.0 1.5 fusion.43
  1108.6 158.3 %all-gather.16.cloned.1.call-done = bf16[1536,1536]{1,0:T(8,128)(2,1)} async-done(((bf16[24,1536]{1,0:T(8,128)(2,1)}), bf16[1536,1536]{1,0:T(8,128)(2,1)}) %all-gather.16.cloned.1.call-update) | async-done | bytes 4718608 | tf_op jit(solution)/shard_map/all_gather | solution.py:141
  1266.9 4.9 fusion.33
  (78 shorter events, 15.4 us)
Async XLA Ops:
  7.2 316.8 %all-gather.12.cloned.1.call-start = ((), (), s32[]{:S(2)}) async-start(), calls=%async_computation.3 | async-start | bytes 4792320 | tf_op jit(solution)/shard_map/all_gather | solution.py:78
  14.8 608.9 %all-gather.10.cloned.1.call-start = ((), (), s32[]{:S(2)}) async-start(), calls=%async_computation.2 | async-start | bytes 2396160 | tf_op jit(solution)/shard_map/all_gather | solution.py:79
  22.5 901.5 %all-gather.8.cloned.1.call-start = ((), (), s32[]{:S(2)}) async-start(), calls=%async_computation.1 | async-start | bytes 2396160 | tf_op jit(solution)/shard_map/all_gather | solution.py:80
  30.3 926.1 %all-gather.14.cloned.1.call-start = ((), (), s32[]{:S(2)}) async-start(), calls=%async_computation.4 | async-start | bytes 3932160 | tf_op jit(solution)/shard_map/all_gather | solution.py:89
  33.3 301.2 %copy-start.4 = (f32[256,48]{0,1:T(8,128)}, f32[256,48]{0,1:T(8,128)S(1)}, u32[]{:S(2)}) copy-start(f32[256,48]{0,1:T(8,128)S(1)} %get-tuple-element.92) | copy-start | bytes 147460
  33.3 301.2 %copy-start.6 = (f32[256,48]{0,1:T(8,128)}, f32[256,48]{0,1:T(8,128)S(1)}, u32[]{:S(2)}) copy-start(f32[256,48]{0,1:T(8,128)S(1)} %get-tuple-element.93) | copy-start | bytes 147460
  323.9 6.8 copy-start.2
  334.6 1.3 copy-start.9
  334.6 8.9 copy-start
  334.9 8.9 copy-start.1
  335.9 931.0 %all-gather.16.cloned.1.call-start = ((), (), s32[]{:S(2)}) async-start(), calls=%async_computation.5 | async-start | bytes 4792320 | tf_op jit(solution)/shard_map/all_gather | solution.py:141
  623.6 4.4 copy-start.3
  628.0 2.6 copy-start.5
  628.0 2.6 copy-start.7
  926.5 0.7 copy-start.8
  1032.9 74.1 %all-to-all-start = ((bf16[4,256,1536]{1,2,0:T(8,128)(2,1)}), bf16[4,256,1536]{1,2,0:T(8,128)(2,1)S(1)}, u32[]{:S(2)}, u32[]{:S(2)}) async-start(bf16[4,256,1536]{1,2,0:T(8,128)(2,1)} %copy.50), calls=%async_computation | async-start | bytes 6291456 | tf_op jit(solution)/shard_map/all_to_all | solution.py:136
Sparse Core Ops, SparseCore 0:
  14.9 308.9 all-gather.11
  325.7 297.8 all-gather.9
  625.4 298.5 all-gather.7
  926.2 30.1 all-gather.13
  958.1 308.7 all-gather.15
where the time goes:
time: 1280 us
  waiting for transfers between devices  1050 us (82%)
  blocking collectives  93.3 us (7%)
  matrix products  65.2 us (5%)
  local copies, waits for them, and re-layouts  28.3 us (2%)
  other arithmetic  22.5 us (2%)
  between operations  14.7 us (1%)
    all_gather x1, waiting for transfers between devices, body(): lax.all_gather(value_cols, 'req', axis=0, tiled=True)  293 us
    all_gather x1, waiting for transfers between devices, body(): lax.all_gather(query_cols, 'req', axis=0, tiled=True)  291 us
    all_gather x1, waiting for transfers between devices, body(): lax.all_gather(key_cols, 'req', axis=0, tiled=True)  279 us
    all_gather x1, waiting for transfers between devices, body(): lax.all_gather(out_cols, 'req', axis=0, tiled=True)  158 us
    all_gather x1, blocking collectives, body(): lax.all_gather(peaks[None], 'kv', axis=0, tiled=True)  55.7 us
    dot_general x8, matrix products, attend(): jnp.einsum('gqk,kd->qgd', weights.astype(jnp.bfloat16), value_block, pref...  31 us
    all_gather x1, waiting for transfers between devices, body(): queries = lax.all_gather(queries_here, 'kv', axis=0, tiled=True)  26.4 us
  transfers between devices with their start and end apart: 6, of which 5 were waited for; matrix products, arithmetic and copies ran while one was open for 8% of the time, Pallas kernels for 0%

commit v1 on v0

v1 whole, which is shorter than its diff:
```python
import jax
import jax.numpy as jnp
from jax import lax
from jax.sharding import PartitionSpec as P

H = 16
KVH = 8
HD = 96


rope_base = 100000.0
masked_score = -1e30


def rms_norm(states, gain):
    mean_square = jnp.mean(states * states, axis=-1, keepdims=True)
    scaled = states * lax.rsqrt(mean_square + 1e-05) * gain.astype(jnp.float32)
    return scaled.astype(jnp.bfloat16)


def rotate(values, positions):
    count = values.shape[0]
    heads = values.shape[1] // HD
    half = HD // 2
    frequency = rope_base ** (-(jnp.arange(half, dtype=jnp.float32) * 2.0 / HD))
    angle = positions[:, None] * frequency[None, :]
    cosine = jnp.cos(angle)[:, None, :]
    sine = jnp.sin(angle)[:, None, :]
    shaped = values.reshape(count, heads, HD)
    first = shaped[..., :half]
    second = shaped[..., half:]
    turned = jnp.concatenate(
        [first * cosine - second * sine, second * cosine + first * sine], axis=-1
    )
    return turned.reshape(count, heads * HD)


def body(hidden, lengths, key_cache, value_cache, norm_gain, w_query, w_key, w_value, w_out):
    rows_here = hidden.shape[1]
    kv_count = lax.axis_size("kv")
    appended = rows_here * kv_count
    slots = key_cache.shape[1]
    groups = H // KVH
    scale = HD ** (-0.5)
    length = lengths[0]
    q_cols = w_query.shape[1]
    k_cols = w_key.shape[1]
    v_cols = w_value.shape[1]
    heads_here = q_cols // HD
    kv_heads_here = k_cols // HD

    normed = rms_norm(hidden[0].astype(jnp.float32), norm_gain)
    normed_all = lax.all_gather(normed, "kv", axis=0, tiled=True)

    pieces = jnp.concatenate([w_query, w_key, w_value, w_out], axis=1)
    cols = lax.all_gather(pieces, "req", axis=0, tiled=True)
    wq = cols[:, :q_cols]
    wk = cols[:, q_cols:q_cols + k_cols]
    wv = cols[:, q_cols + k_cols:q_cols + k_cols + v_cols]
    wo = cols[:, q_cols + k_cols + v_cols:]

    positions = (length + jnp.arange(appended, dtype=jnp.int32)).astype(jnp.float32)
    proj_q = jnp.dot(normed_all, wq, preferred_element_type=jnp.float32)
    proj_k = jnp.dot(normed_all, wk, preferred_element_type=jnp.float32)
    proj_v = jnp.dot(normed_all, wv, preferred_element_type=jnp.float32)
    queries = rotate(proj_q, positions).astype(jnp.bfloat16)
    keys_new = rotate(proj_k, positions).astype(jnp.bfloat16)
    values_new = proj_v.astype(jnp.bfloat16)

    new_keys = lax.all_to_all(keys_new, "kv", split_axis=0, concat_axis=1, tiled=True)
    new_values = lax.all_to_all(values_new, "kv", split_axis=0, concat_axis=1, tiled=True)

    keys_old = lax.all_to_all(key_cache[0], "kv", split_axis=1, concat_axis=0, tiled=True)
    values_old = lax.all_to_all(value_cache[0], "kv", split_axis=1, concat_axis=0, tiled=True)
    cache_slots = keys_old.shape[0]

    keys_all = jnp.concatenate([keys_old, keys_new], axis=0)
    values_all = jnp.concatenate([values_old, values_new], axis=0)
    key_count = keys_all.shape[0]
    query_index = jnp.arange(appended, dtype=jnp.int32)
    cache_live = jnp.arange(cache_slots, dtype=jnp.int32) < length
    visible = jnp.concatenate(
        [
            jnp.broadcast_to(cache_live[None, :], (appended, cache_slots)),
            query_index[None, :] <= query_index[:, None],
        ],
        axis=1,
    )
    query_heads = jnp.transpose(
        queries.reshape(appended, kv_heads_here, groups, HD), (1, 0, 2, 3)
    )
    key_heads = jnp.transpose(keys_all.reshape(key_count, kv_heads_here, HD), (1, 0, 2))
    value_heads = jnp.transpose(values_all.reshape(key_count, kv_heads_here, HD), (1, 0, 2))

    def attend(operands):
        query_block, key_block, value_block = operands
        score = (
            jnp.einsum("qgd,kd->gqk", query_block, key_block, preferred_element_type=jnp.float32)
            * scale
        )
        score = jnp.where(visible[None], score, masked_score)
        peak = jnp.max(score, axis=-1)
        weights = jnp.where(visible[None], jnp.exp(score - peak[..., None]), 0.0)
        total = jnp.sum(weights, axis=-1)
        context = jnp.einsum(
            "gqk,kd->qgd",
            weights.astype(jnp.bfloat16),
            value_block,
            preferred_element_type=jnp.float32,
        )
        return context / jnp.transpose(total)[:, :, None]

    contexts = lax.map(attend, (query_heads, key_heads, value_heads))
    context = (
        jnp.transpose(contexts, (1, 0, 2, 3)).reshape(appended, heads_here * HD).astype(jnp.bfloat16)
    )
    context_all = lax.all_gather(context, "kv", axis=1, tiled=True)
    attended_cols = jnp.dot(context_all, wo, preferred_element_type=jnp.float32).astype(jnp.bfloat16)
    attended = lax.all_to_all(attended_cols, "kv", split_axis=0, concat_axis=1, tiled=True)
    return (attended[None], new_keys[None], new_values[None])


def solution(mesh):
    return jax.shard_map(
        body,
        mesh=mesh,
        in_specs=(
            P("req", "kv", None),
            P("req"),
            P("req", "kv", None),
            P("req", "kv", None),
            P(),
            P("req", "kv"),
            P("req", "kv"),
            P("req", "kv"),
            P("req", "kv"),
        ),
        out_specs=(P("req", "kv", None), P("req", "kv", None), P("req", "kv", None)),
        check_vma=False,
    )
```

time: 1280 us -> 497 us (0.39)
  the two profiles are of different devices: /device:TPU:16 before, /device:TPU:1 now
where the time goes in v1:
time: 497 us; the launch traced here: 496 us
  waiting for transfers between devices  319 us (64%)
  starting transfers between devices  68.6 us (14%)
  matrix products  65.6 us (13%)
  local copies, waits for them, and re-layouts  16 us (3%)
  between operations  14.6 us (3%)
  other arithmetic  12.3 us (2%)
    all_gather x1, waiting for transfers between devices, body(): cols = lax.all_gather(pieces, 'req', axis=0, tiled=True)  259 us
    all_to_all x1, starting transfers between devices, body(): lax.all_to_all(keys_new, 'kv', split_axis=0, concat_axis=1, tiled=True)  48.5 us
    sub x2, matrix products, attend(): weights = jnp.where(visible[None], jnp.exp(score - peak[..., None]), 0.0)  38.6 us
    all_gather x1, waiting for transfers between devices, body(): context_all = lax.all_gather(context, 'kv', axis=1, tiled=True)  18.9 us
    all_to_all x1, waiting for transfers between devices, body(): lax.all_to_all(value_cache[0], 'kv', split_axis=1, concat_axis=0, tiled=T...  14.8 us
    dot_general x2, matrix products, attend(): jnp.einsum('gqk,kd->qgd', weights.astype(jnp.bfloat16), value_block, pref...  13.4 us
    all_to_all x1, waiting for transfers between devices, body(): lax.all_to_all(attended_cols, 'kv', split_axis=0, concat_axis=1, tiled=True)  10.5 us
  transfers between devices with their start and end apart: 8, of which 6 were waited for; matrix products, arithmetic and copies ran while one was open for 4% of the time, Pallas kernels for 0%

profile of v1, /device:TPU:1, one launch (start us, length us, event | category | flops | bytes accessed | tf_op | source)
XLA Modules:
  0.0 496.3 jit_solution(3980875130991210258)
XLA Ops:
  7.3 0.8 convert_element_type.52
  8.0 1.4 fusion.49
  9.5 2.3 fusion.51
  11.9 0.7 concatenate.28
  12.6 1.2 copy.38
  13.8 6.7 %all-to-all-start.1 = ((bf16[512,4,192]{0,2,1:T(8,128)(2,1)}), bf16[512,4,192]{0,2,1:T(8,128)(2,1)S(1)}, u32[]{:S(2)}, u32[]{:S(2)}) async-start(bf16[512,4,192]{0,2,1:T(8,128)(2,1)} %bitcast.16), calls=%async_computation.1 | async-start | bytes 1572864 | tf_op jit(solution)/shard_map/all_to_all | solution.py:73
  21.2 1.2 copy.36
  22.4 0.3 iota_compare_fusion
  22.7 1.5 multiply_cosine_fusion
  24.2 8.6 %all-to-all-done.1 = bf16[512,4,192]{0,2,1:T(8,128)(2,1)S(1)} async-done(((bf16[512,4,192]{0,2,1:T(8,128)(2,1)}), bf16[512,4,192]{0,2,1:T(8,128)(2,1)S(1)}, u32[]{:S(2)}, u32[]{:S(2)}) %all-to-all-start.1) | async-done | bytes 786464 | tf_op jit(solution)/shard_map/all_to_all | solution.py:73
  32.8 5.2 %all-to-all-start = ((bf16[512,4,192]{0,2,1:T(8,128)(2,1)}), bf16[512,4,192]{0,2,1:T(8,128)(2,1)S(1)}, u32[]{:S(2)}, u32[]{:S(2)}) async-start(bf16[512,4,192]{0,2,1:T(8,128)(2,1)} %bitcast.9), calls=%async_computation | async-start | bytes 1572864 | tf_op jit(solution)/shard_map/all_to_all | solution.py:74
  38.0 3.5 pad_add_fusion
  41.5 0.6 copy.39
  42.1 1.5 concatenate.32
  43.6 14.8 %all-to-all-done = bf16[512,4,192]{0,2,1:T(8,128)(2,1)S(1)} async-done(((bf16[512,4,192]{0,2,1:T(8,128)(2,1)}), bf16[512,4,192]{0,2,1:T(8,128)(2,1)S(1)}, u32[]{:S(2)}, u32[]{:S(2)}) %all-to-all-start) | async-done | bytes 786464 | tf_op jit(solution)/shard_map/all_to_all | solution.py:74
  58.4 0.6 copy.37
  59.0 1.5 concatenate.27
  60.5 259.1 %all-gather.6.cloned.1.call-done = bf16[1536,1152]{1,0:T(8,128)(2,1)} async-done(((bf16[24,1152]{1,0:T(8,128)(2,1)}), bf16[1536,1152]{1,0:T(8,128)(2,1)}) %all-gather.6.cloned.1.call-update) | async-done | bytes 3538960 | tf_op jit(solution)/shard_map/all_gather | solution.py:56
  319.5 3.3 fusion.55
  322.8 0.1 multiply_subtract_fusion
  323.0 2.7 fusion.53
  325.7 0.3 subtract_convert_fusion
  326.0 0.8 copy-done.1
  326.8 1.1 maximum_bitcast_fusion.1
  327.9 0.9 pad_maximum_fusion
  328.8 2.7 convolution_convert_fusion.1
  331.6 0.6 copy-done.5
  332.3 53.8 %while.10 = (s32[]{:T(128)}, bf16[2,1024,2,96]{1,3,2,0:T(8,128)(2,1)}, bf16[2,3072,96]{1,2,0:T(8,128)(2,1)S(1)}, pred[1024,3072]{0,1:T(8,128)(4,1)}, bf16[2,3072...) while((s32[]{:T(128)}, bf16[2,1024,2,96]{1,3,2,0:T(8,128)(2,1)}, ...), condition=%wide.region_4.5_spmd, body=%wide.region_1.4_spmd.sunk | while | flops 2453867520 | bytes 40126596 | solution.py:113
  332.3 19.3 %fusion.82 = (f32[2,1024]{1,0:T(2,128)S(1)}, bf16[2,1024,3072]{1,2,0:T(8,128)(2,1)}) fusion(pred[1024,3072]{0,1:T(8,128)(4,1)} %get-tuple-element.125, bf16[2,3072,96]{1,2,0:T(8,128)(2,1)} %get-tuple-element.126, s32[]{:T(128)} %get-tuple-element.115, bf16[2,1024,2,96]{1,3,2,0:T(8,128)(2,1)} %get-tuple-element.127), kind=kOutput, calls=%fused_computation.60.clone.1 | convolution fusion | flops 1245711360 | bytes 19866624 | tf_op jit(solution)/shard_map/while/body/eval_jaxpr/sub | solution.py:103
  351.6 6.7 %fusion.83 = bf16[2,1024,2,96]{1,3,2,0:T(8,128)(2,1)S(1)} fusion(bf16[2,1024,2,96]{1,3,2,0:T(8,128)(2,1)S(1)} %copy-done.9, s32[]{:T(128)} %get-tuple-element.115, bf16[2,1024,3072]{1,2,0:T(8,128)(2,1)} %get-tuple-element.106, bf16[2,3072,96]{1,2,0:T(8,128)(2,1)S(1)} %get-tuple-element.124, f32[1024,2]{0,1:T(2,128)S(1)} %bitcast.127), kind=kOutput, calls=%fused_computation.13.clone.1 | convolution fusion | flops 1208156160 | bytes 13968384 | tf_op jit(solution)/shard_map/while/body/eval_jaxpr/gqk,kd->qgd/dot_general | solution.py:105
  358.3 0.9 copy-done.10
  359.2 19.3 %fusion.82 = (f32[2,1024]{1,0:T(2,128)S(1)}, bf16[2,1024,3072]{1,2,0:T(8,128)(2,1)}) fusion(pred[1024,3072]{0,1:T(8,128)(4,1)} %get-tuple-element.125, bf16[2,3072,96]{1,2,0:T(8,128)(2,1)} %get-tuple-element.126, s32[]{:T(128)} %get-tuple-element.115, bf16[2,1024,2,96]{1,3,2,0:T(8,128)(2,1)} %get-tuple-element.127), kind=kOutput, calls=%fused_computation.60.clone.1 | convolution fusion | flops 1245711360 | bytes 19866624 | tf_op jit(solution)/shard_map/while/body/eval_jaxpr/sub | solution.py:103
  378.5 6.7 %fusion.83 = bf16[2,1024,2,96]{1,3,2,0:T(8,128)(2,1)S(1)} fusion(bf16[2,1024,2,96]{1,3,2,0:T(8,128)(2,1)S(1)} %copy-done.9, s32[]{:T(128)} %get-tuple-element.115, bf16[2,1024,3072]{1,2,0:T(8,128)(2,1)} %get-tuple-element.106, bf16[2,3072,96]{1,2,0:T(8,128)(2,1)S(1)} %get-tuple-element.124, f32[1024,2]{0,1:T(2,128)S(1)} %bitcast.127), kind=kOutput, calls=%fused_computation.13.clone.1 | convolution fusion | flops 1208156160 | bytes 13968384 | tf_op jit(solution)/shard_map/while/body/eval_jaxpr/gqk,kd->qgd/dot_general | solution.py:105
  385.2 0.9 copy-done.10
  386.1 0.3 convert_element_type.62
  386.4 0.8 copy.41
  387.2 48.5 %all-to-all-start.3 = ((bf16[4,256,192]{1,2,0:T(8,128)(2,1)}), bf16[4,256,192]{1,2,0:T(8,128)(2,1)S(1)}, u32[]{:S(2)}, u32[]{:S(2)}) async-start(bf16[4,256,192]{1,2,0:T(8,128)(2,1)} %copy.41), calls=%async_computation.3 | async-start | bytes 786432 | tf_op jit(solution)/shard_map/all_to_all | solution.py:70
  435.7 0.8 copy.48
  436.5 7.3 %all-to-all-done.3 = bf16[4,256,192]{1,2,0:T(8,128)(2,1)S(1)} async-done(((bf16[4,256,192]{1,2,0:T(8,128)(2,1)}), bf16[4,256,192]{1,2,0:T(8,128)(2,1)S(1)}, u32[]{:S(2)}, u32[]{:S(2)}) %all-to-all-start.3) | async-done | bytes 393248 | tf_op jit(solution)/shard_map/all_to_all | solution.py:70
  443.8 4.3 all-to-all-start.4
  448.1 18.9 %all-gather.8.cloned.1.call-done = bf16[1024,1536]{0,1:T(8,128)(2,1)} async-done(((bf16[1024,384]{0,1:T(8,128)(2,1)}), bf16[1024,1536]{0,1:T(8,128)(2,1)}) %all-gather.8.cloned.1.call-update) | async-done | bytes 3145744 | tf_op jit(solution)/shard_map/all_gather | solution.py:117
  467.0 4.9 convolution_convert_fusion
  471.9 3.7 all-to-all-start.2
  475.7 0.9 copy.43
  476.6 0.9 copy.44
  477.5 10.5 %all-to-all-done.2 = bf16[4,256,384]{2,1,0:T(8,128)(2,1)S(1)} async-done(((bf16[4,256,384]{2,1,0:T(8,128)(2,1)}), bf16[4,256,384]{2,1,0:T(8,128)(2,1)S(1)}, u32[]{:S(2)}, u32[]{:S(2)}) %all-to-all-start.2) | async-done | bytes 786464 | tf_op jit(solution)/shard_map/all_to_all | solution.py:119
  488.0 0.6 copy.40
  488.6 1.2 broadcast_in_dim.58
  (46 shorter events, 0.4 us)
Async XLA Ops:
  7.2 4.6 copy-start.11
  7.2 4.6 copy-start.13
  7.2 4.6 copy-start.14
  7.2 4.6 copy-start.12
  7.2 5.4 %copy-start.7 = (bf16[1,512,768]{2,1,0:T(8,128)(2,1)S(1)}, bf16[1,512,768]{2,1,0:T(8,128)(2,1)}, u32[]{:S(2)}) copy-start(bf16[1,512,768]{2,1,0:T(8,128)(2,1)} %param.13) | copy-start | bytes 2359300
  7.2 53.3 %all-gather.4.cloned.1.call-start = ((), (), s32[]{:S(2)}) async-start(), calls=%async_computation.5 | async-start | bytes 3932160 | tf_op jit(solution)/shard_map/all_gather | solution.py:53
  8.0 13.1 %copy-start.8 = (bf16[1,512,768]{2,1,0:T(8,128)(2,1)S(1)}, bf16[1,512,768]{2,1,0:T(8,128)(2,1)}, u32[]{:S(2)}) copy-start(bf16[1,512,768]{2,1,0:T(8,128)(2,1)} %param.14) | copy-start | bytes 2359300
  11.8 307.8 %all-gather.6.cloned.1.call-start = ((), (), s32[]{:S(2)}) async-start(), calls=%async_computation.6 | async-start | bytes 3594240 | tf_op jit(solution)/shard_map/all_gather | solution.py:56
  13.8 19.0 %all-to-all-start.1 = ((bf16[512,4,192]{0,2,1:T(8,128)(2,1)}), bf16[512,4,192]{0,2,1:T(8,128)(2,1)S(1)}, u32[]{:S(2)}, u32[]{:S(2)}) async-start(bf16[512,4,192]{0,2,1:T(8,128)(2,1)} %bitcast.16), calls=%async_computation.1 | async-start | bytes 1572864 | tf_op jit(solution)/shard_map/all_to_all | solution.py:73
  32.8 25.6 %all-to-all-start = ((bf16[512,4,192]{0,2,1:T(8,128)(2,1)}), bf16[512,4,192]{0,2,1:T(8,128)(2,1)S(1)}, u32[]{:S(2)}, u32[]{:S(2)}) async-start(bf16[512,4,192]{0,2,1:T(8,128)(2,1)} %bitcast.9), calls=%async_computation | async-start | bytes 1572864 | tf_op jit(solution)/shard_map/all_to_all | solution.py:74
  38.0 429.0 %all-gather.8.cloned.1.call-start = ((), (), s32[]{:S(2)}) async-start(), calls=%async_computation.7 | async-start | bytes 3932160 | tf_op jit(solution)/shard_map/all_gather | solution.py:117
  60.5 262.3 %copy-start.3 = (f32[1024,48]{0,1:T(8,128)S(1)}, f32[1024,48]{0,1:T(8,128)}, u32[]{:S(2)}) copy-start(f32[1024,48]{0,1:T(8,128)} %get-tuple-element.63) | copy-start | bytes 589828
  60.5 262.3 %copy-start.4 = (f32[1024,48]{0,1:T(8,128)S(1)}, f32[1024,48]{0,1:T(8,128)}, u32[]{:S(2)}) copy-start(f32[1024,48]{0,1:T(8,128)} %get-tuple-element.64) | copy-start | bytes 589828
  60.5 262.5 %copy-start = (bf16[1024,1536]{1,0:T(8,128)(2,1)S(1)}, bf16[1024,1536]{1,0:T(8,128)(2,1)}, u32[]{:S(2)}) copy-start(bf16[1024,1536]{1,0:T(8,128)(2,1)} %all-gather.4.cloned.1.call-done) | copy-start | bytes 9437188
  325.7 1.1 copy-start.1
  327.9 3.6 copy-start.2
  331.5 0.8 copy-start.5
  332.3 19.3 %copy-start.9 = (bf16[2,1024,2,96]{1,3,2,0:T(8,128)(2,1)S(1)}, bf16[2,1024,2,96]{1,3,2,0:T(8,128)(2,1)}, u32[]{:S(2)}) copy-start(bf16[2,1024,2,96]{1,3,2,0:T(8,128)(2,1)} %get-tuple-element.116) | copy-start | bytes 2359300 | tf_op jit(solution)/shard_map/while
  358.3 0.9 copy-start.10
  359.2 19.3 %copy-start.9 = (bf16[2,1024,2,96]{1,3,2,0:T(8,128)(2,1)S(1)}, bf16[2,1024,2,96]{1,3,2,0:T(8,128)(2,1)}, u32[]{:S(2)}) copy-start(bf16[2,1024,2,96]{1,3,2,0:T(8,128)(2,1)} %get-tuple-element.116) | copy-start | bytes 2359300 | tf_op jit(solution)/shard_map/while
  385.2 0.9 copy-start.10
  386.1 49.6 %copy-start.6 = (bf16[1024,192]{0,1:T(8,128)(2,1)S(1)}, bf16[1024,192]{0,1:T(8,128)(2,1)}, u32[]{:S(2)}) copy-start(bf16[1024,192]{0,1:T(8,128)(2,1)} %copy-done.5) | copy-start | bytes 1179652
  387.2 56.6 %all-to-all-start.3 = ((bf16[4,256,192]{1,2,0:T(8,128)(2,1)}), bf16[4,256,192]{1,2,0:T(8,128)(2,1)S(1)}, u32[]{:S(2)}, u32[]{:S(2)}) async-start(bf16[4,256,192]{1,2,0:T(8,128)(2,1)} %copy.41), calls=%async_computation.3 | async-start | bytes 786432 | tf_op jit(solution)/shard_map/all_to_all | solution.py:70
  443.8 28.2 %all-to-all-start.4 = ((bf16[4,256,192]{1,2,0:T(8,128)(2,1)}), bf16[4,256,192]{1,2,0:T(8,128)(2,1)S(1)}, u32[]{:S(2)}, u32[]{:S(2)}) async-start(bf16[4,256,192]{1,2,0:T(8,128)(2,1)} %bitcast.97), calls=%async_computation.4 | async-start | bytes 786432 | tf_op jit(solution)/shard_map/all_to_all | solution.py:71
  471.9 16.0 %all-to-all-start.2 = ((bf16[4,256,384]{2,1,0:T(8,128)(2,1)}), bf16[4,256,384]{2,1,0:T(8,128)(2,1)S(1)}, u32[]{:S(2)}, u32[]{:S(2)}) async-start(bf16[4,256,384]{2,1,0:T(8,128)(2,1)} %bitcast.25), calls=%async_computation.2 | async-start | bytes 1572864 | tf_op jit(solution)/shard_map/all_to_all | solution.py:119
Sparse Core Ops, SparseCore 0:
  11.9 47.5 all-gather.3
  61.2 258.2 all-gather.5
  386.2 80.7 all-gather.7

commit v2 on v1

--- a/solution.py
+++ b/solution.py
@@ -1,7 +1,11 @@
+import functools
+
 import jax
 import jax.numpy as jnp
 from jax import lax
 from jax.sharding import PartitionSpec as P
+from jax.experimental import pallas as pl
+from jax.experimental.pallas import tpu as pltpu
 
 H = 16
 KVH = 8
@@ -35,6 +39,81 @@
     return turned.reshape(count, heads * HD)
 
 
+def fan_out_kernel(count, src_ref, out_ref, send_sem, recv_sem, local_sem):
+    me = lax.axis_index("req")
+    kv = lax.axis_index("kv")
+    barrier = pltpu.get_barrier_semaphore()
+
+    def greet(step, carry):
+        peer = lax.rem(me + step, count)
+        pl.semaphore_signal(
+            barrier, inc=1, device_id=(peer, kv), device_id_type=pl.DeviceIdType.MESH
+        )
+        return carry
+
+    lax.fori_loop(1, count, greet, 0)
+    pl.semaphore_wait(barrier, count - 1)
+
+    local = pltpu.make_async_copy(src_ref, out_ref.at[me], local_sem)
+    local.start()
+
+    def send(step, carry):
+        peer = lax.rem(me + step, count)
+        pltpu.make_async_remote_copy(
+            src_ref=src_ref,
+            dst_ref=out_ref.at[me],
+            send_sem=send_sem.at[step - 1],
+            recv_sem=recv_sem.at[step - 1],
+            device_id=(peer, kv),
+            device_id_type=pl.DeviceIdType.MESH,
+        ).start()
+        return carry
+
+    lax.fori_loop(1, count, send, 0)
+
+    def finish(step, carry):
+        peer = lax.rem(me + step, count)
+        source = lax.rem(me + count - step, count)
+        pltpu.make_async_remote_copy(
+            src_ref=src_ref,
+            dst_ref=out_ref.at[me],
+            send_sem=send_sem.at[step - 1],
+            recv_sem=recv_sem.at[step - 1],
+            device_id=(peer, kv),
+            device_id_type=pl.DeviceIdType.MESH,
+        ).wait_send()
+        pltpu.make_async_remote_copy(
+            src_ref=src_ref,
+            dst_ref=out_ref.at[source],
+            send_sem=send_sem.at[step - 1],
+            recv_sem=recv_sem.at[step - 1],
+            device_id=(source, kv),
+            device_id_type=pl.DeviceIdType.MESH,
+        ).wait_recv()
+        return carry
+
+    lax.fori_loop(1, count, finish, 0)
+    local.wait()
+
+
+def gather_req(piece):
+    count = lax.axis_size("req")
+    rows, width = piece.shape
+    gathered = pl.pallas_call(
+        functools.partial(fan_out_kernel, count),
+        out_shape=jax.ShapeDtypeStruct((count, rows, width), piece.dtype),
+        in_specs=[pl.BlockSpec(memory_space=pl.ANY)],
+        out_specs=pl.BlockSpec(memory_space=pl.ANY),
+        scratch_shapes=[
+            pltpu.SemaphoreType.DMA((count - 1,)),
+            pltpu.SemaphoreType.DMA((count - 1,)),
+            pltpu.SemaphoreType.DMA,
+        ],
+        compiler_params=pltpu.CompilerParams(collective_id=0, has_side_effects=True),
+    )(piece)
+    return gathered.reshape(count * rows, width)
+
+
 def body(hidden, lengths, key_cache, value_cache, norm_gain, w_query, w_key, w_value, w_out):
     rows_here = hidden.shape[1]
     kv_count = lax.axis_size("kv")
@@ -53,7 +132,7 @@
     normed_all = lax.all_gather(normed, "kv", axis=0, tiled=True)
 
     pieces = jnp.concatenate([w_query, w_key, w_value, w_out], axis=1)
-    cols = lax.all_gather(pieces, "req", axis=0, tiled=True)
+    cols = gather_req(pieces)
     wq = cols[:, :q_cols]
     wk = cols[:, q_cols:q_cols + k_cols]
     wv = cols[:, q_cols + k_cols:q_cols + k_cols + v_cols]

time: 497 us -> 274 us (0.55)
  waiting for transfers between devices: 319 us -> 35.2 us
  Pallas kernels: 0 us -> 90.6 us
  starting transfers between devices: 68.6 us -> 28.4 us
  local copies, waits for them, and re-layouts: 16 us -> 26.4 us
    all_gather x1 -> x0, waiting for transfers between devices: 259 us -> none  [body(): cols = lax.all_gather(pieces, 'req', axis=0, tiled=True)]
    pallas_call x0 -> x1, Pallas kernels: none -> 90.6 us  [gather_req(): pl.pallas_call(functools.partial(fan_out_kernel, count), out_shape=jax.Sh...]
    all_to_all x1, starting transfers between devices: 48.5 us -> 4.93 us  [body(): lax.all_to_all(keys_new, 'kv', split_axis=0, concat_axis=1, tiled=True)]
    all_to_all x1, waiting for transfers between devices: 14.8 us -> 3.24 us  [body(): lax.all_to_all(value_cache[0], 'kv', split_axis=1, concat_axis=0, tiled=T...]
    all_to_all x1, waiting for transfers between devices: 8.59 us -> 0.01 us  [body(): lax.all_to_all(key_cache[0], 'kv', split_axis=1, concat_axis=0, tiled=True)]
  transfers between devices with their start and end apart: 8 -> 7, of which waited for: 6 -> 4; matrix products, arithmetic and copies ran while one was open for 4% -> 12% of each run, Pallas kernels for 0% -> 33%
where the time goes in v2:
time: 274 us; the launch traced here: 273 us
  Pallas kernels  90.6 us (33%)
  matrix products  64.4 us (24%)
  waiting for transfers between devices  35.2 us (13%)
  starting transfers between devices  28.4 us (10%)
  local copies, waits for them, and re-layouts  26.4 us (10%)
  between operations  14.9 us (5%)
  other arithmetic  13.4 us (5%)
    pallas_call x1, Pallas kernels, gather_req(): pl.pallas_call(functools.partial(fan_out_kernel, count), out_shape=jax.Sh...  90.6 us
    sub x2, matrix products, attend(): weights = jnp.where(visible[None], jnp.exp(score - peak[..., None]), 0.0)  38.5 us
    dot_general x2, matrix products, attend(): jnp.einsum('gqk,kd->qgd', weights.astype(jnp.bfloat16), value_block, pref...  15.3 us
    all_gather x1, waiting for transfers between devices, body(): context_all = lax.all_gather(context, 'kv', axis=1, tiled=True)  14.4 us
    all_to_all x1, waiting for transfers between devices, body(): lax.all_to_all(keys_new, 'kv', split_axis=0, concat_axis=1, tiled=True)  9.1 us
    all_to_all x1, waiting for transfers between devices, body(): lax.all_to_all(attended_cols, 'kv', split_axis=0, concat_axis=1, tiled=True)  8.46 us
    unnamed x34, local copies, waits for them, and re-layouts  7.19 us
    all_to_all x1, starting transfers between devices, body(): lax.all_to_all(value_cache[0], 'kv', split_axis=1, concat_axis=0, tiled=T...  7.14 us
  transfers between devices with their start and end apart: 7, of which 4 were waited for; matrix products, arithmetic and copies ran while one was open for 12% of the time, Pallas kernels for 33%

profile of v2, /device:TPU:1, one launch (start us, length us, event | category | flops | bytes accessed | tf_op | source)
XLA Modules:
  0.0 273.4 jit_solution(13711520836901055589)
XLA Ops:
  7.2 0.0 all-gather.3.cloned.1.call-start
  7.2 0.8 convert_element_type.52
  8.0 1.4 fusion.49
  9.4 2.3 fusion.51
  11.7 0.0 all-gather.3.cloned.1.call-update
  11.7 1.2 copy.38
  13.0 6.7 %all-to-all-start.1 = ((bf16[512,4,192]{0,2,1:T(8,128)(2,1)}), bf16[512,4,192]{0,2,1:T(8,128)(2,1)S(1)}, u32[]{:S(2)}, u32[]{:S(2)}) async-start(bf16[512,4,192]{0,2,1:T(8,128)(2,1)} %bitcast.17), calls=%async_computation.1 | async-start | bytes 1572864 | tf_op jit(solution)/shard_map/all_to_all | solution.py:152
  19.7 0.7 concatenate.28.src_ref
  20.4 90.6 %shard_map.112 = bf16[64,24,1152]{2,1,0:T(8,128)(2,1)} custom-call(bf16[24,1152]{1,0:T(8,128)(2,1)} %concatenate.28.src_ref), custom_call_target="tpu_custom_call" | custom-call | tf_op jit(solution)/shard_map/pallas_call | solution.py:102
  111.7 1.2 copy.36
  113.0 0.3 iota_compare_fusion
  113.3 1.5 multiply_cosine_fusion
  114.8 7.1 %all-to-all-start = ((bf16[512,4,192]{0,2,1:T(8,128)(2,1)}), bf16[512,4,192]{0,2,1:T(8,128)(2,1)}, u32[]{:S(2)}, u32[]{:S(2)}) async-start(bf16[512,4,192]{0,2,1:T(8,128)(2,1)} %bitcast.9), calls=%async_computation | async-start | bytes 1572864 | tf_op jit(solution)/shard_map/all_to_all | solution.py:153
  122.0 3.5 %pad_add_fusion = pred[1024,3072]{0,1:T(8,128)(4,1)} fusion(pred[1024,1024]{0,1:T(8,128)(4,1)S(1)} %iota_compare_fusion, pred[3072]{0:T(1024)(128)(4,1)S(1)} %pad.6.clone), kind=kLoop, calls=%fused_computation.30 | loop fusion | flops 3145728 | bytes 4197376 | tf_op jit(solution)/shard_map/concatenate | solution.py:161
  125.5 2.8 %copy.39 = bf16[4,512,192]{1,0,2:T(4,128)(2,1)} copy(bf16[4,512,192]{1,2,0:T(8,128)(2,1)} %bitcast.122) | data formatting | bytes 1572864 | tf_op jit(solution)/shard_map/all_to_all | solution.py:152
  128.3 2.8 %concatenate.32 = bf16[2048,2,96]{0,2,1:T(8,128)(2,1)} reshape(bf16[4,512,192]{1,0,2:T(4,128)(2,1)} %copy.39) | data formatting | bytes 1572864 | tf_op jit(solution)/shard_map/concatenate | solution.py:156
  131.1 3.2 %all-to-all-done = bf16[512,4,192]{0,2,1:T(8,128)(2,1)} async-done(((bf16[512,4,192]{0,2,1:T(8,128)(2,1)}), bf16[512,4,192]{0,2,1:T(8,128)(2,1)}, u32[]{:S(2)}, u32[]{:S(2)}) %all-to-all-start) | async-done | bytes 786464 | tf_op jit(solution)/shard_map/all_to_all | solution.py:153
  134.3 2.6 copy.37
  137.0 2.8 %concatenate.27 = bf16[2048,2,96]{0,2,1:T(8,128)(2,1)} reshape(bf16[4,512,192]{1,0,2:T(4,128)(2,1)} %copy.37) | data formatting | bytes 1572864 | tf_op jit(solution)/shard_map/concatenate | solution.py:157
  139.8 3.2 %fusion.55 = f32[1024,192]{0,1:T(8,128)S(1)} fusion(bf16[1024,1536]{1,0:T(8,128)(2,1)} %all-gather.3.cloned.1.call-done, bf16[1536,1152]{1,0:T(8,128)(2,1)S(1)} %bitcast.117), kind=kOutput, calls=%fused_computation.44 | convolution fusion | flops 603979776 | bytes 4718592 | tf_op jit(solution)/shard_map/dot_general | solution.py:143
  143.1 0.1 multiply_subtract_fusion
  143.2 1.5 fusion.53
  144.7 0.3 subtract_convert_fusion
  145.0 0.7 copy-done.1
  145.7 0.1 copy-done.4
  145.8 1.1 maximum_bitcast_fusion.1
  146.9 0.9 pad_maximum_fusion
  147.8 1.4 convolution_convert_fusion.1
  149.3 1.1 maximum_bitcast_fusion
  150.4 53.8 %while.10 = (s32[]{:T(128)}, bf16[2,1024,2,96]{1,3,2,0:T(8,128)(2,1)}, bf16[2,3072,96]{1,2,0:T(8,128)(2,1)}, pred[1024,3072]{0,1:T(8,128)(4,1)}, bf16[2,3072,96]...) while((s32[]{:T(128)}, bf16[2,1024,2,96]{1,3,2,0:T(8,128)(2,1)}, ...), condition=%wide.region_4.5_spmd, body=%wide.region_1.4_spmd.sunk | while | flops 2453867520 | bytes 33835084 | solution.py:192
  150.4 19.2 %fusion.82 = (f32[2,1024]{1,0:T(2,128)S(1)}, bf16[2,1024,3072]{1,2,0:T(8,128)(2,1)}) fusion(pred[1024,3072]{0,1:T(8,128)(4,1)} %get-tuple-element.125, bf16[2,3072,96]{1,2,0:T(8,128)(2,1)} %get-tuple-element.126, s32[]{:T(128)} %get-tuple-element.115, bf16[2,1024,2,96]{1,3,2,0:T(8,128)(2,1)} %get-tuple-element.127), kind=kOutput, calls=%fused_computation.60.clone.1 | convolution fusion | flops 1245711360 | bytes 19866624 | tf_op jit(solution)/shard_map/while/body/eval_jaxpr/sub | solution.py:182
  169.7 7.6 %fusion.83 = bf16[2,1024,2,96]{1,3,2,0:T(8,128)(2,1)} fusion(bf16[2,1024,2,96]{1,3,2,0:T(8,128)(2,1)} %get-tuple-element.116, s32[]{:T(128)} %get-tuple-element.115, bf16[2,1024,3072]{1,2,0:T(8,128)(2,1)} %get-tuple-element.106, bf16[2,3072,96]{1,2,0:T(8,128)(2,1)} %get-tuple-element.124, f32[1024,2]{0,1:T(2,128)S(1)} %bitcast.131), kind=kOutput, calls=%fused_computation.13.clone.1 | convolution fusion | flops 1208156160 | bytes 13968384 | tf_op jit(solution)/shard_map/while/body/eval_jaxpr/gqk,kd->qgd/dot_general | solution.py:184
  177.3 19.2 %fusion.82 = (f32[2,1024]{1,0:T(2,128)S(1)}, bf16[2,1024,3072]{1,2,0:T(8,128)(2,1)}) fusion(pred[1024,3072]{0,1:T(8,128)(4,1)} %get-tuple-element.125, bf16[2,3072,96]{1,2,0:T(8,128)(2,1)} %get-tuple-element.126, s32[]{:T(128)} %get-tuple-element.115, bf16[2,1024,2,96]{1,3,2,0:T(8,128)(2,1)} %get-tuple-element.127), kind=kOutput, calls=%fused_computation.60.clone.1 | convolution fusion | flops 1245711360 | bytes 19866624 | tf_op jit(solution)/shard_map/while/body/eval_jaxpr/sub | solution.py:182
  196.5 7.6 %fusion.83 = bf16[2,1024,2,96]{1,3,2,0:T(8,128)(2,1)} fusion(bf16[2,1024,2,96]{1,3,2,0:T(8,128)(2,1)} %get-tuple-element.116, s32[]{:T(128)} %get-tuple-element.115, bf16[2,1024,3072]{1,2,0:T(8,128)(2,1)} %get-tuple-element.106, bf16[2,3072,96]{1,2,0:T(8,128)(2,1)} %get-tuple-element.124, f32[1024,2]{0,1:T(2,128)S(1)} %bitcast.131), kind=kOutput, calls=%fused_computation.13.clone.1 | convolution fusion | flops 1208156160 | bytes 13968384 | tf_op jit(solution)/shard_map/while/body/eval_jaxpr/gqk,kd->qgd/dot_general | solution.py:184
  204.2 2.0 convert_element_type.62
  206.2 1.8 copy.41
  208.0 4.9 %all-to-all-start.3 = ((bf16[4,256,192]{1,2,0:T(8,128)(2,1)}), bf16[4,256,192]{1,2,0:T(8,128)(2,1)}, u32[]{:S(2)}, u32[]{:S(2)}) async-start(bf16[4,256,192]{1,2,0:T(8,128)(2,1)} %copy.41), calls=%async_computation.3 | async-start | bytes 786432 | tf_op jit(solution)/shard_map/all_to_all | solution.py:149
  213.0 1.8 copy.48
  214.8 9.1 %all-to-all-done.3 = bf16[4,256,192]{1,2,0:T(8,128)(2,1)} async-done(((bf16[4,256,192]{1,2,0:T(8,128)(2,1)}), bf16[4,256,192]{1,2,0:T(8,128)(2,1)}, u32[]{:S(2)}, u32[]{:S(2)}) %all-to-all-start.3) | async-done | bytes 393248 | tf_op jit(solution)/shard_map/all_to_all | solution.py:149
  223.9 5.9 %all-to-all-start.4 = ((bf16[4,256,192]{1,2,0:T(8,128)(2,1)}), bf16[4,256,192]{1,2,0:T(8,128)(2,1)}, u32[]{:S(2)}, u32[]{:S(2)}) async-start(bf16[4,256,192]{1,2,0:T(8,128)(2,1)} %bitcast.126), calls=%async_computation.4 | async-start | bytes 786432 | tf_op jit(solution)/shard_map/all_to_all | solution.py:150
  229.7 14.4 %all-gather.5.cloned.1.call-done = bf16[1024,1536]{0,1:T(8,128)(2,1)} async-done(((bf16[1024,384]{0,1:T(8,128)(2,1)}), bf16[1024,1536]{0,1:T(8,128)(2,1)}) %all-gather.5.cloned.1.call-update) | async-done | bytes 3145744 | tf_op jit(solution)/shard_map/all_gather | solution.py:196
  244.2 4.6 %convolution_convert_fusion = bf16[1024,384]{1,0:T(8,128)(2,1)} fusion(bf16[1024,1536]{0,1:T(8,128)(2,1)} %all-gather.5.cloned.1.call-done, bf16[1536,1152]{1,0:T(8,128)(2,1)S(1)} %bitcast.120), kind=kOutput, calls=%fused_computation.37 | convolution fusion | flops 1208352768 | bytes 5111808 | tf_op jit(solution)/shard_map/dot_general | solution.py:197
  248.7 3.7 %all-to-all-start.2 = ((bf16[4,256,384]{2,1,0:T(8,128)(2,1)}), bf16[4,256,384]{2,1,0:T(8,128)(2,1)S(1)}, u32[]{:S(2)}, u32[]{:S(2)}) async-start(bf16[4,256,384]{2,1,0:T(8,128)(2,1)} %bitcast.130), calls=%async_computation.2 | async-start | bytes 1572864 | tf_op jit(solution)/shard_map/all_to_all | solution.py:198
  252.5 1.9 copy.43
  254.4 1.9 copy.44
  256.3 8.5 %all-to-all-done.2 = bf16[4,256,384]{2,1,0:T(8,128)(2,1)S(1)} async-done(((bf16[4,256,384]{2,1,0:T(8,128)(2,1)}), bf16[4,256,384]{2,1,0:T(8,128)(2,1)S(1)}, u32[]{:S(2)}, u32[]{:S(2)}) %all-to-all-start.2) | async-done | bytes 786464 | tf_op jit(solution)/shard_map/all_to_all | solution.py:198
  264.8 0.6 copy.40
  265.4 1.2 broadcast_in_dim.58
  (40 shorter events, 0.2 us)
Async XLA Ops:
  7.2 4.5 %copy-start.9 = (bf16[1,512,768]{2,1,0:T(8,128)(2,1)S(1)}, bf16[1,512,768]{2,1,0:T(8,128)(2,1)}, u32[]{:S(2)}) copy-start(bf16[1,512,768]{2,1,0:T(8,128)(2,1)} %param.13) | copy-start | bytes 2359300
  7.2 132.6 %all-gather.3.cloned.1.call-start = ((), (), s32[]{:S(2)}) async-start(), calls=%async_computation.5 | async-start | bytes 3932160 | tf_op jit(solution)/shard_map/all_gather | solution.py:132
  8.0 11.7 %copy-start.11 = (bf16[24,384]{1,0:T(8,128)(2,1)S(1)}, bf16[24,384]{1,0:T(8,128)(2,1)}, u32[]{:S(2)}) copy-start(bf16[24,384]{1,0:T(8,128)(2,1)} %param.16) | copy-start | bytes 55300
  8.0 11.7 %copy-start.12 = (bf16[24,384]{1,0:T(8,128)(2,1)S(1)}, bf16[24,384]{1,0:T(8,128)(2,1)}, u32[]{:S(2)}) copy-start(bf16[24,384]{1,0:T(8,128)(2,1)} %param.19) | copy-start | bytes 55300
  8.0 11.7 %copy-start.13 = (bf16[24,192]{1,0:T(8,128)(2,1)S(1)}, bf16[24,192]{1,0:T(8,128)(2,1)}, u32[]{:S(2)}) copy-start(bf16[24,192]{1,0:T(8,128)(2,1)} %param.17) | copy-start | bytes 27652
  8.0 11.7 %copy-start.14 = (bf16[24,192]{1,0:T(8,128)(2,1)S(1)}, bf16[24,192]{1,0:T(8,128)(2,1)}, u32[]{:S(2)}) copy-start(bf16[24,192]{1,0:T(8,128)(2,1)} %param.18) | copy-start | bytes 27652
  11.7 100.0 %copy-start.10 = (bf16[1,512,768]{2,1,0:T(8,128)(2,1)S(1)}, bf16[1,512,768]{2,1,0:T(8,128)(2,1)}, u32[]{:S(2)}) copy-start(bf16[1,512,768]{2,1,0:T(8,128)(2,1)} %param.14) | copy-start | bytes 2359300
  13.0 101.8 %all-to-all-start.1 = ((bf16[512,4,192]{0,2,1:T(8,128)(2,1)}), bf16[512,4,192]{0,2,1:T(8,128)(2,1)S(1)}, u32[]{:S(2)}, u32[]{:S(2)}) async-start(bf16[512,4,192]{0,2,1:T(8,128)(2,1)} %bitcast.17), calls=%async_computation.1 | async-start | bytes 1572864 | tf_op jit(solution)/shard_map/all_to_all | solution.py:152
  114.8 10.7 %copy-start.3 = (bf16[512,4,192]{0,2,1:T(8,128)(2,1)}, bf16[512,4,192]{0,2,1:T(8,128)(2,1)S(1)}, u32[]{:S(2)}) copy-start(bf16[512,4,192]{0,2,1:T(8,128)(2,1)S(1)} %all-to-all-done.1) | copy-start | bytes 2359300
  114.8 19.5 %all-to-all-start = ((bf16[512,4,192]{0,2,1:T(8,128)(2,1)}), bf16[512,4,192]{0,2,1:T(8,128)(2,1)}, u32[]{:S(2)}, u32[]{:S(2)}) async-start(bf16[512,4,192]{0,2,1:T(8,128)(2,1)} %bitcast.9), calls=%async_computation | async-start | bytes 1572864 | tf_op jit(solution)/shard_map/all_to_all | solution.py:153
  122.0 122.2 %all-gather.5.cloned.1.call-start = ((), (), s32[]{:S(2)}) async-start(), calls=%async_computation.6 | async-start | bytes 3932160 | tf_op jit(solution)/shard_map/all_gather | solution.py:196
  125.5 14.3 %copy-start = (bf16[64,24,1152]{2,1,0:T(8,128)(2,1)S(1)}, bf16[64,24,1152]{2,1,0:T(8,128)(2,1)}, u32[]{:S(2)}) copy-start(bf16[64,24,1152]{2,1,0:T(8,128)(2,1)} %shard_map.112) | copy-start | bytes 10616836
  139.8 3.2 %copy-start.6 = (f32[1024,48]{0,1:T(8,128)S(1)}, f32[1024,48]{0,1:T(8,128)}, u32[]{:S(2)}) copy-start(f32[1024,48]{0,1:T(8,128)} %get-tuple-element.63) | copy-start | bytes 589828
  139.8 3.3 %copy-start.7 = (f32[1024,48]{0,1:T(8,128)S(1)}, f32[1024,48]{0,1:T(8,128)}, u32[]{:S(2)}) copy-start(f32[1024,48]{0,1:T(8,128)} %get-tuple-element.64) | copy-start | bytes 589828
  139.8 3.4 %copy-start.2 = (bf16[1024,1536]{1,0:T(8,128)(2,1)S(1)}, bf16[1024,1536]{1,0:T(8,128)(2,1)}, u32[]{:S(2)}) copy-start(bf16[1024,1536]{1,0:T(8,128)(2,1)} %all-gather.3.cloned.1.call-done) | copy-start | bytes 9437188
  144.7 1.1 copy-start.4
  145.0 0.7 copy-start.1
  146.9 2.3 copy-start.5
  149.3 1.2 copy-start.8
  208.0 15.8 %all-to-all-start.3 = ((bf16[4,256,192]{1,2,0:T(8,128)(2,1)}), bf16[4,256,192]{1,2,0:T(8,128)(2,1)}, u32[]{:S(2)}, u32[]{:S(2)}) async-start(bf16[4,256,192]{1,2,0:T(8,128)(2,1)} %copy.41), calls=%async_computation.3 | async-start | bytes 786432 | tf_op jit(solution)/shard_map/all_to_all | solution.py:149
  223.9 24.9 %all-to-all-start.4 = ((bf16[4,256,192]{1,2,0:T(8,128)(2,1)}), bf16[4,256,192]{1,2,0:T(8,128)(2,1)}, u32[]{:S(2)}, u32[]{:S(2)}) async-start(bf16[4,256,192]{1,2,0:T(8,128)(2,1)} %bitcast.126), calls=%async_computation.4 | async-start | bytes 786432 | tf_op jit(solution)/shard_map/all_to_all | solution.py:150
  248.7 16.0 %all-to-all-start.2 = ((bf16[4,256,384]{2,1,0:T(8,128)(2,1)}), bf16[4,256,384]{2,1,0:T(8,128)(2,1)S(1)}, u32[]{:S(2)}, u32[]{:S(2)}) async-start(bf16[4,256,384]{2,1,0:T(8,128)(2,1)} %bitcast.130), calls=%async_computation.2 | async-start | bytes 1572864 | tf_op jit(solution)/shard_map/all_to_all | solution.py:198
Sparse Core Ops, SparseCore 0:
  11.8 54.7 all-gather.2
  204.3 39.7 all-gather.4

commit v3 on v1

--- a/solution.py
+++ b/solution.py
@@ -1,7 +1,11 @@
+import functools
+
 import jax
 import jax.numpy as jnp
 from jax import lax
 from jax.sharding import PartitionSpec as P
+from jax.experimental import pallas as pl
+from jax.experimental.pallas import tpu as pltpu
 
 H = 16
 KVH = 8
@@ -35,6 +39,136 @@
     return turned.reshape(count, heads * HD)
 
 
+Z_RUN = 8
+Y_RUN = 2
+MESH = pl.DeviceIdType.MESH
+
+
+def remote(src, dst, send, recv, device):
+    return pltpu.make_async_remote_copy(
+        src_ref=src, dst_ref=dst, send_sem=send, recv_sem=recv,
+        device_id=device, device_id_type=MESH,
+    )
+
+
+def plane_ring_kernel(planes, runs, src_ref, out_ref, s1_send, s1_recv, r_send, r_recv,
+                      l_send, l_recv, local_sem):
+    me = lax.axis_index("req")
+    kv = lax.axis_index("kv")
+    y_me = lax.rem(me, Y_RUN)
+    z_me = lax.rem(me // Y_RUN, runs)
+    x_me = me // (Y_RUN * runs)
+    q_me = x_me * Y_RUN + y_me
+    right_hops = runs // 2
+    left_hops = runs - 1 - right_hops
+
+    def plane_peer(q):
+        return ((q // Y_RUN) * runs + z_me) * Y_RUN + lax.rem(q, Y_RUN)
+
+    def ring_peer(z):
+        return (x_me * runs + z) * Y_RUN + y_me
+
+    z_right = lax.rem(z_me + 1, runs)
+    z_left = lax.rem(z_me + runs - 1, runs)
+
+    barrier = pltpu.get_barrier_semaphore()
+
+    def greet(step, carry):
+        q = lax.rem(q_me + step, planes)
+        pl.semaphore_signal(barrier, inc=1, device_id=(plane_peer(q), kv), device_id_type=MESH)
+        return carry
+
+    lax.fori_loop(1, planes, greet, 0)
+    pl.semaphore_signal(barrier, inc=1, device_id=(ring_peer(z_right), kv), device_id_type=MESH)
+    pl.semaphore_signal(barrier, inc=1, device_id=(ring_peer(z_left), kv), device_id_type=MESH)
+    pl.semaphore_wait(barrier, planes + 1)
+
+    local = pltpu.make_async_copy(src_ref, out_ref.at[z_me, q_me], local_sem)
+    local.start()
+
+    def send(step, carry):
+        q = lax.rem(q_me + step, planes)
+        remote(src_ref, out_ref.at[z_me, q_me], s1_send.at[step - 1], s1_recv.at[step - 1],
+               (plane_peer(q), kv)).start()
+        return carry
+
+    lax.fori_loop(1, planes, send, 0)
+
+    def finish(step, carry):
+        q = lax.rem(q_me + step, planes)
+        source = lax.rem(q_me + planes - step, planes)
+        remote(src_ref, out_ref.at[z_me, q_me], s1_send.at[step - 1], s1_recv.at[step - 1],
+               (plane_peer(q), kv)).wait_send()
+        remote(src_ref, out_ref.at[z_me, source], s1_send.at[step - 1], s1_recv.at[step - 1],
+               (plane_peer(source), kv)).wait_recv()
+        return carry
+
+    lax.fori_loop(1, planes, finish, 0)
+    local.wait()
+
+    sent = []
+    if right_hops > 0:
+        c = remote(out_ref.at[z_me], out_ref.at[z_me], r_send.at[0], r_recv.at[0],
+                   (ring_peer(z_right), kv))
+        c.start()
+        sent.append(c)
+    if left_hops > 0:
+        c = remote(out_ref.at[z_me], out_ref.at[z_me], l_send.at[0], l_recv.at[0],
+                   (ring_peer(z_left), kv))
+        c.start()
+        sent.append(c)
+    for k in range(1, max(right_hops, left_hops) + 1):
+        if k <= right_hops:
+            z_from = lax.rem(z_me + runs - k, runs)
+            remote(out_ref.at[z_from], out_ref.at[z_from], r_send.at[k - 1], r_recv.at[k - 1],
+                   (ring_peer(z_right), kv)).wait_recv()
+            if k < right_hops:
+                c = remote(out_ref.at[z_from], out_ref.at[z_from], r_send.at[k], r_recv.at[k],
+                           (ring_peer(z_right), kv))
+                c.start()
+                sent.append(c)
+        if k <= left_hops:
+            z_from = lax.rem(z_me + k, runs)
+            remote(out_ref.at[z_from], out_ref.at[z_from], l_send.at[k - 1], l_recv.at[k - 1],
+                   (ring_peer(z_left), kv)).wait_recv()
+            if k < left_hops:
+                c = remote(out_ref.at[z_from], out_ref.at[z_from], l_send.at[k], l_recv.at[k],
+                           (ring_peer(z_left), kv))
+                c.start()
+                sent.append(c)
+    for c in sent:
+        c.wait_send()
+
+
+def gather_req(piece):
+    count = lax.axis_size("req")
+    runs = min(Z_RUN, count // Y_RUN)
+    planes = count // runs
+    rows, width = piece.shape
+    hops = max(runs - 1, 1)
+    gathered = pl.pallas_call(
+        functools.partial(plane_ring_kernel, planes, runs),
+        out_shape=jax.ShapeDtypeStruct((runs, planes, rows, width), piece.dtype),
+        in_specs=[pl.BlockSpec(memory_space=pl.ANY)],
+        out_specs=pl.BlockSpec(memory_space=pl.ANY),
+        scratch_shapes=[
+            pltpu.SemaphoreType.DMA((planes - 1,)),
+            pltpu.SemaphoreType.DMA((planes - 1,)),
+            pltpu.SemaphoreType.DMA((hops,)),
+            pltpu.SemaphoreType.DMA((hops,)),
+            pltpu.SemaphoreType.DMA((hops,)),
+            pltpu.SemaphoreType.DMA((hops,)),
+            pltpu.SemaphoreType.DMA,
+        ],
+        compiler_params=pltpu.CompilerParams(collective_id=0, has_side_effects=True),
+    )(piece)
+    x_count = planes // Y_RUN
+    ordered = jnp.transpose(
+        gathered.reshape(runs, x_count, Y_RUN, rows, width), (1, 0, 2, 3, 4)
+    )
+    return ordered.reshape(count * rows, width)
+
+
 def body(hidden, lengths, key_cache, value_cache, norm_gain, w_query, w_key, w_value, w_out):
     rows_here = hidden.shape[1]
     kv_count = lax.axis_size("kv")
@@ -53,7 +187,7 @@
     normed_all = lax.all_gather(normed, "kv", axis=0, tiled=True)
 
     pieces = jnp.concatenate([w_query, w_key, w_value, w_out], axis=1)
-    cols = lax.all_gather(pieces, "req", axis=0, tiled=True)
+    cols = gather_req(pieces)
     wq = cols[:, :q_cols]
     wk = cols[:, q_cols:q_cols + k_cols]
     wv = cols[:, q_cols + k_cols:q_cols + k_cols + v_cols]

time: 497 us -> 251 us (0.51)
  waiting for transfers between devices: 319 us -> 35.3 us
  Pallas kernels: 0 us -> 62.1 us
  starting transfers between devices: 68.6 us -> 28.2 us
  local copies, waits for them, and re-layouts: 16 us -> 29.5 us
    all_gather x1 -> x0, waiting for transfers between devices: 259 us -> none  [body(): cols = lax.all_gather(pieces, 'req', axis=0, tiled=True)]
    pallas_call x0 -> x1, Pallas kernels: none -> 62.1 us  [gather_req(): pl.pallas_call(functools.partial(plane_ring_kernel, planes, runs), out_sh...]
    all_to_all x1, starting transfers between devices: 48.5 us -> 4.95 us  [body(): lax.all_to_all(keys_new, 'kv', split_axis=0, concat_axis=1, tiled=True)]
    all_to_all x1, waiting for transfers between devices: 14.8 us -> 2.88 us  [body(): lax.all_to_all(value_cache[0], 'kv', split_axis=1, concat_axis=0, tiled=T...]
    all_to_all x1, waiting for transfers between devices: 8.59 us -> 0.01 us  [body(): lax.all_to_all(key_cache[0], 'kv', split_axis=1, concat_axis=0, tiled=True)]
    all_gather x1, waiting for transfers between devices: 18.9 us -> 13.4 us  [body(): context_all = lax.all_gather(context, 'kv', axis=1, tiled=True)]
  transfers between devices with their start and end apart: 8 -> 7, of which waited for: 6 -> 4; matrix products, arithmetic and copies ran while one was open for 4% -> 15% of each run, Pallas kernels for 0% -> 25%
where the time goes in v3:
time: 251 us; the launch traced here: 249 us
  matrix products  64.5 us (26%)
  Pallas kernels  62.1 us (25%)
  waiting for transfers between devices  35.3 us (14%)
  local copies, waits for them, and re-layouts  29.5 us (12%)
  starting transfers between devices  28.2 us (11%)
  other arithmetic  15 us (6%)
  between operations  14.8 us (6%)
    pallas_call x1, Pallas kernels, gather_req(): pl.pallas_call(functools.partial(plane_ring_kernel, planes, runs), out_sh...  62.1 us
    sub x2, matrix products, attend(): weights = jnp.where(visible[None], jnp.exp(score - peak[..., None]), 0.0)  38.5 us
    dot_general x2, matrix products, attend(): jnp.einsum('gqk,kd->qgd', weights.astype(jnp.bfloat16), value_block, pref...  15.3 us
    all_gather x1, waiting for transfers between devices, body(): context_all = lax.all_gather(context, 'kv', axis=1, tiled=True)  13.4 us
    all_to_all x1, waiting for transfers between devices, body(): lax.all_to_all(keys_new, 'kv', split_axis=0, concat_axis=1, tiled=True)  10.6 us
    all_to_all x1, waiting for transfers between devices, body(): lax.all_to_all(attended_cols, 'kv', split_axis=0, concat_axis=1, tiled=True)  8.46 us
    unnamed x28, local copies, waits for them, and re-layouts  8.24 us
    all_to_all x1, starting transfers between devices, body(): lax.all_to_all(key_cache[0], 'kv', split_axis=1, concat_axis=0, tiled=True)  7.39 us
  transfers between devices with their start and end apart: 7, of which 4 were waited for; matrix products, arithmetic and copies ran while one was open for 15% of the time, Pallas kernels for 25%

profile of v3, /device:TPU:1, one launch (start us, length us, event | category | flops | bytes accessed | tf_op | source)
XLA Modules:
  0.0 249.5 jit_solution(17422679968009367056)
XLA Ops:
  7.2 0.0 all-gather.3.cloned.1.call-start
  7.2 0.8 convert_element_type.52
  8.0 1.4 fusion.49
  9.4 2.3 fusion.51
  11.7 1.2 copy.41
  13.0 7.4 %all-to-all-start.1 = ((bf16[512,4,192]{0,2,1:T(8,128)(2,1)}), bf16[512,4,192]{0,2,1:T(8,128)(2,1)}, u32[]{:S(2)}, u32[]{:S(2)}) async-start(bf16[512,4,192]{0,2,1:T(8,128)(2,1)} %bitcast.19), calls=%async_computation.1 | async-start | bytes 1572864 | tf_op jit(solution)/shard_map/all_to_all | solution.py:207
  20.4 0.7 concatenate.28.src_ref
  21.1 62.1 %shard_map.112 = bf16[8,8,24,1152]{3,2,1,0:T(8,128)(2,1)} custom-call(bf16[24,1152]{1,0:T(8,128)(2,1)} %concatenate.28.src_ref), custom_call_target="tpu_custom_call" | custom-call | tf_op jit(solution)/shard_map/pallas_call | solution.py:149
  83.2 2.3 copy.40
  86.1 2.3 copy.38
  88.5 1.3 iota_compare_fusion
  89.8 1.5 multiply_cosine_fusion
  91.3 7.2 %all-to-all-start = ((bf16[512,4,192]{0,2,1:T(8,128)(2,1)}), bf16[512,4,192]{0,2,1:T(8,128)(2,1)}, u32[]{:S(2)}, u32[]{:S(2)}) async-start(bf16[512,4,192]{0,2,1:T(8,128)(2,1)} %bitcast.126), calls=%async_computation | async-start | bytes 1572864 | tf_op jit(solution)/shard_map/all_to_all | solution.py:208
  98.5 4.1 %pad_add_fusion = pred[1024,3072]{0,1:T(8,128)(4,1)} fusion(pred[1024,1024]{0,1:T(8,128)(4,1)} %iota_compare_fusion, pred[3072]{0:T(1024)(128)(4,1)S(1)} %pad.6.clone), kind=kLoop, calls=%fused_computation.30 | loop fusion | flops 3145728 | bytes 4197376 | tf_op jit(solution)/shard_map/concatenate | solution.py:216
  102.6 2.6 %copy.42 = bf16[4,512,192]{1,0,2:T(4,128)(2,1)} copy(bf16[4,512,192]{1,2,0:T(8,128)(2,1)} %bitcast.20) | data formatting | bytes 1572864 | tf_op jit(solution)/shard_map/all_to_all | solution.py:207
  105.2 2.8 %concatenate.32 = bf16[2048,2,96]{0,2,1:T(8,128)(2,1)} reshape(bf16[4,512,192]{1,0,2:T(4,128)(2,1)} %copy.42) | data formatting | bytes 1572864 | tf_op jit(solution)/shard_map/concatenate | solution.py:211
  108.0 2.9 %all-to-all-done = bf16[512,4,192]{0,2,1:T(8,128)(2,1)} async-done(((bf16[512,4,192]{0,2,1:T(8,128)(2,1)}), bf16[512,4,192]{0,2,1:T(8,128)(2,1)}, u32[]{:S(2)}, u32[]{:S(2)}) %all-to-all-start) | async-done | bytes 786464 | tf_op jit(solution)/shard_map/all_to_all | solution.py:208
  110.9 2.6 %copy.39 = bf16[4,512,192]{1,0,2:T(4,128)(2,1)} copy(bf16[4,512,192]{1,2,0:T(8,128)(2,1)} %bitcast.10) | data formatting | bytes 1572864 | tf_op jit(solution)/shard_map/all_to_all | solution.py:208
  113.5 2.8 %concatenate.27 = bf16[2048,2,96]{0,2,1:T(8,128)(2,1)} reshape(bf16[4,512,192]{1,0,2:T(4,128)(2,1)} %copy.39) | data formatting | bytes 1572864 | tf_op jit(solution)/shard_map/concatenate | solution.py:212
  116.3 3.2 %fusion.55 = f32[1024,192]{0,1:T(8,128)S(1)} fusion(bf16[1024,1536]{1,0:T(8,128)(2,1)} %all-gather.3.cloned.1.call-done, bf16[1536,1152]{1,0:T(8,128)(2,1)S(1)} %bitcast.121), kind=kOutput, calls=%fused_computation.44 | convolution fusion | flops 603979776 | bytes 4718592 | tf_op jit(solution)/shard_map/dot_general | solution.py:198
  119.6 0.1 multiply_subtract_fusion
  119.7 1.5 fusion.53
  121.2 0.3 subtract_convert_fusion
  121.5 0.7 copy-done
  122.2 0.1 copy-done.2
  122.3 1.1 maximum_bitcast_fusion.1
  123.4 0.9 pad_maximum_fusion
  124.3 1.4 convolution_convert_fusion.1
  125.8 1.2 maximum_bitcast_fusion
  126.9 53.8 %while.10 = (s32[]{:T(128)}, bf16[2,1024,2,96]{1,3,2,0:T(8,128)(2,1)}, bf16[2,3072,96]{1,2,0:T(8,128)(2,1)}, pred[1024,3072]{0,1:T(8,128)(4,1)}, bf16[2,3072,96]...) while((s32[]{:T(128)}, bf16[2,1024,2,96]{1,3,2,0:T(8,128)(2,1)}, ...), condition=%wide.region_4.5_spmd, body=%wide.region_1.4_spmd.sunk | while | flops 2453867520 | bytes 33835084 | solution.py:247
  126.9 19.3 %fusion.82 = (f32[2,1024]{1,0:T(2,128)S(1)}, bf16[2,1024,3072]{1,2,0:T(8,128)(2,1)}) fusion(pred[1024,3072]{0,1:T(8,128)(4,1)} %get-tuple-element.125, bf16[2,3072,96]{1,2,0:T(8,128)(2,1)} %get-tuple-element.126, s32[]{:T(128)} %get-tuple-element.115, bf16[2,1024,2,96]{1,3,2,0:T(8,128)(2,1)} %get-tuple-element.127), kind=kOutput, calls=%fused_computation.60.clone.1 | convolution fusion | flops 1245711360 | bytes 19866624 | tf_op jit(solution)/shard_map/while/body/eval_jaxpr/sub | solution.py:237
  146.2 7.6 %fusion.83 = bf16[2,1024,2,96]{1,3,2,0:T(8,128)(2,1)} fusion(bf16[2,1024,2,96]{1,3,2,0:T(8,128)(2,1)} %get-tuple-element.116, s32[]{:T(128)} %get-tuple-element.115, bf16[2,1024,3072]{1,2,0:T(8,128)(2,1)} %get-tuple-element.106, bf16[2,3072,96]{1,2,0:T(8,128)(2,1)} %get-tuple-element.124, f32[1024,2]{0,1:T(2,128)S(1)} %bitcast.135), kind=kOutput, calls=%fused_computation.13.clone.1 | convolution fusion | flops 1208156160 | bytes 13968384 | tf_op jit(solution)/shard_map/while/body/eval_jaxpr/gqk,kd->qgd/dot_general | solution.py:239
  153.8 19.2 %fusion.82 = (f32[2,1024]{1,0:T(2,128)S(1)}, bf16[2,1024,3072]{1,2,0:T(8,128)(2,1)}) fusion(pred[1024,3072]{0,1:T(8,128)(4,1)} %get-tuple-element.125, bf16[2,3072,96]{1,2,0:T(8,128)(2,1)} %get-tuple-element.126, s32[]{:T(128)} %get-tuple-element.115, bf16[2,1024,2,96]{1,3,2,0:T(8,128)(2,1)} %get-tuple-element.127), kind=kOutput, calls=%fused_computation.60.clone.1 | convolution fusion | flops 1245711360 | bytes 19866624 | tf_op jit(solution)/shard_map/while/body/eval_jaxpr/sub | solution.py:237
  173.1 7.6 %fusion.83 = bf16[2,1024,2,96]{1,3,2,0:T(8,128)(2,1)} fusion(bf16[2,1024,2,96]{1,3,2,0:T(8,128)(2,1)} %get-tuple-element.116, s32[]{:T(128)} %get-tuple-element.115, bf16[2,1024,3072]{1,2,0:T(8,128)(2,1)} %get-tuple-element.106, bf16[2,3072,96]{1,2,0:T(8,128)(2,1)} %get-tuple-element.124, f32[1024,2]{0,1:T(2,128)S(1)} %bitcast.135), kind=kOutput, calls=%fused_computation.13.clone.1 | convolution fusion | flops 1208156160 | bytes 13968384 | tf_op jit(solution)/shard_map/while/body/eval_jaxpr/gqk,kd->qgd/dot_general | solution.py:239
  180.7 2.0 convert_element_type.62
  182.8 1.8 copy.44
  184.6 5.0 %all-to-all-start.3 = ((bf16[4,256,192]{1,2,0:T(8,128)(2,1)}), bf16[4,256,192]{1,2,0:T(8,128)(2,1)}, u32[]{:S(2)}, u32[]{:S(2)}) async-start(bf16[4,256,192]{1,2,0:T(8,128)(2,1)} %copy.44), calls=%async_computation.3 | async-start | bytes 786432 | tf_op jit(solution)/shard_map/all_to_all | solution.py:204
  189.5 1.8 copy.51
  191.3 10.6 %all-to-all-done.3 = bf16[4,256,192]{1,2,0:T(8,128)(2,1)} async-done(((bf16[4,256,192]{1,2,0:T(8,128)(2,1)}), bf16[4,256,192]{1,2,0:T(8,128)(2,1)}, u32[]{:S(2)}, u32[]{:S(2)}) %all-to-all-start.3) | async-done | bytes 393248 | tf_op jit(solution)/shard_map/all_to_all | solution.py:204
  201.9 5.0 %all-to-all-start.4 = ((bf16[4,256,192]{1,2,0:T(8,128)(2,1)}), bf16[4,256,192]{1,2,0:T(8,128)(2,1)}, u32[]{:S(2)}, u32[]{:S(2)}) async-start(bf16[4,256,192]{1,2,0:T(8,128)(2,1)} %bitcast.130), calls=%async_computation.4 | async-start | bytes 786432 | tf_op jit(solution)/shard_map/all_to_all | solution.py:205
  206.9 13.4 %all-gather.5.cloned.1.call-done = bf16[1024,1536]{0,1:T(8,128)(2,1)} async-done(((bf16[1024,384]{0,1:T(8,128)(2,1)}), bf16[1024,1536]{0,1:T(8,128)(2,1)}) %all-gather.5.cloned.1.call-update) | async-done | bytes 3145744 | tf_op jit(solution)/shard_map/all_gather | solution.py:251
  220.2 4.6 %convolution_convert_fusion = bf16[1024,384]{1,0:T(8,128)(2,1)} fusion(bf16[1024,1536]{0,1:T(8,128)(2,1)} %all-gather.5.cloned.1.call-done, bf16[1536,1152]{1,0:T(8,128)(2,1)S(1)} %bitcast.124), kind=kOutput, calls=%fused_computation.37 | convolution fusion | flops 1208352768 | bytes 5111808 | tf_op jit(solution)/shard_map/dot_general | solution.py:252
  224.8 3.7 %all-to-all-start.2 = ((bf16[4,256,384]{2,1,0:T(8,128)(2,1)}), bf16[4,256,384]{2,1,0:T(8,128)(2,1)S(1)}, u32[]{:S(2)}, u32[]{:S(2)}) async-start(bf16[4,256,384]{2,1,0:T(8,128)(2,1)} %bitcast.134), calls=%async_computation.2 | async-start | bytes 1572864 | tf_op jit(solution)/shard_map/all_to_all | solution.py:253
  228.5 1.9 copy.46
  230.4 1.9 copy.47
  232.4 8.5 %all-to-all-done.2 = bf16[4,256,384]{2,1,0:T(8,128)(2,1)S(1)} async-done(((bf16[4,256,384]{2,1,0:T(8,128)(2,1)}), bf16[4,256,384]{2,1,0:T(8,128)(2,1)S(1)}, u32[]{:S(2)}, u32[]{:S(2)}) %all-to-all-start.2) | async-done | bytes 786464 | tf_op jit(solution)/shard_map/all_to_all | solution.py:253
  240.8 0.6 copy.43
  241.4 1.2 broadcast_in_dim.58
  (35 shorter events, 0.2 us)
Async XLA Ops:
  7.2 4.5 %copy-start.7 = (bf16[1,512,768]{2,1,0:T(8,128)(2,1)S(1)}, bf16[1,512,768]{2,1,0:T(8,128)(2,1)}, u32[]{:S(2)}) copy-start(bf16[1,512,768]{2,1,0:T(8,128)(2,1)} %param.13) | copy-start | bytes 2359300
  7.2 109.1 %all-gather.3.cloned.1.call-start = ((), (), s32[]{:S(2)}) async-start(), calls=%async_computation.5 | async-start | bytes 3932160 | tf_op jit(solution)/shard_map/all_gather | solution.py:187
  8.0 12.4 %copy-start.8 = (bf16[24,384]{1,0:T(8,128)(2,1)S(1)}, bf16[24,384]{1,0:T(8,128)(2,1)}, u32[]{:S(2)}) copy-start(bf16[24,384]{1,0:T(8,128)(2,1)} %param.16) | copy-start | bytes 55300
  8.0 12.4 %copy-start.9 = (bf16[24,384]{1,0:T(8,128)(2,1)S(1)}, bf16[24,384]{1,0:T(8,128)(2,1)}, u32[]{:S(2)}) copy-start(bf16[24,384]{1,0:T(8,128)(2,1)} %param.19) | copy-start | bytes 55300
  8.0 12.4 %copy-start.10 = (bf16[24,192]{1,0:T(8,128)(2,1)S(1)}, bf16[24,192]{1,0:T(8,128)(2,1)}, u32[]{:S(2)}) copy-start(bf16[24,192]{1,0:T(8,128)(2,1)} %param.17) | copy-start | bytes 27652
  8.0 12.4 %copy-start.11 = (bf16[24,192]{1,0:T(8,128)(2,1)S(1)}, bf16[24,192]{1,0:T(8,128)(2,1)}, u32[]{:S(2)}) copy-start(bf16[24,192]{1,0:T(8,128)(2,1)} %param.18) | copy-start | bytes 27652
  13.0 78.3 %all-to-all-start.1 = ((bf16[512,4,192]{0,2,1:T(8,128)(2,1)}), bf16[512,4,192]{0,2,1:T(8,128)(2,1)}, u32[]{:S(2)}, u32[]{:S(2)}) async-start(bf16[512,4,192]{0,2,1:T(8,128)(2,1)} %bitcast.19), calls=%async_computation.1 | async-start | bytes 1572864 | tf_op jit(solution)/shard_map/all_to_all | solution.py:207
  91.3 19.6 %all-to-all-start = ((bf16[512,4,192]{0,2,1:T(8,128)(2,1)}), bf16[512,4,192]{0,2,1:T(8,128)(2,1)}, u32[]{:S(2)}, u32[]{:S(2)}) async-start(bf16[512,4,192]{0,2,1:T(8,128)(2,1)} %bitcast.126), calls=%async_computation | async-start | bytes 1572864 | tf_op jit(solution)/shard_map/all_to_all | solution.py:208
  98.5 121.7 %all-gather.5.cloned.1.call-start = ((), (), s32[]{:S(2)}) async-start(), calls=%async_computation.6 | async-start | bytes 3932160 | tf_op jit(solution)/shard_map/all_gather | solution.py:251
  116.3 3.2 %copy-start.4 = (f32[1024,48]{0,1:T(8,128)S(1)}, f32[1024,48]{0,1:T(8,128)}, u32[]{:S(2)}) copy-start(f32[1024,48]{0,1:T(8,128)} %get-tuple-element.63) | copy-start | bytes 589828
  116.3 3.2 %copy-start.5 = (f32[1024,48]{0,1:T(8,128)S(1)}, f32[1024,48]{0,1:T(8,128)}, u32[]{:S(2)}) copy-start(f32[1024,48]{0,1:T(8,128)} %get-tuple-element.64) | copy-start | bytes 589828
  116.3 3.4 %copy-start.1 = (bf16[1024,1536]{1,0:T(8,128)(2,1)S(1)}, bf16[1024,1536]{1,0:T(8,128)(2,1)}, u32[]{:S(2)}) copy-start(bf16[1024,1536]{1,0:T(8,128)(2,1)} %all-gather.3.cloned.1.call-done) | copy-start | bytes 9437188
  121.2 1.1 copy-start.2
  121.5 0.7 copy-start
  123.4 2.3 copy-start.3
  125.7 1.2 copy-start.6
  184.6 17.3 %all-to-all-start.3 = ((bf16[4,256,192]{1,2,0:T(8,128)(2,1)}), bf16[4,256,192]{1,2,0:T(8,128)(2,1)}, u32[]{:S(2)}, u32[]{:S(2)}) async-start(bf16[4,256,192]{1,2,0:T(8,128)(2,1)} %copy.44), calls=%async_computation.3 | async-start | bytes 786432 | tf_op jit(solution)/shard_map/all_to_all | solution.py:204
  201.9 22.9 %all-to-all-start.4 = ((bf16[4,256,192]{1,2,0:T(8,128)(2,1)}), bf16[4,256,192]{1,2,0:T(8,128)(2,1)}, u32[]{:S(2)}, u32[]{:S(2)}) async-start(bf16[4,256,192]{1,2,0:T(8,128)(2,1)} %bitcast.130), calls=%async_computation.4 | async-start | bytes 786432 | tf_op jit(solution)/shard_map/all_to_all | solution.py:205
  224.8 16.0 %all-to-all-start.2 = ((bf16[4,256,384]{2,1,0:T(8,128)(2,1)}), bf16[4,256,384]{2,1,0:T(8,128)(2,1)S(1)}, u32[]{:S(2)}, u32[]{:S(2)}) async-start(bf16[4,256,384]{2,1,0:T(8,128)(2,1)} %bitcast.134), calls=%async_computation.2 | async-start | bytes 1572864 | tf_op jit(solution)/shard_map/all_to_all | solution.py:253
Sparse Core Ops, SparseCore 0:
  11.8 44.5 all-gather.2
  180.9 39.2 all-gather.4

commit v4 on v3

--- a/solution.py
+++ b/solution.py
@@ -193,6 +193,8 @@
     wv = cols[:, q_cols + k_cols:q_cols + k_cols + v_cols]
     wo = cols[:, q_cols + k_cols + v_cols:]
 
+    wo_full = lax.all_gather(wo, "kv", axis=1, tiled=True)
+
     positions = (length + jnp.arange(appended, dtype=jnp.int32)).astype(jnp.float32)
     proj_q = jnp.dot(normed_all, wq, preferred_element_type=jnp.float32)
     proj_k = jnp.dot(normed_all, wk, preferred_element_type=jnp.float32)
@@ -248,9 +250,8 @@
     context = (
         jnp.transpose(contexts, (1, 0, 2, 3)).reshape(appended, heads_here * HD).astype(jnp.bfloat16)
     )
-    context_all = lax.all_gather(context, "kv", axis=1, tiled=True)
-    attended_cols = jnp.dot(context_all, wo, preferred_element_type=jnp.float32).astype(jnp.bfloat16)
-    attended = lax.all_to_all(attended_cols, "kv", split_axis=0, concat_axis=1, tiled=True)
+    context_rows = lax.all_to_all(context, "kv", split_axis=0, concat_axis=1, tiled=True)
+    attended = jnp.dot(context_rows, wo_full, preferred_element_type=jnp.float32).astype(jnp.bfloat16)
     return (attended[None], new_keys[None], new_values[None])
 
 

time: 251 us -> 237 us (0.944)
  waiting for transfers between devices: 35.3 us -> 19.2 us
    all_gather x1, waiting for transfers between devices: 13.4 us -> 0.01 us  [body(): wo_full = lax.all_gather(wo, 'kv', axis=1, tiled=True)]
    all_to_all x1, waiting for transfers between devices: 10.6 us -> 0.01 us  [body(): lax.all_to_all(keys_new, 'kv', split_axis=0, concat_axis=1, tiled=True)]
    all_to_all x1, waiting for transfers between devices: 2.88 us -> 9.71 us  [body(): lax.all_to_all(value_cache[0], 'kv', split_axis=1, concat_axis=0, tiled=T...]
    convert_element_type x0 -> x2, local copies, waits for them, and re-layouts: none -> 2.93 us  [body(): jnp.transpose(contexts, (1, 0, 2, 3)).reshape(appended, heads_here * HD)]
    sub x2, matrix products: 38.5 us -> 35.9 us  [attend(): weights = jnp.where(visible[None], jnp.exp(score - peak[..., None]), 0.0)]
    unnamed x28 -> x32, local copies, waits for them, and re-layouts: 8.24 us -> 6.34 us
  transfers between devices with their start and end apart: 7 -> 7, of which waited for: 4 -> 2; matrix products, arithmetic and copies ran while one was open for 15% -> 42% of each run, Pallas kernels for 25% -> 26%
where the time goes in v4:
time: 237 us; the launch traced here: 235 us
  matrix products  63.8 us (27%)
  Pallas kernels  62.1 us (26%)
  starting transfers between devices  30 us (13%)
  local copies, waits for them, and re-layouts  28.9 us (12%)
  waiting for transfers between devices  19.2 us (8%)
  other arithmetic  16 us (7%)
  between operations  14.9 us (6%)
    pallas_call x1, Pallas kernels, gather_req(): pl.pallas_call(functools.partial(plane_ring_kernel, planes, runs), out_sh...  62.1 us
    sub x2, matrix products, attend(): weights = jnp.where(visible[None], jnp.exp(score - peak[..., None]), 0.0)  35.9 us
    dot_general x2, matrix products, attend(): jnp.einsum('gqk,kd->qgd', weights.astype(jnp.bfloat16), value_block, pref...  15.3 us
    all_to_all x1, waiting for transfers between devices, body(): lax.all_to_all(value_cache[0], 'kv', split_axis=1, concat_axis=0, tiled=T...  9.71 us
    all_to_all x1, waiting for transfers between devices, body(): lax.all_to_all(context, 'kv', split_axis=0, concat_axis=1, tiled=True)  9.46 us
    all_to_all x1, starting transfers between devices, body(): lax.all_to_all(key_cache[0], 'kv', split_axis=1, concat_axis=0, tiled=True)  7.39 us
    all_to_all x1, starting transfers between devices, body(): lax.all_to_all(value_cache[0], 'kv', split_axis=1, concat_axis=0, tiled=T...  7.08 us
    unnamed x32, local copies, waits for them, and re-layouts  6.34 us
  transfers between devices with their start and end apart: 7, of which 2 were waited for; matrix products, arithmetic and copies ran while one was open for 42% of the time, Pallas kernels for 26%

profile of v4, /device:TPU:1, one launch (start us, length us, event | category | flops | bytes accessed | tf_op | source)
XLA Modules:
  0.0 234.8 jit_solution(10024467772439089973)
XLA Ops:
  7.2 0.0 all-gather.3.cloned.1.call-start
  7.2 0.8 convert_element_type.53
  8.0 1.4 fusion.50
  9.4 2.3 fusion.52
  11.8 0.0 all-gather.3.cloned.1.call-update
  11.8 1.2 copy.39
  13.0 7.4 %all-to-all-start.1 = ((bf16[512,4,192]{0,2,1:T(8,128)(2,1)}), bf16[512,4,192]{0,2,1:T(8,128)(2,1)}, u32[]{:S(2)}, u32[]{:S(2)}) async-start(bf16[512,4,192]{0,2,1:T(8,128)(2,1)} %bitcast.19), calls=%async_computation.1 | async-start | bytes 1572864 | tf_op jit(solution)/shard_map/all_to_all | solution.py:209
  20.4 0.7 concatenate.28.src_ref
  21.1 62.1 %shard_map.112 = bf16[8,8,24,1152]{3,2,1,0:T(8,128)(2,1)} custom-call(bf16[24,1152]{1,0:T(8,128)(2,1)} %concatenate.28.src_ref), custom_call_target="tpu_custom_call" | custom-call | tf_op jit(solution)/shard_map/pallas_call | solution.py:149
  83.2 2.3 copy.38
  85.5 1.2 slice.39
  86.6 0.0 all-gather.5.cloned.1.call-update
  87.3 2.3 copy.36
  89.7 1.3 iota_compare_fusion
  90.9 1.5 multiply_cosine_fusion
  92.5 7.1 %all-to-all-start = ((bf16[512,4,192]{0,2,1:T(8,128)(2,1)}), bf16[512,4,192]{0,2,1:T(8,128)(2,1)}, u32[]{:S(2)}, u32[]{:S(2)}) async-start(bf16[512,4,192]{0,2,1:T(8,128)(2,1)} %bitcast.134), calls=%async_computation | async-start | bytes 1572864 | tf_op jit(solution)/shard_map/all_to_all | solution.py:210
  99.6 4.3 %pad_add_fusion = pred[1024,3072]{0,1:T(8,128)(4,1)} fusion(pred[1024,1024]{0,1:T(8,128)(4,1)} %iota_compare_fusion, pred[3072]{0:T(1024)(128)(4,1)S(1)} %pad.6.clone), kind=kLoop, calls=%fused_computation.30 | loop fusion | flops 3145728 | bytes 4197376 | tf_op jit(solution)/shard_map/concatenate | solution.py:218
  103.8 2.6 %copy.40 = bf16[4,512,192]{1,0,2:T(4,128)(2,1)} copy(bf16[4,512,192]{1,2,0:T(8,128)(2,1)} %bitcast.20) | data formatting | bytes 1572864 | tf_op jit(solution)/shard_map/all_to_all | solution.py:209
  106.5 2.8 %concatenate.32 = bf16[2048,2,96]{0,2,1:T(8,128)(2,1)} reshape(bf16[4,512,192]{1,0,2:T(4,128)(2,1)} %copy.40) | data formatting | bytes 1572864 | tf_op jit(solution)/shard_map/concatenate | solution.py:213
  109.2 9.7 %all-to-all-done = bf16[512,4,192]{0,2,1:T(8,128)(2,1)} async-done(((bf16[512,4,192]{0,2,1:T(8,128)(2,1)}), bf16[512,4,192]{0,2,1:T(8,128)(2,1)}, u32[]{:S(2)}, u32[]{:S(2)}) %all-to-all-start) | async-done | bytes 786464 | tf_op jit(solution)/shard_map/all_to_all | solution.py:210
  119.0 2.7 %copy.37 = bf16[4,512,192]{1,0,2:T(4,128)(2,1)} copy(bf16[4,512,192]{1,2,0:T(8,128)(2,1)} %bitcast.10) | data formatting | bytes 1572864 | tf_op jit(solution)/shard_map/all_to_all | solution.py:210
  121.6 2.8 %concatenate.27 = bf16[2048,2,96]{0,2,1:T(8,128)(2,1)} reshape(bf16[4,512,192]{1,0,2:T(4,128)(2,1)} %copy.37) | data formatting | bytes 1572864 | tf_op jit(solution)/shard_map/concatenate | solution.py:214
  124.4 3.2 %fusion.55 = f32[1024,192]{0,1:T(8,128)S(1)} fusion(bf16[1024,1536]{1,0:T(8,128)(2,1)} %all-gather.3.cloned.1.call-done, bf16[1536,1152]{1,0:T(8,128)(2,1)S(1)} %bitcast.130), kind=kOutput, calls=%fused_computation.44 | convolution fusion | flops 603979776 | bytes 4718592 | tf_op jit(solution)/shard_map/dot_general | solution.py:200
  127.6 0.1 multiply_subtract_fusion
  127.7 0.8 maximum_convert_fusion
  128.5 2.0 convert_element_type.63
  130.5 1.8 copy.42
  132.3 5.8 %all-to-all-start.3 = ((bf16[4,256,192]{1,2,0:T(8,128)(2,1)}), bf16[4,256,192]{1,2,0:T(8,128)(2,1)}, u32[]{:S(2)}, u32[]{:S(2)}) async-start(bf16[4,256,192]{1,2,0:T(8,128)(2,1)} %copy.42), calls=%async_computation.3 | async-start | bytes 786432 | tf_op jit(solution)/shard_map/all_to_all | solution.py:206
  138.2 3.5 %fusion.53 = f32[1024,384]{0,1:T(8,128)S(1)} fusion(bf16[1024,1536]{1,0:T(8,128)(2,1)} %all-gather.3.cloned.1.call-done, bf16[1536,1152]{1,0:T(8,128)(2,1)S(1)} %bitcast.131), kind=kOutput, calls=%fused_computation.40 | convolution fusion | flops 1207959552 | bytes 5898240 | tf_op jit(solution)/shard_map/dot_general | solution.py:199
  141.7 1.4 convolution_convert_fusion.1
  143.1 0.8 copy.49
  143.9 0.2 subtract_convert_fusion
  144.1 1.0 pad_maximum_fusion
  145.1 1.1 maximum_bitcast_fusion.1
  146.2 1.1 maximum_bitcast_fusion
  147.4 4.8 %all-to-all-start.4 = ((bf16[4,256,192]{1,2,0:T(8,128)(2,1)}), bf16[4,256,192]{1,2,0:T(8,128)(2,1)S(1)}, u32[]{:S(2)}, u32[]{:S(2)}) async-start(bf16[4,256,192]{1,2,0:T(8,128)(2,1)} %bitcast.109), calls=%async_computation.4 | async-start | bytes 786432 | tf_op jit(solution)/shard_map/all_to_all | solution.py:207
  152.2 51.2 %while.10 = (s32[]{:T(128)}, bf16[2,1024,2,96]{1,3,2,0:T(8,128)(2,1)}, bf16[2,3072,96]{1,2,0:T(8,128)(2,1)}, pred[1024,3072]{0,1:T(8,128)(4,1)S(1)}, bf16[2,3072...) while((s32[]{:T(128)}, bf16[2,1024,2,96]{1,3,2,0:T(8,128)(2,1)}, ...), condition=%wide.region_4.5_spmd, body=%wide.region_1.4_spmd.sunk | while | flops 2453867520 | bytes 33835084 | solution.py:249
  152.2 18.0 %fusion.83 = (f32[2,1024]{1,0:T(2,128)S(1)}, bf16[2,1024,3072]{1,2,0:T(8,128)(2,1)}) fusion(pred[1024,3072]{0,1:T(8,128)(4,1)S(1)} %get-tuple-element.125, bf16[2,3072,96]{1,2,0:T(8,128)(2,1)} %get-tuple-element.126, s32[]{:T(128)} %get-tuple-element.115, bf16[2,1024,2,96]{1,3,2,0:T(8,128)(2,1)} %get-tuple-element.127), kind=kOutput, calls=%fused_computation.61.clone.1 | convolution fusion | flops 1245711360 | bytes 19866624 | tf_op jit(solution)/shard_map/while/body/eval_jaxpr/sub | solution.py:239
  170.1 7.6 %fusion.84 = bf16[2,1024,2,96]{1,3,2,0:T(8,128)(2,1)} fusion(bf16[2,1024,2,96]{1,3,2,0:T(8,128)(2,1)} %get-tuple-element.116, s32[]{:T(128)} %get-tuple-element.115, bf16[2,1024,3072]{1,2,0:T(8,128)(2,1)} %get-tuple-element.106, bf16[2,3072,96]{1,2,0:T(8,128)(2,1)} %get-tuple-element.124, f32[1024,2]{0,1:T(2,128)S(1)} %bitcast.142), kind=kOutput, calls=%fused_computation.13.clone.1 | convolution fusion | flops 1208156160 | bytes 13968384 | tf_op jit(solution)/shard_map/while/body/eval_jaxpr/gqk,kd->qgd/dot_general | solution.py:241
  177.8 17.9 %fusion.83 = (f32[2,1024]{1,0:T(2,128)S(1)}, bf16[2,1024,3072]{1,2,0:T(8,128)(2,1)}) fusion(pred[1024,3072]{0,1:T(8,128)(4,1)S(1)} %get-tuple-element.125, bf16[2,3072,96]{1,2,0:T(8,128)(2,1)} %get-tuple-element.126, s32[]{:T(128)} %get-tuple-element.115, bf16[2,1024,2,96]{1,3,2,0:T(8,128)(2,1)} %get-tuple-element.127), kind=kOutput, calls=%fused_computation.61.clone.1 | convolution fusion | flops 1245711360 | bytes 19866624 | tf_op jit(solution)/shard_map/while/body/eval_jaxpr/sub | solution.py:239
  195.7 7.6 %fusion.84 = bf16[2,1024,2,96]{1,3,2,0:T(8,128)(2,1)} fusion(bf16[2,1024,2,96]{1,3,2,0:T(8,128)(2,1)} %get-tuple-element.116, s32[]{:T(128)} %get-tuple-element.115, bf16[2,1024,3072]{1,2,0:T(8,128)(2,1)} %get-tuple-element.106, bf16[2,3072,96]{1,2,0:T(8,128)(2,1)} %get-tuple-element.124, f32[1024,2]{0,1:T(2,128)S(1)} %bitcast.142), kind=kOutput, calls=%fused_computation.13.clone.1 | convolution fusion | flops 1208156160 | bytes 13968384 | tf_op jit(solution)/shard_map/while/body/eval_jaxpr/gqk,kd->qgd/dot_general | solution.py:241
  203.3 1.9 convert_element_type.61
  205.3 1.0 copy.41
  206.3 4.8 %all-to-all-start.2 = ((bf16[4,256,384]{1,2,0:T(8,128)(2,1)}), bf16[4,256,384]{1,2,0:T(8,128)(2,1)S(1)}, u32[]{:S(2)}, u32[]{:S(2)}) async-start(bf16[4,256,384]{1,2,0:T(8,128)(2,1)} %copy.41), calls=%async_computation.2 | async-start | bytes 1572864 | tf_op jit(solution)/shard_map/all_to_all | solution.py:253
  211.1 1.9 copy.44
  213.0 0.9 copy.45
  213.9 9.5 %all-to-all-done.2 = bf16[4,256,384]{1,2,0:T(8,128)(2,1)S(1)} async-done(((bf16[4,256,384]{1,2,0:T(8,128)(2,1)}), bf16[4,256,384]{1,2,0:T(8,128)(2,1)S(1)}, u32[]{:S(2)}, u32[]{:S(2)}) %all-to-all-start.2) | async-done | bytes 786464 | tf_op jit(solution)/shard_map/all_to_all | solution.py:253
  223.4 4.6 %fusion.49 = bf16[1,256,1536]{2,1,0:T(8,128)(2,1)} fusion(bf16[256,1536]{0,1:T(8,128)(2,1)S(1)} %bitcast.141, bf16[1536,1536]{1,0:T(8,128)(2,1)} %all-gather.5.cloned.1.call-done), kind=kOutput, calls=%fused_computation.33 | convolution fusion | flops 1208352768 | bytes 6291456 | tf_op jit(solution)/shard_map/dot_general | solution.py:254
  (40 shorter events, 0.1 us)
Async XLA Ops:
  7.2 4.6 %copy-start.9 = (bf16[1,512,768]{2,1,0:T(8,128)(2,1)S(1)}, bf16[1,512,768]{2,1,0:T(8,128)(2,1)}, u32[]{:S(2)}) copy-start(bf16[1,512,768]{2,1,0:T(8,128)(2,1)} %param.13) | copy-start | bytes 2359300
  7.2 117.2 %all-gather.3.cloned.1.call-start = ((), (), s32[]{:S(2)}) async-start(), calls=%async_computation.5 | async-start | bytes 3932160 | tf_op jit(solution)/shard_map/all_gather | solution.py:187
  8.0 12.4 %copy-start.10 = (bf16[24,384]{1,0:T(8,128)(2,1)S(1)}, bf16[24,384]{1,0:T(8,128)(2,1)}, u32[]{:S(2)}) copy-start(bf16[24,384]{1,0:T(8,128)(2,1)} %param.16) | copy-start | bytes 55300
  8.0 12.4 %copy-start.11 = (bf16[24,384]{1,0:T(8,128)(2,1)S(1)}, bf16[24,384]{1,0:T(8,128)(2,1)}, u32[]{:S(2)}) copy-start(bf16[24,384]{1,0:T(8,128)(2,1)} %param.19) | copy-start | bytes 55300
  8.0 12.4 %copy-start.12 = (bf16[24,192]{1,0:T(8,128)(2,1)S(1)}, bf16[24,192]{1,0:T(8,128)(2,1)}, u32[]{:S(2)}) copy-start(bf16[24,192]{1,0:T(8,128)(2,1)} %param.17) | copy-start | bytes 27652
  8.0 12.4 %copy-start.13 = (bf16[24,192]{1,0:T(8,128)(2,1)S(1)}, bf16[24,192]{1,0:T(8,128)(2,1)}, u32[]{:S(2)}) copy-start(bf16[24,192]{1,0:T(8,128)(2,1)} %param.18) | copy-start | bytes 27652
  13.0 79.5 %all-to-all-start.1 = ((bf16[512,4,192]{0,2,1:T(8,128)(2,1)}), bf16[512,4,192]{0,2,1:T(8,128)(2,1)}, u32[]{:S(2)}, u32[]{:S(2)}) async-start(bf16[512,4,192]{0,2,1:T(8,128)(2,1)} %bitcast.19), calls=%async_computation.1 | async-start | bytes 1572864 | tf_op jit(solution)/shard_map/all_to_all | solution.py:209
  20.4 203.0 %all-gather.5.cloned.1.call-start = ((), (), s32[]{:S(2)}) async-start(), calls=%async_computation.6 | async-start | bytes 5898240 | tf_op jit(solution)/shard_map/all_gather | solution.py:196
  92.5 26.5 %all-to-all-start = ((bf16[512,4,192]{0,2,1:T(8,128)(2,1)}), bf16[512,4,192]{0,2,1:T(8,128)(2,1)}, u32[]{:S(2)}, u32[]{:S(2)}) async-start(bf16[512,4,192]{0,2,1:T(8,128)(2,1)} %bitcast.134), calls=%async_computation | async-start | bytes 1572864 | tf_op jit(solution)/shard_map/all_to_all | solution.py:210
  124.4 3.2 %copy-start.5 = (f32[1024,48]{0,1:T(8,128)S(1)}, f32[1024,48]{0,1:T(8,128)}, u32[]{:S(2)}) copy-start(f32[1024,48]{0,1:T(8,128)} %get-tuple-element.63) | copy-start | bytes 589828
  124.4 3.2 %copy-start.7 = (f32[1024,48]{0,1:T(8,128)S(1)}, f32[1024,48]{0,1:T(8,128)}, u32[]{:S(2)}) copy-start(f32[1024,48]{0,1:T(8,128)} %get-tuple-element.64) | copy-start | bytes 589828
  132.3 15.0 %all-to-all-start.3 = ((bf16[4,256,192]{1,2,0:T(8,128)(2,1)}), bf16[4,256,192]{1,2,0:T(8,128)(2,1)}, u32[]{:S(2)}, u32[]{:S(2)}) async-start(bf16[4,256,192]{1,2,0:T(8,128)(2,1)} %copy.42), calls=%async_computation.3 | async-start | bytes 786432 | tf_op jit(solution)/shard_map/all_to_all | solution.py:206
  138.2 3.5 %copy-start.1 = (bf16[1024,1536]{1,0:T(8,128)(2,1)S(1)}, bf16[1024,1536]{1,0:T(8,128)(2,1)}, u32[]{:S(2)}) copy-start(bf16[1024,1536]{1,0:T(8,128)(2,1)} %all-gather.3.cloned.1.call-done) | copy-start | bytes 9437188
  141.7 2.2 copy-start.6
  141.7 2.2 copy-start.8
  143.1 2.0 copy-start
  143.1 2.0 copy-start.3
  143.9 2.4 %copy-start.4 = (bf16[2048,2,96]{0,2,1:T(8,128)(2,1)S(1)}, bf16[2048,2,96]{0,2,1:T(8,128)(2,1)}, u32[]{:S(2)}) copy-start(bf16[2048,2,96]{0,2,1:T(8,128)(2,1)} %concatenate.27) | copy-start | bytes 2359300
  145.1 7.1 %copy-start.2 = (pred[1024,3072]{0,1:T(8,128)(4,1)S(1)}, pred[1024,3072]{0,1:T(8,128)(4,1)}, u32[]{:S(2)}) copy-start(pred[1024,3072]{0,1:T(8,128)(4,1)} %pad_add_fusion) | copy-start | bytes 9437188
  147.4 58.9 %all-to-all-start.4 = ((bf16[4,256,192]{1,2,0:T(8,128)(2,1)}), bf16[4,256,192]{1,2,0:T(8,128)(2,1)S(1)}, u32[]{:S(2)}, u32[]{:S(2)}) async-start(bf16[4,256,192]{1,2,0:T(8,128)(2,1)} %bitcast.109), calls=%async_computation.4 | async-start | bytes 786432 | tf_op jit(solution)/shard_map/all_to_all | solution.py:207
  206.3 17.1 %all-to-all-start.2 = ((bf16[4,256,384]{1,2,0:T(8,128)(2,1)}), bf16[4,256,384]{1,2,0:T(8,128)(2,1)S(1)}, u32[]{:S(2)}, u32[]{:S(2)}) async-start(bf16[4,256,384]{1,2,0:T(8,128)(2,1)} %copy.41), calls=%async_computation.2 | async-start | bytes 1572864 | tf_op jit(solution)/shard_map/all_to_all | solution.py:253
Sparse Core Ops, SparseCore 0:
  11.9 44.4 all-gather.2
  86.8 52.5 all-gather.4

commit v5 on v4

--- a/solution.py
+++ b/solution.py
@@ -169,6 +169,89 @@
     return ordered.reshape(count * rows, width)
 
 
+BLOCK_Q = 512
+BLOCK_K = 512
+
+
+def flash_kernel(tokens, scale, len_ref, q_ref, kc_ref, vc_ref, kn_ref, vn_ref, o_ref):
+    block_q = q_ref.shape[1]
+    block_k = BLOCK_K
+    width = q_ref.shape[2]
+    i = pl.program_id(1)
+    length = len_ref[0]
+    first = lax.rem(i * block_q, tokens)
+    q = q_ref[0]
+    query_index = first + lax.broadcasted_iota(jnp.int32, (block_q, block_k), 0)
+    key_offset = lax.broadcasted_iota(jnp.int32, (block_q, block_k), 1)
+
+    def step(keys, values, visible, carry):
+        peak, total, acc = carry
+        score = lax.dot_general(
+            q, keys, (((1,), (1,)), ((), ())), preferred_element_type=jnp.float32
+        ) * scale
+        score = jnp.where(visible, score, masked_score)
+        new_peak = jnp.maximum(peak, jnp.max(score, axis=1, keepdims=True))
+        alpha = jnp.exp(peak - new_peak)
+        weights = jnp.where(visible, jnp.exp(score - new_peak), 0.0)
+        total = alpha * total + jnp.sum(weights, axis=1, keepdims=True)
+        acc = alpha * acc + jnp.dot(
+            weights.astype(jnp.bfloat16), values, preferred_element_type=jnp.float32
+        )
+        return new_peak, total, acc
+
+    def cache_step(block, carry):
+        start = pl.multiple_of(block * block_k, block_k)
+        keys = kc_ref[0, pl.ds(start, block_k), :]
+        values = vc_ref[0, pl.ds(start, block_k), :]
+        visible = start + key_offset < length
+        return step(keys, values, visible, carry)
+
+    def new_step(block, carry):
+        start = pl.multiple_of(block * block_k, block_k)
+        keys = kn_ref[0, pl.ds(start, block_k), :]
+        values = vn_ref[0, pl.ds(start, block_k), :]
+        visible = start + key_offset <= query_index
+        return step(keys, values, visible, carry)
+
+    carry = (
+        jnp.full((block_q, 1), -jnp.inf, jnp.float32),
+        jnp.zeros((block_q, 1), jnp.float32),
+        jnp.zeros((block_q, width), jnp.float32),
+    )
+    live_blocks = (length + block_k - 1) // block_k
+    carry = lax.fori_loop(0, live_blocks, cache_step, carry)
+    new_blocks = (first + block_q - 1) // block_k + 1
+    peak, total, acc = lax.fori_loop(0, new_blocks, new_step, carry)
+    o_ref[0] = (acc / total).astype(o_ref.dtype)
+
+
+def flash_attention(lengths, queries, keys_old, values_old, keys_new, values_new, tokens, scale):
+    heads, rows, width = queries.shape
+    slots = keys_old.shape[1]
+    block_q = min(BLOCK_Q, tokens)
+    grid = (heads, rows // block_q)
+    whole_cache = pl.BlockSpec((1, slots, width), lambda c, i, n: (c, 0, 0))
+    whole_new = pl.BlockSpec((1, tokens, width), lambda c, i, n: (c, 0, 0))
+    return pl.pallas_call(
+        functools.partial(flash_kernel, tokens, scale),
+        out_shape=jax.ShapeDtypeStruct((heads, rows, width), jnp.bfloat16),
+        grid_spec=pltpu.PrefetchScalarGridSpec(
+            num_scalar_prefetch=1,
+            grid=grid,
+            in_specs=[
+                pl.BlockSpec((1, block_q, width), lambda c, i, n: (c, i, 0)),
+                whole_cache, whole_cache, whole_new, whole_new,
+            ],
+            out_specs=pl.BlockSpec((1, block_q, width), lambda c, i, n: (c, i, 0)),
+        ),
+        cost_estimate=pl.CostEstimate(
+            flops=4 * heads * rows * (slots + tokens) * width,
+            transcendentals=heads * rows * (slots + tokens),
+            bytes_accessed=2 * width * heads * (2 * rows + 2 * slots + 2 * tokens),
+        ),
+    )(lengths, queries, keys_old, values_old, keys_new, values_new)
+
+
 def body(hidden, lengths, key_cache, value_cache, norm_gain, w_query, w_key, w_value, w_out):
     rows_here = hidden.shape[1]
     kv_count = lax.axis_size("kv")
@@ -210,46 +293,20 @@
     values_old = lax.all_to_all(value_cache[0], "kv", split_axis=1, concat_axis=0, tiled=True)
     cache_slots = keys_old.shape[0]
 
-    keys_all = jnp.concatenate([keys_old, keys_new], axis=0)
-    values_all = jnp.concatenate([values_old, values_new], axis=0)
-    key_count = keys_all.shape[0]
-    query_index = jnp.arange(appended, dtype=jnp.int32)
-    cache_live = jnp.arange(cache_slots, dtype=jnp.int32) < length
-    visible = jnp.concatenate(
-        [
-            jnp.broadcast_to(cache_live[None, :], (appended, cache_slots)),
-            query_index[None, :] <= query_index[:, None],
-        ],
-        axis=1,
-    )
+    def by_head(values):
+        count = values.shape[0]
+        return jnp.transpose(values.reshape(count, kv_heads_here, HD), (1, 0, 2))
+
     query_heads = jnp.transpose(
-        queries.reshape(appended, kv_heads_here, groups, HD), (1, 0, 2, 3)
-    )
-    key_heads = jnp.transpose(keys_all.reshape(key_count, kv_heads_here, HD), (1, 0, 2))
-    value_heads = jnp.transpose(values_all.reshape(key_count, kv_heads_here, HD), (1, 0, 2))
-
-    def attend(operands):
-        query_block, key_block, value_block = operands
-        score = (
-            jnp.einsum("qgd,kd->gqk", query_block, key_block, preferred_element_type=jnp.float32)
-            * scale
-        )
-        score = jnp.where(visible[None], score, masked_score)
-        peak = jnp.max(score, axis=-1)
-        weights = jnp.where(visible[None], jnp.exp(score - peak[..., None]), 0.0)
-        total = jnp.sum(weights, axis=-1)
-        context = jnp.einsum(
-            "gqk,kd->qgd",
-            weights.astype(jnp.bfloat16),
-            value_block,
-            preferred_element_type=jnp.float32,
-        )
-        return context / jnp.transpose(total)[:, :, None]
-
-    contexts = lax.map(attend, (query_heads, key_heads, value_heads))
-    context = (
-        jnp.transpose(contexts, (1, 0, 2, 3)).reshape(appended, heads_here * HD).astype(jnp.bfloat16)
-    )
+        queries.reshape(appended, kv_heads_here, groups, HD), (1, 2, 0, 3)
+    ).reshape(kv_heads_here, groups * appended, HD)
+    contexts = flash_attention(
+        lengths, query_heads, by_head(keys_old), by_head(values_old),
+        by_head(keys_new), by_head(values_new), appended, scale,
+    )
+    context = jnp.transpose(
+        contexts.reshape(kv_heads_here, groups, appended, HD), (2, 0, 1, 3)
+    ).reshape(appended, heads_here * HD)
     context_rows = lax.all_to_all(context, "kv", split_axis=0, concat_axis=1, tiled=True)
     attended = jnp.dot(context_rows, wo_full, preferred_element_type=jnp.float32).astype(jnp.bfloat16)
     return (attended[None], new_keys[None], new_values[None])

time: 237 us -> 247 us (1.042)
  the two profiles are of different devices: /device:TPU:1 before, /device:TPU:78 now
where the time goes in v5:
time: 247 us; the launch traced here: 246 us
  Pallas kernels  93.9 us (38%)
  local copies, waits for them, and re-layouts  52.3 us (21%)
  waiting for transfers between devices  34.9 us (14%)
  starting transfers between devices  22.1 us (9%)
  matrix products  15.1 us (6%)
  between operations  14.9 us (6%)
  other arithmetic  12.5 us (5%)
    pallas_call x1, Pallas kernels, gather_req(): pl.pallas_call(functools.partial(plane_ring_kernel, planes, runs), out_sh...  56.7 us
    pallas_call x1, Pallas kernels, flash_attention(): pl.pallas_call(functools.partial(flash_kernel, tokens, scale), out_shape=...  37.2 us
    all_to_all x1, waiting for transfers between devices, body(): lax.all_to_all(key_cache[0], 'kv', split_axis=1, concat_axis=0, tiled=True)  16.2 us
    unnamed x22, local copies, waits for them, and re-layouts  13.1 us
    reshape x5, local copies, waits for them, and re-layouts, by_head(): return jnp.transpose(values.reshape(count, kv_heads_here, HD), (1, 0, 2))  12 us
    all_to_all x1, waiting for transfers between devices, body(): lax.all_to_all(context, 'kv', split_axis=0, concat_axis=1, tiled=True)  10.3 us
    all_to_all x1, waiting for transfers between devices, body(): lax.all_to_all(value_cache[0], 'kv', split_axis=1, concat_axis=0, tiled=T...  8.29 us
    convert_element_type x3, local copies, waits for them, and re-layouts, body(): keys_new = rotate(proj_k, positions).astype(jnp.bfloat16)  5.79 us
  transfers between devices with their start and end apart: 7, of which 3 were waited for; matrix products, arithmetic and copies ran while one was open for 28% of the time, Pallas kernels for 38%

profile of v5, /device:TPU:78, one launch (start us, length us, event | category | flops | bytes accessed | tf_op | source)
XLA Modules:
  0.0 245.7 jit_solution(6265293239583953010)
XLA Ops:
  7.9 1.4 fusion.1
  9.3 2.3 fusion.3
  11.7 0.7 concatenate.10.src_ref
  12.4 56.7 %shard_map.112 = bf16[8,8,24,1152]{3,2,1,0:T(8,128)(2,1)} custom-call(bf16[24,1152]{1,0:T(8,128)(2,1)} %concatenate.10.src_ref), custom_call_target="tpu_custom_call" | custom-call | tf_op jit(solution)/shard_map/pallas_call | solution.py:149
  69.1 2.3 copy.56
  71.4 1.2 slice.39
  72.6 2.3 copy.58
  74.9 4.2 %all-to-all-start = ((bf16[512,4,192]{0,2,1:T(8,128)(2,1)}), bf16[512,4,192]{0,2,1:T(8,128)(2,1)}, u32[]{:S(2)}, u32[]{:S(2)}) async-start(bf16[512,4,192]{0,2,1:T(8,128)(2,1)} %bitcast.67), calls=%async_computation | async-start | bytes 1572864 | tf_op jit(solution)/shard_map/all_to_all | solution.py:292
  79.1 2.4 copy.61
  81.5 16.2 %all-to-all-done = bf16[512,4,192]{0,2,1:T(8,128)(2,1)} async-done(((bf16[512,4,192]{0,2,1:T(8,128)(2,1)}), bf16[512,4,192]{0,2,1:T(8,128)(2,1)}, u32[]{:S(2)}, u32[]{:S(2)}) %all-to-all-start) | async-done | bytes 786464 | tf_op jit(solution)/shard_map/all_to_all | solution.py:292
  97.7 4.2 %all-to-all-start.1 = ((bf16[512,4,192]{0,2,1:T(8,128)(2,1)}), bf16[512,4,192]{0,2,1:T(8,128)(2,1)}, u32[]{:S(2)}, u32[]{:S(2)}) async-start(bf16[512,4,192]{0,2,1:T(8,128)(2,1)} %bitcast.66), calls=%async_computation.1 | async-start | bytes 1572864 | tf_op jit(solution)/shard_map/all_to_all | solution.py:293
  102.6 1.5 multiply_cosine_fusion
  104.1 1.9 copy.65
  106.0 1.9 copy.67
  108.0 2.6 %copy.59 = bf16[4,512,192]{1,0,2:T(4,128)(2,1)} copy(bf16[4,512,192]{1,2,0:T(8,128)(2,1)} %bitcast.11) | data formatting | bytes 1572864 | tf_op jit(solution)/shard_map/all_to_all | solution.py:292
  110.6 2.8 %reshape.137 = bf16[2048,2,96]{0,2,1:T(8,128)(2,1)} reshape(bf16[4,512,192]{1,0,2:T(4,128)(2,1)} %copy.59) | data formatting | bytes 1572864 | tf_op jit(solution)/shard_map/reshape | solution.py:298
  113.4 2.2 copy.60
  115.6 8.3 %all-to-all-done.1 = bf16[512,4,192]{0,2,1:T(8,128)(2,1)} async-done(((bf16[512,4,192]{0,2,1:T(8,128)(2,1)}), bf16[512,4,192]{0,2,1:T(8,128)(2,1)}, u32[]{:S(2)}, u32[]{:S(2)}) %all-to-all-start.1) | async-done | bytes 786464 | tf_op jit(solution)/shard_map/all_to_all | solution.py:293
  123.9 2.7 %copy.62 = bf16[4,512,192]{1,0,2:T(4,128)(2,1)} copy(bf16[4,512,192]{1,2,0:T(8,128)(2,1)} %bitcast.14) | data formatting | bytes 1572864 | tf_op jit(solution)/shard_map/all_to_all | solution.py:293
  126.6 2.8 %reshape.138 = bf16[2048,2,96]{0,2,1:T(8,128)(2,1)} reshape(bf16[4,512,192]{1,0,2:T(4,128)(2,1)} %copy.62) | data formatting | bytes 1572864 | tf_op jit(solution)/shard_map/reshape | solution.py:298
  129.4 2.2 copy.63
  131.6 3.1 %fusion.7 = f32[1024,192]{0,1:T(8,128)S(1)} fusion(bf16[1024,1536]{1,0:T(8,128)(2,1)} %all-gather.3.cloned.1.call-done, bf16[1536,1152]{1,0:T(8,128)(2,1)S(1)} %bitcast.61), kind=kOutput, calls=%fused_computation.14 | convolution fusion | flops 603979776 | bytes 4718592 | tf_op jit(solution)/shard_map/dot_general | solution.py:283
  134.7 0.9 fusion.9
  135.6 2.3 copy.76
  137.9 2.3 copy.77
  140.3 3.4 %fusion.4 = f32[1024,384]{0,1:T(8,128)S(1)} fusion(bf16[1024,1536]{1,0:T(8,128)(2,1)} %all-gather.3.cloned.1.call-done, bf16[1536,1152]{1,0:T(8,128)(2,1)S(1)} %bitcast.62), kind=kOutput, calls=%fused_computation.8 | convolution fusion | flops 1207959552 | bytes 5898240 | tf_op jit(solution)/shard_map/dot_general | solution.py:282
  143.9 0.9 pad_maximum_fusion
  144.9 2.3 copy.57
  147.1 2.1 multiply_subtract_fusion
  149.2 0.8 copy-done
  150.2 1.1 maximum_convert_fusion
  151.3 2.0 copy.71
  153.3 2.0 convert_element_type.47
  155.3 1.8 copy.72
  157.1 4.3 %all-to-all-start.3 = ((bf16[4,256,192]{1,2,0:T(8,128)(2,1)}), bf16[4,256,192]{1,2,0:T(8,128)(2,1)}, u32[]{:S(2)}, u32[]{:S(2)}) async-start(bf16[4,256,192]{1,2,0:T(8,128)(2,1)} %copy.72), calls=%async_computation.3 | async-start | bytes 786432 | tf_op jit(solution)/shard_map/all_to_all | solution.py:289
  161.4 4.0 %convolution_convert_fusion.1 = bf16[1024,192]{0,1:T(8,128)(2,1)} fusion(bf16[1024,1536]{1,0:T(8,128)(2,1)} %all-gather.3.cloned.1.call-done, bf16[1536,1152]{1,0:T(8,128)(2,1)S(1)} %bitcast.63), kind=kOutput, calls=%fused_computation.7 | convolution fusion | flops 604176384 | bytes 4325376 | tf_op jit(solution)/shard_map/dot_general | solution.py:284
  165.4 2.0 copy.68
  167.4 1.8 copy.80
  169.2 2.3 fusion.15.kn_ref
  171.5 4.6 %all-to-all-start.4 = ((bf16[4,256,192]{1,2,0:T(8,128)(2,1)}), bf16[4,256,192]{1,2,0:T(8,128)(2,1)S(1)}, u32[]{:S(2)}, u32[]{:S(2)}) async-start(bf16[4,256,192]{1,2,0:T(8,128)(2,1)} %bitcast.57), calls=%async_computation.4 | async-start | bytes 786432 | tf_op jit(solution)/shard_map/all_to_all | solution.py:290
  176.0 37.2 %shard_map.113 = bf16[2,2048,96]{2,1,0:T(8,128)(2,1)} custom-call(s32[1]{0:T(128)} %copy.81.len_ref, bf16[2,2048,96]{2,1,0:T(8,128)(2,1)} %bitcast.74, bf16[2,2048,96]{2,1,0:T(8,128)(2,1)} %bitcast.72, bf16[2,2048,96]{2,1,0:T(8,128)(2,1)} %bitcast.73, bf16[2,1024,96]{2,1,0:T(8,128)(2,1)} %fusion.15.kn_ref, bf16[2,1024,96]{2,1,0:T(8,128)(2,1)} %bitcast.77), custom_call_target="tpu_custom_call" | custom-call | flops 4831838208 | bytes 3932160 | tf_op jit(solution)/shard_map/pallas_call | solution.py:235
  213.3 1.5 copy.69
  215.3 1.0 copy.70
  216.3 4.8 %all-to-all-start.2 = ((bf16[4,256,384]{1,2,0:T(8,128)(2,1)}), bf16[4,256,384]{1,2,0:T(8,128)(2,1)S(1)}, u32[]{:S(2)}, u32[]{:S(2)}) async-start(bf16[4,256,384]{1,2,0:T(8,128)(2,1)} %copy.70), calls=%async_computation.2 | async-start | bytes 1572864 | tf_op jit(solution)/shard_map/all_to_all | solution.py:310
  221.1 1.9 copy.74
  223.0 0.9 copy.75
  223.9 10.3 %all-to-all-done.2 = bf16[4,256,384]{1,2,0:T(8,128)(2,1)S(1)} async-done(((bf16[4,256,384]{1,2,0:T(8,128)(2,1)}), bf16[4,256,384]{1,2,0:T(8,128)(2,1)S(1)}, u32[]{:S(2)}, u32[]{:S(2)}) %all-to-all-start.2) | async-done | bytes 786464 | tf_op jit(solution)/shard_map/all_to_all | solution.py:310
  234.2 4.6 %fusion = bf16[1,256,1536]{2,1,0:T(8,128)(2,1)} fusion(bf16[256,1536]{0,1:T(8,128)(2,1)S(1)} %bitcast.76, bf16[1536,1536]{1,0:T(8,128)(2,1)} %all-gather.5.cloned.1.call-done), kind=kOutput, calls=%fused_computation.1 | convolution fusion | flops 1208352768 | bytes 6291456 | tf_op jit(solution)/shard_map/dot_general | solution.py:311
  (29 shorter events, 1.9 us)
Async XLA Ops:
  7.2 4.5 %copy-start.4 = (bf16[24,384]{1,0:T(8,128)(2,1)S(1)}, bf16[24,384]{1,0:T(8,128)(2,1)}, u32[]{:S(2)}) copy-start(bf16[24,384]{1,0:T(8,128)(2,1)} %param.14) | copy-start | bytes 55300
  7.2 4.5 %copy-start.6 = (bf16[24,192]{1,0:T(8,128)(2,1)S(1)}, bf16[24,192]{1,0:T(8,128)(2,1)}, u32[]{:S(2)}) copy-start(bf16[24,192]{1,0:T(8,128)(2,1)} %param.15) | copy-start | bytes 27652
  7.2 4.5 %copy-start.7 = (bf16[24,192]{1,0:T(8,128)(2,1)S(1)}, bf16[24,192]{1,0:T(8,128)(2,1)}, u32[]{:S(2)}) copy-start(bf16[24,192]{1,0:T(8,128)(2,1)} %param.16) | copy-start | bytes 27652
  7.2 4.5 %copy-start.5 = (bf16[24,384]{1,0:T(8,128)(2,1)S(1)}, bf16[24,384]{1,0:T(8,128)(2,1)}, u32[]{:S(2)}) copy-start(bf16[24,384]{1,0:T(8,128)(2,1)} %param.17) | copy-start | bytes 55300
  7.2 124.4 %all-gather.3.cloned.1.call-start = ((), (), s32[]{:S(2)}) async-start(), calls=%async_computation.5 | async-start | bytes 3932160 | tf_op jit(solution)/shard_map/all_gather | solution.py:270
  11.6 222.6 %all-gather.5.cloned.1.call-start = ((), (), s32[]{:S(2)}) async-start(), calls=%async_computation.6 | async-start | bytes 5898240 | tf_op jit(solution)/shard_map/all_gather | solution.py:279
  74.9 22.8 %all-to-all-start = ((bf16[512,4,192]{0,2,1:T(8,128)(2,1)}), bf16[512,4,192]{0,2,1:T(8,128)(2,1)}, u32[]{:S(2)}, u32[]{:S(2)}) async-start(bf16[512,4,192]{0,2,1:T(8,128)(2,1)} %bitcast.67), calls=%async_computation | async-start | bytes 1572864 | tf_op jit(solution)/shard_map/all_to_all | solution.py:292
  97.7 26.2 %all-to-all-start.1 = ((bf16[512,4,192]{0,2,1:T(8,128)(2,1)}), bf16[512,4,192]{0,2,1:T(8,128)(2,1)}, u32[]{:S(2)}, u32[]{:S(2)}) async-start(bf16[512,4,192]{0,2,1:T(8,128)(2,1)} %bitcast.66), calls=%async_computation.1 | async-start | bytes 1572864 | tf_op jit(solution)/shard_map/all_to_all | solution.py:293
  140.3 3.4 %copy-start.2 = (f32[1024,48]{0,1:T(8,128)S(1)}, f32[1024,48]{0,1:T(8,128)}, u32[]{:S(2)}) copy-start(f32[1024,48]{0,1:T(8,128)} %get-tuple-element.18) | copy-start | bytes 589828
  140.3 3.4 %copy-start.3 = (f32[1024,48]{0,1:T(8,128)S(1)}, f32[1024,48]{0,1:T(8,128)}, u32[]{:S(2)}) copy-start(f32[1024,48]{0,1:T(8,128)} %get-tuple-element.19) | copy-start | bytes 589828
  149.2 0.8 copy-start
  149.2 1.0 copy-start.1
  157.1 14.4 %all-to-all-start.3 = ((bf16[4,256,192]{1,2,0:T(8,128)(2,1)}), bf16[4,256,192]{1,2,0:T(8,128)(2,1)}, u32[]{:S(2)}, u32[]{:S(2)}) async-start(bf16[4,256,192]{1,2,0:T(8,128)(2,1)} %copy.72), calls=%async_computation.3 | async-start | bytes 786432 | tf_op jit(solution)/shard_map/all_to_all | solution.py:289
  171.5 44.8 %all-to-all-start.4 = ((bf16[4,256,192]{1,2,0:T(8,128)(2,1)}), bf16[4,256,192]{1,2,0:T(8,128)(2,1)S(1)}, u32[]{:S(2)}, u32[]{:S(2)}) async-start(bf16[4,256,192]{1,2,0:T(8,128)(2,1)} %bitcast.57), calls=%async_computation.4 | async-start | bytes 786432 | tf_op jit(solution)/shard_map/all_to_all | solution.py:290
  216.3 17.9 %all-to-all-start.2 = ((bf16[4,256,384]{1,2,0:T(8,128)(2,1)}), bf16[4,256,384]{1,2,0:T(8,128)(2,1)S(1)}, u32[]{:S(2)}, u32[]{:S(2)}) async-start(bf16[4,256,384]{1,2,0:T(8,128)(2,1)} %copy.70), calls=%async_computation.2 | async-start | bytes 1572864 | tf_op jit(solution)/shard_map/all_to_all | solution.py:310
Sparse Core Ops, SparseCore 0:
  11.7 36.3 all-gather.2
  72.7 54.7 all-gather.4

commit v6 on v5

--- a/solution.py
+++ b/solution.py
@@ -51,8 +51,8 @@
     )
 
 
-def plane_ring_kernel(planes, runs, src_ref, out_ref, s1_send, s1_recv, r_send, r_recv,
-                      l_send, l_recv, local_sem):
+def plane_ring_kernel(planes, runs, src_ref, kc_ref, vc_ref, out_ref, kc_out, vc_out, s1_send,
+                      s1_recv, r_send, r_recv, l_send, l_recv, local_sem, kv_send, kv_recv, kv_local):
     me = lax.axis_index("req")
     kv = lax.axis_index("kv")
     y_me = lax.rem(me, Y_RUN)
@@ -81,10 +81,33 @@
     lax.fori_loop(1, planes, greet, 0)
     pl.semaphore_signal(barrier, inc=1, device_id=(ring_peer(z_right), kv), device_id_type=MESH)
     pl.semaphore_signal(barrier, inc=1, device_id=(ring_peer(z_left), kv), device_id_type=MESH)
-    pl.semaphore_wait(barrier, planes + 1)
+    kv_count = lax.axis_size("kv")
+
+    def greet_kv(step, carry):
+        peer = lax.rem(kv + step, kv_count)
+        pl.semaphore_signal(barrier, inc=1, device_id=(me, peer), device_id_type=MESH)
+        return carry
+
+    lax.fori_loop(1, kv_count, greet_kv, 0)
+    pl.semaphore_wait(barrier, planes + 1 + kv_count - 1)
 
     local = pltpu.make_async_copy(src_ref, out_ref.at[z_me, q_me], local_sem)
     local.start()
+    caches = ((kc_ref, kc_out), (vc_ref, vc_out))
+    local_cache = []
+    for which, (cache_src, cache_dst) in enumerate(caches):
+        c = pltpu.make_async_copy(cache_src.at[kv], cache_dst.at[kv], kv_local.at[which])
+        c.start()
+        local_cache.append(c)
+
+    def send_kv(step, carry):
+        peer = lax.rem(kv + step, kv_count)
+        for which, (cache_src, cache_dst) in enumerate(caches):
+            remote(cache_src.at[peer], cache_dst.at[kv], kv_send.at[which, step - 1],
+                   kv_recv.at[which, step - 1], (me, peer)).start()
+        return carry
+
+    lax.fori_loop(1, kv_count, send_kv, 0)
 
     def send(step, carry):
         q = lax.rem(q_me + step, planes)
@@ -139,18 +162,38 @@
     for c in sent:
         c.wait_send()
 
-
-def gather_req(piece):
+    def finish_kv(step, carry):
+        peer = lax.rem(kv + step, kv_count)
+        source = lax.rem(kv + kv_count - step, kv_count)
+        for which, (cache_src, cache_dst) in enumerate(caches):
+            remote(cache_src.at[peer], cache_dst.at[kv], kv_send.at[which, step - 1],
+                   kv_recv.at[which, step - 1], (me, peer)).wait_send()
+            remote(cache_src.at[kv], cache_dst.at[source], kv_send.at[which, step - 1],
+                   kv_recv.at[which, step - 1], (me, source)).wait_recv()
+        return carry
+
+    lax.fori_loop(1, kv_count, finish_kv, 0)
+    for c in local_cache:
+        c.wait()
+
+
+def gather_req(piece, keys_send, values_send):
     count = lax.axis_size("req")
+    kv_count = lax.axis_size("kv")
     runs = min(Z_RUN, count // Y_RUN)
     planes = count // runs
     rows, width = piece.shape
     hops = max(runs - 1, 1)
-    gathered = pl.pallas_call(
+    anywhere = pl.BlockSpec(memory_space=pl.ANY)
+    gathered, keys_old, values_old = pl.pallas_call(
         functools.partial(plane_ring_kernel, planes, runs),
-        out_shape=jax.ShapeDtypeStruct((runs, planes, rows, width), piece.dtype),
-        in_specs=[pl.BlockSpec(memory_space=pl.ANY)],
-        out_specs=pl.BlockSpec(memory_space=pl.ANY),
+        out_shape=(
+            jax.ShapeDtypeStruct((runs, planes, rows, width), piece.dtype),
+            jax.ShapeDtypeStruct(keys_send.shape, keys_send.dtype),
+            jax.ShapeDtypeStruct(values_send.shape, values_send.dtype),
+        ),
+        in_specs=[anywhere, anywhere, anywhere],
+        out_specs=(anywhere, anywhere, anywhere),
         scratch_shapes=[
             pltpu.SemaphoreType.DMA((planes - 1,)),
             pltpu.SemaphoreType.DMA((planes - 1,)),
@@ -159,14 +202,17 @@
             pltpu.SemaphoreType.DMA((hops,)),
             pltpu.SemaphoreType.DMA((hops,)),
             pltpu.SemaphoreType.DMA,
+            pltpu.SemaphoreType.DMA((2, kv_count - 1)),
+            pltpu.SemaphoreType.DMA((2, kv_count - 1)),
+            pltpu.SemaphoreType.DMA((2,)),
         ],
         compiler_params=pltpu.CompilerParams(collective_id=0, has_side_effects=True),
-    )(piece)
+    )(piece, keys_send, values_send)
     x_count = planes // Y_RUN
     ordered = jnp.transpose(
         gathered.reshape(runs, x_count, Y_RUN, rows, width), (1, 0, 2, 3, 4)
     )
-    return ordered.reshape(count * rows, width)
+    return ordered.reshape(count * rows, width), keys_old, values_old
 
 
 BLOCK_Q = 512
@@ -175,7 +221,7 @@
 
 def flash_kernel(tokens, scale, len_ref, q_ref, kc_ref, vc_ref, kn_ref, vn_ref, o_ref):
     block_q = q_ref.shape[1]
-    block_k = BLOCK_K
+    block_k = kc_ref.shape[2]
     width = q_ref.shape[2]
     i = pl.program_id(1)
     length = len_ref[0]
@@ -201,8 +247,8 @@
 
     def cache_step(block, carry):
         start = pl.multiple_of(block * block_k, block_k)
-        keys = kc_ref[0, pl.ds(start, block_k), :]
-        values = vc_ref[0, pl.ds(start, block_k), :]
+        keys = kc_ref[block, 0]
+        values = vc_ref[block, 0]
         visible = start + key_offset < length
         return step(keys, values, visible, carry)
 
@@ -227,10 +273,11 @@
 
 def flash_attention(lengths, queries, keys_old, values_old, keys_new, values_new, tokens, scale):
     heads, rows, width = queries.shape
-    slots = keys_old.shape[1]
+    blocks, _, block_k, _ = keys_old.shape
+    slots = blocks * block_k
     block_q = min(BLOCK_Q, tokens)
     grid = (heads, rows // block_q)
-    whole_cache = pl.BlockSpec((1, slots, width), lambda c, i, n: (c, 0, 0))
+    whole_cache = pl.BlockSpec((blocks, 1, block_k, width), lambda c, i, n: (0, c, 0, 0))
     whole_new = pl.BlockSpec((1, tokens, width), lambda c, i, n: (c, 0, 0))
     return pl.pallas_call(
         functools.partial(flash_kernel, tokens, scale),
@@ -270,7 +317,14 @@
     normed_all = lax.all_gather(normed, "kv", axis=0, tiled=True)
 
     pieces = jnp.concatenate([w_query, w_key, w_value, w_out], axis=1)
-    cols = gather_req(pieces)
+    def to_peers(cache):
+        return jnp.transpose(
+            cache.reshape(slots, kv_count, kv_heads_here, HD), (1, 2, 0, 3)
+        )
+
+    cols, keys_old, values_old = gather_req(
+        pieces, to_peers(key_cache[0]), to_peers(value_cache[0])
+    )
     wq = cols[:, :q_cols]
     wk = cols[:, q_cols:q_cols + k_cols]
     wv = cols[:, q_cols + k_cols:q_cols + k_cols + v_cols]
@@ -289,9 +343,6 @@
     new_keys = lax.all_to_all(keys_new, "kv", split_axis=0, concat_axis=1, tiled=True)
     new_values = lax.all_to_all(values_new, "kv", split_axis=0, concat_axis=1, tiled=True)
 
-    keys_old = lax.all_to_all(key_cache[0], "kv", split_axis=1, concat_axis=0, tiled=True)
-    values_old = lax.all_to_all(value_cache[0], "kv", split_axis=1, concat_axis=0, tiled=True)
-    cache_slots = keys_old.shape[0]
 
     def by_head(values):
         count = values.shape[0]
@@ -301,7 +352,7 @@
         queries.reshape(appended, kv_heads_here, groups, HD), (1, 2, 0, 3)
     ).reshape(kv_heads_here, groups * appended, HD)
     contexts = flash_attention(
-        lengths, query_heads, by_head(keys_old), by_head(values_old),
+        lengths, query_heads, keys_old, values_old,
         by_head(keys_new), by_head(values_new), appended, scale,
     )
     context = jnp.transpose(

time: 247 us -> 238 us (0.964)
  the two profiles are of different devices: /device:TPU:78 before, /device:TPU:2 now
where the time goes in v6:
time: 238 us; the launch traced here: 237 us
  Pallas kernels  135 us (57%)
  local copies, waits for them, and re-layouts  35.7 us (15%)
  matrix products  15.1 us (6%)
  between operations  14.9 us (6%)
  starting transfers between devices  13.7 us (6%)
  other arithmetic  12.7 us (5%)
  waiting for transfers between devices  10.4 us (4%)
    pallas_call x1, Pallas kernels, gather_req(): pl.pallas_call(functools.partial(plane_ring_kernel, planes, runs), out_sh...  97.1 us
    pallas_call x1, Pallas kernels, flash_attention(): pl.pallas_call(functools.partial(flash_kernel, tokens, scale), out_shape=...  37.7 us
    all_to_all x1, waiting for transfers between devices, body(): lax.all_to_all(context, 'kv', split_axis=0, concat_axis=1, tiled=True)  10.3 us
    unnamed x26, local copies, waits for them, and re-layouts  9.12 us
    convert_element_type x3, local copies, waits for them, and re-layouts, body(): keys_new = rotate(proj_k, positions).astype(jnp.bfloat16)  5.82 us
    all_to_all x1, starting transfers between devices, body(): lax.all_to_all(context, 'kv', split_axis=0, concat_axis=1, tiled=True)  4.79 us
  transfers between devices with their start and end apart: 5, of which 1 were waited for; matrix products, arithmetic and copies ran while one was open for 22% of the time, Pallas kernels for 57%

profile of v6, /device:TPU:2, one launch (start us, length us, event | category | flops | bytes accessed | tf_op | source)
XLA Modules:
  0.0 237.3 jit_solution(7409277158135220635)
XLA Ops:
  7.2 0.0 all-gather.3.cloned.1.call-start
  7.2 0.8 convert_element_type.40
  8.0 1.4 fusion.1
  9.4 2.3 fusion.3
  11.7 0.0 all-gather.3.cloned.1.call-update
  11.8 0.0 all-gather.5.cloned.1.call-start
  11.8 0.3 copy.52
  12.1 1.3 copy.53
  13.4 0.3 copy.54
  13.7 1.4 copy.55
  15.1 0.7 concatenate.10.src_ref
  15.8 97.1 %shard_map.112 = (bf16[8,8,24,1152]{3,2,1,0:T(8,128)(2,1)}, bf16[4,2,512,96]{3,2,1,0:T(8,128)(2,1)}, bf16[4,2,512,96]{3,2,1,0:T(8,128)(2,1)}) custom-call(bf16[24,1152]{1,0:T(8,128)(2,1)} %concatenate.10.src_ref, bf16[4,2,512,96]{3,2,1,0:T(8,128)(2,1)} %bitcast.57, bf16[4,2,512,96]{3,2,1,0:T(8,128)(2,1)} %bitcast.58), custom_call_target="tpu_custom_call" | custom-call | tf_op jit(solution)/shard_map/pallas_call | solution.py:188
  112.9 2.3 copy.56
  115.2 1.2 slice.39
  116.4 0.0 all-gather.5.cloned.1.call-update
  117.1 1.5 multiply_cosine_fusion
  118.6 2.0 copy.59
  120.6 2.0 copy.61
  122.6 3.1 %fusion.7 = f32[1024,192]{0,1:T(8,128)S(1)} fusion(bf16[1024,1536]{1,0:T(8,128)(2,1)} %all-gather.3.cloned.1.call-done, bf16[1536,1152]{1,0:T(8,128)(2,1)S(1)} %bitcast.54), kind=kOutput, calls=%fused_computation.14 | convolution fusion | flops 603979776 | bytes 4718592 | tf_op jit(solution)/shard_map/dot_general | solution.py:337
  125.6 0.9 fusion.9
  126.6 2.4 copy.70
  128.9 2.4 %copy.71 = f32[1024,2,48]{2,0,1:T(8,128)} copy(f32[1024,2,48]{0,2,1:T(8,128)} %get-tuple-element.22) | data formatting | bytes 786432
  131.3 3.4 %fusion.4 = f32[1024,384]{0,1:T(8,128)S(1)} fusion(bf16[1024,1536]{1,0:T(8,128)(2,1)} %all-gather.3.cloned.1.call-done, bf16[1536,1152]{1,0:T(8,128)(2,1)S(1)} %bitcast.55), kind=kOutput, calls=%fused_computation.8 | convolution fusion | flops 1207959552 | bytes 5898240 | tf_op jit(solution)/shard_map/dot_general | solution.py:336
  134.7 0.3 subtract_convert_fusion
  135.0 0.9 pad_maximum_fusion
  135.9 2.3 copy.57
  138.2 2.1 multiply_subtract_fusion
  140.3 0.8 copy-done
  141.1 0.1 copy-done.1
  141.2 1.1 maximum_convert_fusion
  142.4 2.0 copy.65
  144.3 2.0 convert_element_type.47
  146.4 1.8 copy.66
  148.2 4.1 %all-to-all-start.1 = ((bf16[4,256,192]{1,2,0:T(8,128)(2,1)}), bf16[4,256,192]{1,2,0:T(8,128)(2,1)}, u32[]{:S(2)}, u32[]{:S(2)}) async-start(bf16[4,256,192]{1,2,0:T(8,128)(2,1)} %copy.66), calls=%async_computation.1 | async-start | bytes 786432 | tf_op jit(solution)/shard_map/all_to_all | solution.py:343
  152.3 4.1 %convolution_convert_fusion.1 = bf16[1024,192]{0,1:T(8,128)(2,1)} fusion(bf16[1024,1536]{1,0:T(8,128)(2,1)} %all-gather.3.cloned.1.call-done, bf16[1536,1152]{1,0:T(8,128)(2,1)S(1)} %bitcast.56), kind=kOutput, calls=%fused_computation.7 | convolution fusion | flops 604176384 | bytes 4325376 | tf_op jit(solution)/shard_map/dot_general | solution.py:338
  156.4 2.0 copy.62
  158.4 1.8 copy.74
  160.2 2.3 fusion.15.kn_ref
  162.5 4.7 %all-to-all-start.2 = ((bf16[4,256,192]{1,2,0:T(8,128)(2,1)}), bf16[4,256,192]{1,2,0:T(8,128)(2,1)S(1)}, u32[]{:S(2)}, u32[]{:S(2)}) async-start(bf16[4,256,192]{1,2,0:T(8,128)(2,1)} %bitcast.51), calls=%async_computation.2 | async-start | bytes 786432 | tf_op jit(solution)/shard_map/all_to_all | solution.py:344
  167.2 37.7 %shard_map.113 = bf16[2,2048,96]{2,1,0:T(8,128)(2,1)} custom-call(s32[1]{0:T(128)} %copy.75.len_ref, bf16[2,2048,96]{2,1,0:T(8,128)(2,1)} %bitcast.68, bf16[4,2,512,96]{3,2,1,0:T(8,128)(2,1)} %get-tuple-element.7.kc_ref, bf16[4,2,512,96]{3,2,1,0:T(8,128)(2,1)} %get-tuple-element.8.vc_ref, bf16[2,1024,96]{2,1,0:T(8,128)(2,1)} %fusion.15.kn_ref, ...), custom_call_target="tpu_custom_call" | custom-call | flops 4831838208 | bytes 3932160 | tf_op jit(solution)/shard_map/pallas_call | solution.py:282
  204.9 1.5 copy.63
  206.3 0.6 all_to_all.36
  206.9 1.0 copy.64
  207.9 4.8 %all-to-all-start = ((bf16[4,256,384]{1,2,0:T(8,128)(2,1)}), bf16[4,256,384]{1,2,0:T(8,128)(2,1)S(1)}, u32[]{:S(2)}, u32[]{:S(2)}) async-start(bf16[4,256,384]{1,2,0:T(8,128)(2,1)} %copy.64), calls=%async_computation | async-start | bytes 1572864 | tf_op jit(solution)/shard_map/all_to_all | solution.py:361
  212.7 1.9 copy.68
  214.6 0.9 copy.69
  215.5 10.3 %all-to-all-done = bf16[4,256,384]{1,2,0:T(8,128)(2,1)S(1)} async-done(((bf16[4,256,384]{1,2,0:T(8,128)(2,1)}), bf16[4,256,384]{1,2,0:T(8,128)(2,1)S(1)}, u32[]{:S(2)}, u32[]{:S(2)}) %all-to-all-start) | async-done | bytes 786464 | tf_op jit(solution)/shard_map/all_to_all | solution.py:361
  225.9 4.6 %fusion = bf16[1,256,1536]{2,1,0:T(8,128)(2,1)} fusion(bf16[256,1536]{0,1:T(8,128)(2,1)S(1)} %bitcast.70, bf16[1536,1536]{1,0:T(8,128)(2,1)} %all-gather.5.cloned.1.call-done), kind=kOutput, calls=%fused_computation.1 | convolution fusion | flops 1208352768 | bytes 6291456 | tf_op jit(solution)/shard_map/dot_general | solution.py:362
  (25 shorter events, 0.1 us)
Async XLA Ops:
  7.2 4.7 %copy-start.4 = (bf16[1,512,768]{2,1,0:T(8,128)(2,1)S(1)}, bf16[1,512,768]{2,1,0:T(8,128)(2,1)}, u32[]{:S(2)}) copy-start(bf16[1,512,768]{2,1,0:T(8,128)(2,1)} %param.11) | copy-start | bytes 2359300
  7.2 115.4 %all-gather.3.cloned.1.call-start = ((), (), s32[]{:S(2)}) async-start(), calls=%async_computation.3 | async-start | bytes 3932160 | tf_op jit(solution)/shard_map/all_gather | solution.py:317
  8.0 5.5 %copy-start.5 = (bf16[1,512,768]{2,1,0:T(8,128)(2,1)S(1)}, bf16[1,512,768]{2,1,0:T(8,128)(2,1)}, u32[]{:S(2)}) copy-start(bf16[1,512,768]{2,1,0:T(8,128)(2,1)} %param.12) | copy-start | bytes 2359300
  11.7 3.4 %copy-start.6 = (bf16[24,384]{1,0:T(8,128)(2,1)S(1)}, bf16[24,384]{1,0:T(8,128)(2,1)}, u32[]{:S(2)}) copy-start(bf16[24,384]{1,0:T(8,128)(2,1)} %param.14) | copy-start | bytes 55300
  11.7 3.4 %copy-start.7 = (bf16[24,384]{1,0:T(8,128)(2,1)S(1)}, bf16[24,384]{1,0:T(8,128)(2,1)}, u32[]{:S(2)}) copy-start(bf16[24,384]{1,0:T(8,128)(2,1)} %param.17) | copy-start | bytes 55300
  11.7 3.4 %copy-start.8 = (bf16[24,192]{1,0:T(8,128)(2,1)S(1)}, bf16[24,192]{1,0:T(8,128)(2,1)}, u32[]{:S(2)}) copy-start(bf16[24,192]{1,0:T(8,128)(2,1)} %param.15) | copy-start | bytes 27652
  11.8 3.3 %copy-start.9 = (bf16[24,192]{1,0:T(8,128)(2,1)S(1)}, bf16[24,192]{1,0:T(8,128)(2,1)}, u32[]{:S(2)}) copy-start(bf16[24,192]{1,0:T(8,128)(2,1)} %param.16) | copy-start | bytes 27652
  11.8 214.1 %all-gather.5.cloned.1.call-start = ((), (), s32[]{:S(2)}) async-start(), calls=%async_computation.4 | async-start | bytes 5898240 | tf_op jit(solution)/shard_map/all_gather | solution.py:333
  131.3 3.4 %copy-start.2 = (f32[1024,48]{0,1:T(8,128)S(1)}, f32[1024,48]{0,1:T(8,128)}, u32[]{:S(2)}) copy-start(f32[1024,48]{0,1:T(8,128)} %get-tuple-element.24) | copy-start | bytes 589828
  131.3 3.4 %copy-start.3 = (f32[1024,48]{0,1:T(8,128)S(1)}, f32[1024,48]{0,1:T(8,128)}, u32[]{:S(2)}) copy-start(f32[1024,48]{0,1:T(8,128)} %get-tuple-element.25) | copy-start | bytes 589828
  140.3 0.8 copy-start
  140.3 1.0 copy-start.1
  148.2 14.3 %all-to-all-start.1 = ((bf16[4,256,192]{1,2,0:T(8,128)(2,1)}), bf16[4,256,192]{1,2,0:T(8,128)(2,1)}, u32[]{:S(2)}, u32[]{:S(2)}) async-start(bf16[4,256,192]{1,2,0:T(8,128)(2,1)} %copy.66), calls=%async_computation.1 | async-start | bytes 786432 | tf_op jit(solution)/shard_map/all_to_all | solution.py:343
  162.5 45.4 %all-to-all-start.2 = ((bf16[4,256,192]{1,2,0:T(8,128)(2,1)}), bf16[4,256,192]{1,2,0:T(8,128)(2,1)S(1)}, u32[]{:S(2)}, u32[]{:S(2)}) async-start(bf16[4,256,192]{1,2,0:T(8,128)(2,1)} %bitcast.51), calls=%async_computation.2 | async-start | bytes 786432 | tf_op jit(solution)/shard_map/all_to_all | solution.py:344
  207.9 17.9 %all-to-all-start = ((bf16[4,256,384]{1,2,0:T(8,128)(2,1)}), bf16[4,256,384]{1,2,0:T(8,128)(2,1)S(1)}, u32[]{:S(2)}, u32[]{:S(2)}) async-start(bf16[4,256,384]{1,2,0:T(8,128)(2,1)} %copy.64), calls=%async_computation | async-start | bytes 1572864 | tf_op jit(solution)/shard_map/all_to_all | solution.py:361
Sparse Core Ops, SparseCore 0:
  11.8 55.0 all-gather.2
  116.6 41.4 all-gather.4

commit v7 on v6

--- a/solution.py
+++ b/solution.py
@@ -100,14 +100,6 @@
         c.start()
         local_cache.append(c)
 
-    def send_kv(step, carry):
-        peer = lax.rem(kv + step, kv_count)
-        for which, (cache_src, cache_dst) in enumerate(caches):
-            remote(cache_src.at[peer], cache_dst.at[kv], kv_send.at[which, step - 1],
-                   kv_recv.at[which, step - 1], (me, peer)).start()
-        return carry
-
-    lax.fori_loop(1, kv_count, send_kv, 0)
 
     def send(step, carry):
         q = lax.rem(q_me + step, planes)
@@ -140,6 +132,14 @@
                    (ring_peer(z_left), kv))
         c.start()
         sent.append(c)
+    def send_kv(step, carry):
+        peer = lax.rem(kv + step, kv_count)
+        for which, (cache_src, cache_dst) in enumerate(caches):
+            remote(cache_src.at[peer], cache_dst.at[kv], kv_send.at[which, step - 1],
+                   kv_recv.at[which, step - 1], (me, peer)).start()
+        return carry
+
+    lax.fori_loop(1, kv_count, send_kv, 0)
     for k in range(1, max(right_hops, left_hops) + 1):
         if k <= right_hops:
             z_from = lax.rem(z_me + runs - k, runs)

time: 238 us -> 200 us (0.84)
  the two profiles are of different devices: /device:TPU:2 before, /device:TPU:1 now
where the time goes in v7:
time: 200 us; the launch traced here: 198 us
  Pallas kernels  95.1 us (48%)
  local copies, waits for them, and re-layouts  35.7 us (18%)
  matrix products  15.2 us (8%)
  starting transfers between devices  15 us (8%)
  between operations  14.9 us (7%)
  other arithmetic  12.7 us (6%)
  waiting for transfers between devices  9.5 us (5%)
    pallas_call x1, Pallas kernels, gather_req(): pl.pallas_call(functools.partial(plane_ring_kernel, planes, runs), out_sh...  57.4 us
    pallas_call x1, Pallas kernels, flash_attention(): pl.pallas_call(functools.partial(flash_kernel, tokens, scale), out_shape=...  37.7 us
    all_to_all x1, waiting for transfers between devices, body(): lax.all_to_all(context, 'kv', split_axis=0, concat_axis=1, tiled=True)  9.46 us
    unnamed x26, local copies, waits for them, and re-layouts  9.11 us
    convert_element_type x3, local copies, waits for them, and re-layouts, body(): keys_new = rotate(proj_k, positions).astype(jnp.bfloat16)  5.8 us
    all_to_all x1, starting transfers between devices, body(): lax.all_to_all(keys_new, 'kv', split_axis=0, concat_axis=1, tiled=True)  5.28 us
    all_to_all x1, starting transfers between devices, body(): lax.all_to_all(values_new, 'kv', split_axis=0, concat_axis=1, tiled=True)  4.8 us
    all_to_all x1, starting transfers between devices, body(): lax.all_to_all(context, 'kv', split_axis=0, concat_axis=1, tiled=True)  4.8 us
  transfers between devices with their start and end apart: 5, of which 1 were waited for; matrix products, arithmetic and copies ran while one was open for 27% of the time, Pallas kernels for 48%

profile of v7, /device:TPU:1, one launch (start us, length us, event | category | flops | bytes accessed | tf_op | source)
XLA Modules:
  0.0 198.0 jit_solution(17913473957276636964)
XLA Ops:
  7.2 0.0 all-gather.3.cloned.1.call-start
  7.2 0.8 convert_element_type.40
  8.0 1.4 fusion.1
  9.4 2.3 %fusion.3 = bf16[256,1536]{1,0:T(8,128)(2,1)} fusion(bf16[1,256,1536]{2,1,0:T(8,128)(2,1)} %param.9, f32[1536]{0:T(1024)S(1)} %convert_element_type.40, f32[256]{0:T(256)S(1)} %add_rsqrt_fusion), kind=kLoop, calls=%fused_computation.6 | loop fusion | flops 1572864 | bytes 1580032 | tf_op jit(solution)/shard_map/convert_element_type | solution.py:22
  11.7 0.0 all-gather.3.cloned.1.call-update
  11.8 0.0 all-gather.5.cloned.1.call-start
  11.8 0.3 copy.52
  12.1 1.3 copy.53
  13.4 0.3 copy.54
  13.7 1.4 copy.55
  15.1 0.7 concatenate.10.src_ref
  15.8 57.4 %shard_map.112 = (bf16[8,8,24,1152]{3,2,1,0:T(8,128)(2,1)}, bf16[4,2,512,96]{3,2,1,0:T(8,128)(2,1)}, bf16[4,2,512,96]{3,2,1,0:T(8,128)(2,1)}) custom-call(bf16[24,1152]{1,0:T(8,128)(2,1)} %concatenate.10.src_ref, bf16[4,2,512,96]{3,2,1,0:T(8,128)(2,1)} %bitcast.57, bf16[4,2,512,96]{3,2,1,0:T(8,128)(2,1)} %bitcast.58), custom_call_target="tpu_custom_call" | custom-call | tf_op jit(solution)/shard_map/pallas_call | solution.py:188
  73.2 2.3 %copy.56 = bf16[8,4,2,24,1152]{4,3,2,0,1:T(8,128)(2,1)S(1)} copy(bf16[8,4,2,24,1152]{4,3,2,1,0:T(8,128)(2,1)} %bitcast.59) | data formatting | bytes 7077888 | tf_op jit(solution)/shard_map/reshape | solution.py:213
  75.5 1.2 slice.39
  76.7 0.0 all-gather.5.cloned.1.call-update
  77.4 1.5 multiply_cosine_fusion
  78.9 2.0 copy.59
  80.9 2.0 copy.61
  82.9 3.1 %fusion.7 = f32[1024,192]{0,1:T(8,128)S(1)} fusion(bf16[1024,1536]{1,0:T(8,128)(2,1)} %all-gather.3.cloned.1.call-done, bf16[1536,1152]{1,0:T(8,128)(2,1)S(1)} %bitcast.54), kind=kOutput, calls=%fused_computation.14 | convolution fusion | flops 603979776 | bytes 4718592 | tf_op jit(solution)/shard_map/dot_general | solution.py:337
  85.9 0.9 fusion.9
  86.9 2.3 %copy.70 = f32[1024,2,48]{2,0,1:T(8,128)} copy(f32[1024,2,48]{0,2,1:T(8,128)} %get-tuple-element.23) | data formatting | bytes 786432
  89.2 2.4 %copy.71 = f32[1024,2,48]{2,0,1:T(8,128)} copy(f32[1024,2,48]{0,2,1:T(8,128)} %get-tuple-element.22) | data formatting | bytes 786432
  91.6 3.4 %fusion.4 = f32[1024,384]{0,1:T(8,128)S(1)} fusion(bf16[1024,1536]{1,0:T(8,128)(2,1)} %all-gather.3.cloned.1.call-done, bf16[1536,1152]{1,0:T(8,128)(2,1)S(1)} %bitcast.55), kind=kOutput, calls=%fused_computation.8 | convolution fusion | flops 1207959552 | bytes 5898240 | tf_op jit(solution)/shard_map/dot_general | solution.py:336
  95.1 0.3 subtract_convert_fusion
  95.3 0.9 pad_maximum_fusion
  96.3 2.2 %copy.57 = bf16[1024,4,96]{2,0,1:T(8,128)(2,1)} copy(bf16[1024,4,96]{0,2,1:T(8,128)(2,1)} %pad_maximum_fusion) | data formatting | bytes 1572864 | tf_op jit(solution)/shard_map/concatenate | solution.py:36
  98.5 2.1 %multiply_subtract_fusion = (bf16[1024,2,48]{2,0,1:T(8,128)(2,1)S(1)}, bf16[1024,2,48]{2,0,1:T(8,128)(2,1)S(1)}) fusion(f32[1024,2,48]{2,0,1:T(8,128)} %copy.71, f32[1024,2,48]{2,0,1:T(8,128)} %copy.70, f32[1024,48]{1,0:T(8,128)} %copy.61, f32[1024,48]{1,0:T(8,128)} %copy.59), kind=kLoop, calls=%fused_computation.12 | loop fusion | flops 786432 | bytes 1572864 | tf_op jit(solution)/shard_map/sub | solution.py:37
  100.6 0.8 copy-done
  101.4 0.1 copy-done.1
  101.6 1.1 maximum_convert_fusion
  102.7 2.0 %copy.65 = bf16[1024,2,96]{0,2,1:T(8,128)(2,1)} copy(bf16[1024,2,96]{2,0,1:T(8,128)(2,1)} %maximum_convert_fusion) | data formatting | bytes 786432 | tf_op jit(solution)/shard_map/convert_element_type | solution.py:340
  104.7 2.0 %convert_element_type.47 = bf16[4,256,192]{1,0,2:T(4,128)(2,1)} reshape(bf16[1024,2,96]{0,2,1:T(8,128)(2,1)} %copy.65) | data formatting | bytes 786432 | tf_op jit(solution)/shard_map/convert_element_type | solution.py:340
  106.7 1.8 copy.66
  108.5 5.3 %all-to-all-start.1 = ((bf16[4,256,192]{1,2,0:T(8,128)(2,1)}), bf16[4,256,192]{1,2,0:T(8,128)(2,1)}, u32[]{:S(2)}, u32[]{:S(2)}) async-start(bf16[4,256,192]{1,2,0:T(8,128)(2,1)} %copy.66), calls=%async_computation.1 | async-start | bytes 786432 | tf_op jit(solution)/shard_map/all_to_all | solution.py:343
  113.8 4.0 %convolution_convert_fusion.1 = bf16[1024,192]{0,1:T(8,128)(2,1)} fusion(bf16[1024,1536]{1,0:T(8,128)(2,1)} %all-gather.3.cloned.1.call-done, bf16[1536,1152]{1,0:T(8,128)(2,1)S(1)} %bitcast.56), kind=kOutput, calls=%fused_computation.7 | convolution fusion | flops 604176384 | bytes 4325376 | tf_op jit(solution)/shard_map/dot_general | solution.py:338
  117.8 2.0 %copy.62 = bf16[1024,2,96]{2,0,1:T(8,128)(2,1)} copy(bf16[1024,2,96]{0,2,1:T(8,128)(2,1)} %bitcast.65) | data formatting | bytes 786432 | tf_op jit(solution)/shard_map/reshape | solution.py:349
  119.8 1.8 copy.74
  121.6 2.3 %fusion.15.kn_ref = bf16[2,1024,96]{2,1,0:T(8,128)(2,1)} fusion(bf16[1024,2,48]{2,0,1:T(8,128)(2,1)} %copy-done.1, bf16[1024,2,48]{2,0,1:T(8,128)(2,1)} %copy-done), kind=kLoop, calls=%fused_computation.26 | loop fusion | flops 786432 | bytes 786432 | tf_op jit(solution)/shard_map/transpose | solution.py:349
  123.9 4.8 %all-to-all-start.2 = ((bf16[4,256,192]{1,2,0:T(8,128)(2,1)}), bf16[4,256,192]{1,2,0:T(8,128)(2,1)S(1)}, u32[]{:S(2)}, u32[]{:S(2)}) async-start(bf16[4,256,192]{1,2,0:T(8,128)(2,1)} %bitcast.51), calls=%async_computation.2 | async-start | bytes 786432 | tf_op jit(solution)/shard_map/all_to_all | solution.py:344
  128.7 37.7 %shard_map.113 = bf16[2,2048,96]{2,1,0:T(8,128)(2,1)} custom-call(s32[1]{0:T(128)} %copy.75.len_ref, bf16[2,2048,96]{2,1,0:T(8,128)(2,1)} %bitcast.68, bf16[4,2,512,96]{3,2,1,0:T(8,128)(2,1)} %get-tuple-element.7.kc_ref, bf16[4,2,512,96]{3,2,1,0:T(8,128)(2,1)} %get-tuple-element.8.vc_ref, bf16[2,1024,96]{2,1,0:T(8,128)(2,1)} %fusion.15.kn_ref, ...), custom_call_target="tpu_custom_call" | custom-call | flops 4831838208 | bytes 3932160 | tf_op jit(solution)/shard_map/pallas_call | solution.py:282
  166.4 1.5 copy.63
  167.8 0.6 all_to_all.36
  168.4 1.0 copy.64
  169.4 4.8 %all-to-all-start = ((bf16[4,256,384]{1,2,0:T(8,128)(2,1)}), bf16[4,256,384]{1,2,0:T(8,128)(2,1)S(1)}, u32[]{:S(2)}, u32[]{:S(2)}) async-start(bf16[4,256,384]{1,2,0:T(8,128)(2,1)} %copy.64), calls=%async_computation | async-start | bytes 1572864 | tf_op jit(solution)/shard_map/all_to_all | solution.py:361
  174.2 1.9 copy.68
  176.1 0.9 copy.69
  177.0 9.5 %all-to-all-done = bf16[4,256,384]{1,2,0:T(8,128)(2,1)S(1)} async-done(((bf16[4,256,384]{1,2,0:T(8,128)(2,1)}), bf16[4,256,384]{1,2,0:T(8,128)(2,1)S(1)}, u32[]{:S(2)}, u32[]{:S(2)}) %all-to-all-start) | async-done | bytes 786464 | tf_op jit(solution)/shard_map/all_to_all | solution.py:361
  186.5 4.6 %fusion = bf16[1,256,1536]{2,1,0:T(8,128)(2,1)} fusion(bf16[256,1536]{0,1:T(8,128)(2,1)S(1)} %bitcast.70, bf16[1536,1536]{1,0:T(8,128)(2,1)} %all-gather.5.cloned.1.call-done), kind=kOutput, calls=%fused_computation.1 | convolution fusion | flops 1208352768 | bytes 6291456 | tf_op jit(solution)/shard_map/dot_general | solution.py:362
  (25 shorter events, 0.1 us)
Async XLA Ops:
  7.2 4.7 %copy-start.4 = (bf16[1,512,768]{2,1,0:T(8,128)(2,1)S(1)}, bf16[1,512,768]{2,1,0:T(8,128)(2,1)}, u32[]{:S(2)}) copy-start(bf16[1,512,768]{2,1,0:T(8,128)(2,1)} %param.11) | copy-start | bytes 2359300
  7.2 75.7 %all-gather.3.cloned.1.call-start = ((), (), s32[]{:S(2)}) async-start(), calls=%async_computation.3 | async-start | bytes 3932160 | tf_op jit(solution)/shard_map/all_gather | solution.py:317
  8.0 5.5 %copy-start.5 = (bf16[1,512,768]{2,1,0:T(8,128)(2,1)S(1)}, bf16[1,512,768]{2,1,0:T(8,128)(2,1)}, u32[]{:S(2)}) copy-start(bf16[1,512,768]{2,1,0:T(8,128)(2,1)} %param.12) | copy-start | bytes 2359300
  11.7 3.4 %copy-start.6 = (bf16[24,384]{1,0:T(8,128)(2,1)S(1)}, bf16[24,384]{1,0:T(8,128)(2,1)}, u32[]{:S(2)}) copy-start(bf16[24,384]{1,0:T(8,128)(2,1)} %param.14) | copy-start | bytes 55300
  11.7 3.4 %copy-start.7 = (bf16[24,384]{1,0:T(8,128)(2,1)S(1)}, bf16[24,384]{1,0:T(8,128)(2,1)}, u32[]{:S(2)}) copy-start(bf16[24,384]{1,0:T(8,128)(2,1)} %param.17) | copy-start | bytes 55300
  11.7 3.4 %copy-start.8 = (bf16[24,192]{1,0:T(8,128)(2,1)S(1)}, bf16[24,192]{1,0:T(8,128)(2,1)}, u32[]{:S(2)}) copy-start(bf16[24,192]{1,0:T(8,128)(2,1)} %param.15) | copy-start | bytes 27652
  11.8 3.3 %copy-start.9 = (bf16[24,192]{1,0:T(8,128)(2,1)S(1)}, bf16[24,192]{1,0:T(8,128)(2,1)}, u32[]{:S(2)}) copy-start(bf16[24,192]{1,0:T(8,128)(2,1)} %param.16) | copy-start | bytes 27652
  11.8 174.7 %all-gather.5.cloned.1.call-start = ((), (), s32[]{:S(2)}) async-start(), calls=%async_computation.4 | async-start | bytes 5898240 | tf_op jit(solution)/shard_map/all_gather | solution.py:333
  91.6 3.4 %copy-start.2 = (f32[1024,48]{0,1:T(8,128)S(1)}, f32[1024,48]{0,1:T(8,128)}, u32[]{:S(2)}) copy-start(f32[1024,48]{0,1:T(8,128)} %get-tuple-element.24) | copy-start | bytes 589828
  91.6 3.4 %copy-start.3 = (f32[1024,48]{0,1:T(8,128)S(1)}, f32[1024,48]{0,1:T(8,128)}, u32[]{:S(2)}) copy-start(f32[1024,48]{0,1:T(8,128)} %get-tuple-element.25) | copy-start | bytes 589828
  100.6 0.8 copy-start
  100.6 1.0 copy-start.1
  108.5 15.4 %all-to-all-start.1 = ((bf16[4,256,192]{1,2,0:T(8,128)(2,1)}), bf16[4,256,192]{1,2,0:T(8,128)(2,1)}, u32[]{:S(2)}, u32[]{:S(2)}) async-start(bf16[4,256,192]{1,2,0:T(8,128)(2,1)} %copy.66), calls=%async_computation.1 | async-start | bytes 786432 | tf_op jit(solution)/shard_map/all_to_all | solution.py:343
  123.9 45.5 %all-to-all-start.2 = ((bf16[4,256,192]{1,2,0:T(8,128)(2,1)}), bf16[4,256,192]{1,2,0:T(8,128)(2,1)S(1)}, u32[]{:S(2)}, u32[]{:S(2)}) async-start(bf16[4,256,192]{1,2,0:T(8,128)(2,1)} %bitcast.51), calls=%async_computation.2 | async-start | bytes 786432 | tf_op jit(solution)/shard_map/all_to_all | solution.py:344
  169.4 17.1 %all-to-all-start = ((bf16[4,256,384]{1,2,0:T(8,128)(2,1)}), bf16[4,256,384]{1,2,0:T(8,128)(2,1)S(1)}, u32[]{:S(2)}, u32[]{:S(2)}) async-start(bf16[4,256,384]{1,2,0:T(8,128)(2,1)} %copy.64), calls=%async_computation | async-start | bytes 1572864 | tf_op jit(solution)/shard_map/all_to_all | solution.py:361
Sparse Core Ops, SparseCore 0:
  11.8 56.1 all-gather.2
  76.9 44.6 all-gather.4

commit v8 on v7

--- a/solution.py
+++ b/solution.py
@@ -333,33 +333,54 @@
     wo_full = lax.all_gather(wo, "kv", axis=1, tiled=True)
 
     positions = (length + jnp.arange(appended, dtype=jnp.int32)).astype(jnp.float32)
-    proj_q = jnp.dot(normed_all, wq, preferred_element_type=jnp.float32)
-    proj_k = jnp.dot(normed_all, wk, preferred_element_type=jnp.float32)
-    proj_v = jnp.dot(normed_all, wv, preferred_element_type=jnp.float32)
-    queries = rotate(proj_q, positions).astype(jnp.bfloat16)
-    keys_new = rotate(proj_k, positions).astype(jnp.bfloat16)
+    half = HD // 2
+    frequency = rope_base ** (-(jnp.arange(half, dtype=jnp.float32) * 2.0 / HD))
+    angle = positions[:, None] * frequency[None, :]
+    cosine = jnp.cos(angle)
+    sine = jnp.sin(angle)
+
+    def turn(values):
+        first = values[..., :half]
+        second = values[..., half:]
+        return jnp.concatenate(
+            [first * cosine - second * sine, second * cosine + first * sine], axis=-1
+        )
+
+    width = normed_all.shape[1]
+    proj_q = jnp.einsum(
+        "td,dcgh->cgth", normed_all, wq.reshape(width, kv_heads_here, groups, HD),
+        preferred_element_type=jnp.float32,
+    )
+    proj_k = jnp.einsum(
+        "td,dch->cth", normed_all, wk.reshape(width, kv_heads_here, HD),
+        preferred_element_type=jnp.float32,
+    )
+    proj_v = jnp.einsum(
+        "td,dch->cth", normed_all, wv.reshape(width, kv_heads_here, HD),
+        preferred_element_type=jnp.float32,
+    )
+    query_heads = turn(proj_q).astype(jnp.bfloat16).reshape(kv_heads_here, groups * appended, HD)
+    keys_new = turn(proj_k).astype(jnp.bfloat16)
     values_new = proj_v.astype(jnp.bfloat16)
 
-    new_keys = lax.all_to_all(keys_new, "kv", split_axis=0, concat_axis=1, tiled=True)
-    new_values = lax.all_to_all(values_new, "kv", split_axis=0, concat_axis=1, tiled=True)
-
-
-    def by_head(values):
-        count = values.shape[0]
-        return jnp.transpose(values.reshape(count, kv_heads_here, HD), (1, 0, 2))
-
-    query_heads = jnp.transpose(
-        queries.reshape(appended, kv_heads_here, groups, HD), (1, 2, 0, 3)
-    ).reshape(kv_heads_here, groups * appended, HD)
+    def to_tokens(values):
+        parts = values.reshape(kv_heads_here, kv_count, rows_here, HD)
+        got = lax.all_to_all(parts, "kv", split_axis=1, concat_axis=1, tiled=True)
+        return jnp.transpose(got, (2, 1, 0, 3)).reshape(rows_here, kv_count * kv_heads_here * HD)
+
+    new_keys = to_tokens(keys_new)
+    new_values = to_tokens(values_new)
+
     contexts = flash_attention(
-        lengths, query_heads, keys_old, values_old,
-        by_head(keys_new), by_head(values_new), appended, scale,
-    )
-    context = jnp.transpose(
-        contexts.reshape(kv_heads_here, groups, appended, HD), (2, 0, 1, 3)
-    ).reshape(appended, heads_here * HD)
-    context_rows = lax.all_to_all(context, "kv", split_axis=0, concat_axis=1, tiled=True)
-    attended = jnp.dot(context_rows, wo_full, preferred_element_type=jnp.float32).astype(jnp.bfloat16)
+        lengths, query_heads, keys_old, values_old, keys_new, values_new, appended, scale,
+    )
+    parts = contexts.reshape(kv_heads_here, groups, kv_count, rows_here, HD)
+    got = lax.all_to_all(parts, "kv", split_axis=2, concat_axis=2, tiled=True)
+    attended = jnp.einsum(
+        "cgsth,scghn->tn", got,
+        wo_full.reshape(kv_count, kv_heads_here, groups, HD, wo_full.shape[1]),
+        preferred_element_type=jnp.float32,
+    ).astype(jnp.bfloat16)
     return (attended[None], new_keys[None], new_values[None])
 
 

time: 200 us -> 182 us (0.910)
  the two profiles are of different devices: /device:TPU:1 before, /device:TPU:6 now
where the time goes in v8:
time: 182 us
  Pallas kernels  96.7 us (53%)
  local copies, waits for them, and re-layouts  21.3 us (12%)
  between operations  14.9 us (8%)
  waiting for transfers between devices  14 us (8%)
  matrix products  13.1 us (7%)
  starting transfers between devices  11.7 us (6%)
  other arithmetic  10 us (5%)
    pallas_call x1, Pallas kernels, gather_req(): pl.pallas_call(functools.partial(plane_ring_kernel, planes, runs), out_sh...  59 us
    pallas_call x1, Pallas kernels, flash_attention(): pl.pallas_call(functools.partial(flash_kernel, tokens, scale), out_shape=...  37.7 us
    all_to_all x1, waiting for transfers between devices, body(): got = lax.all_to_all(parts, 'kv', split_axis=2, concat_axis=2, tiled=True)  11.3 us
    all_to_all x2, starting transfers between devices, to_tokens(): got = lax.all_to_all(parts, 'kv', split_axis=1, concat_axis=1, tiled=True)  7.1 us
    dot_general x1, matrix products, body(): jnp.einsum('cgsth,scghn->tn', got, wo_full.reshape(kv_count, kv_heads_her...  4.62 us
    all_to_all x1, starting transfers between devices, body(): got = lax.all_to_all(parts, 'kv', split_axis=2, concat_axis=2, tiled=True)  4.55 us
    dot_general x1, matrix products, body(): jnp.einsum('td,dcgh->cgth', normed_all, wq.reshape(width, kv_heads_here,...  3.8 us
  transfers between devices with their start and end apart: 5, of which 2 were waited for; matrix products, arithmetic and copies ran while one was open for 19% of the time, Pallas kernels for 53%

profile of v8, /device:TPU:6, one launch (start us, length us, event | category | flops | bytes accessed | tf_op | source)
XLA Modules:
  0.0 181.8 jit_solution(11706488543891486283)
XLA Ops:
  7.2 0.0 all-gather.3.cloned.1.call-start
  7.2 0.8 convert_element_type.32
  8.0 1.4 fusion.17
  9.3 2.3 %fusion.19 = bf16[256,1536]{1,0:T(8,128)(2,1)} fusion(bf16[1,256,1536]{2,1,0:T(8,128)(2,1)} %param.9, f32[1536]{0:T(1024)S(1)} %convert_element_type.32, f32[256]{0:T(256)S(1)} %add_rsqrt_fusion), kind=kLoop, calls=%fused_computation.15 | loop fusion | flops 1572864 | bytes 1580032 | tf_op jit(solution)/shard_map/convert_element_type | solution.py:22
  11.6 0.0 all-gather.3.cloned.1.call-update
  11.6 0.0 all-gather.5.cloned.1.call-start
  11.7 0.3 copy.64
  12.0 1.3 copy.65
  13.3 0.0 copy-start.11
  13.3 0.3 copy.66
  13.6 1.4 copy.67
  15.0 0.7 concatenate.24.src_ref
  15.7 59.0 %shard_map.112 = (bf16[8,8,24,1152]{3,2,1,0:T(8,128)(2,1)}, bf16[4,2,512,96]{3,2,1,0:T(8,128)(2,1)}, bf16[4,2,512,96]{3,2,1,0:T(8,128)(2,1)}) custom-call(bf16[24,1152]{1,0:T(8,128)(2,1)} %concatenate.24.src_ref, bf16[4,2,512,96]{3,2,1,0:T(8,128)(2,1)} %bitcast.69, bf16[4,2,512,96]{3,2,1,0:T(8,128)(2,1)} %bitcast.71), custom_call_target="tpu_custom_call" | custom-call | tf_op jit(solution)/shard_map/pallas_call | solution.py:188
  74.7 2.3 %copy.68 = bf16[8,4,2,24,1152]{4,3,2,0,1:T(8,128)(2,1)S(1)} copy(bf16[8,4,2,24,1152]{4,3,2,1,0:T(8,128)(2,1)} %bitcast.73) | data formatting | bytes 7077888 | tf_op jit(solution)/shard_map/reshape | solution.py:213
  77.0 1.7 fusion.31
  78.7 0.0 all-gather.5.cloned.1.call-update
  78.7 1.5 fusion.30
  80.2 2.3 %copy.72 = bf16[1536,192]{0,1:T(8,128)(2,1)} copy(bf16[1536,192]{1,0:T(8,128)(2,1)} %get-tuple-element.19) | data formatting | bytes 1179648 | tf_op jit(solution)/shard_map/slice | solution.py:329
  83.2 0.8 multiply_cosine_fusion
  84.0 0.2 copy.74
  84.2 1.0 copy.75
  85.2 1.5 copy.69
  86.7 0.3 copy.76
  86.9 0.0 all-gather.3.cloned.1.call-done
  87.0 3.5 %fusion.23 = f32[2,1024,96]{2,1,0:T(8,128)S(1)} fusion(bf16[1536,2,96]{0,2,1:T(8,128)(2,1)} %bitcast.83, bf16[1024,1536]{1,0:T(8,128)(2,1)} %all-gather.3.cloned.1.call-done), kind=kOutput, calls=%fused_computation.17 | convolution fusion | flops 603979776 | bytes 4521984 | tf_op jit(solution)/shard_map/td,dch->cth/dot_general | solution.py:354
  90.5 0.5 subtract_convert_fusion
  91.0 0.2 copy.81
  91.2 0.2 copy.82
  91.4 0.8 pad_maximum_fusion.2
  92.2 3.5 %all-to-all-start.1 = ((bf16[2,4,256,96]{2,3,0,1:T(8,128)(2,1)}), bf16[2,4,256,96]{2,3,0,1:T(8,128)(2,1)S(1)}, u32[]{:S(2)}, u32[]{:S(2)}) async-start(bf16[2,4,256,96]{2,3,0,1:T(8,128)(2,1)} %pad_maximum_fusion.2), calls=%async_computation.1 | async-start | bytes 786432 | tf_op jit(solution)/shard_map/all_to_all | solution.py:368
  95.7 3.8 %fusion.20 = f32[2,2,1024,96]{2,3,1,0:T(8,128)S(1)} fusion(bf16[1536,2,2,96]{0,3,2,1:T(8,128)(2,1)} %bitcast.81, bf16[1024,1536]{1,0:T(8,128)(2,1)} %all-gather.3.cloned.1.call-done), kind=kOutput, calls=%fused_computation.16 | convolution fusion | flops 1207959552 | bytes 5898240 | tf_op jit(solution)/shard_map/td,dcgh->cgth/dot_general | solution.py:350
  99.5 1.0 subtract_convert_fusion.1
  100.5 1.2 fusion.26
  101.7 1.1 pad_maximum_fusion.1.kn_ref
  102.7 0.5 copy.70
  103.2 0.5 copy.71
  103.7 0.3 copy.77
  104.0 1.0 copy.83
  105.0 1.5 pad_maximum_fusion.q_ref
  106.5 2.6 %all-to-all-done.1 = bf16[2,4,256,96]{2,3,0,1:T(8,128)(2,1)S(1)} async-done(((bf16[2,4,256,96]{2,3,0,1:T(8,128)(2,1)}), bf16[2,4,256,96]{2,3,0,1:T(8,128)(2,1)S(1)}, u32[]{:S(2)}, u32[]{:S(2)}) %all-to-all-start.1) | async-done | bytes 393248 | tf_op jit(solution)/shard_map/all_to_all | solution.py:368
  109.1 3.6 %all-to-all-start.2 = ((bf16[2,4,256,96]{2,3,0,1:T(8,128)(2,1)}), bf16[2,4,256,96]{2,3,0,1:T(8,128)(2,1)S(1)}, u32[]{:S(2)}, u32[]{:S(2)}) async-start(bf16[2,4,256,96]{2,3,0,1:T(8,128)(2,1)} %copy.83), calls=%async_computation.2 | async-start | bytes 786432 | tf_op jit(solution)/shard_map/all_to_all | solution.py:368
  112.7 37.7 %shard_map.113 = bf16[2,2048,96]{2,1,0:T(8,128)(2,1)} custom-call(s32[1]{0:T(128)} %copy.99.len_ref, bf16[2,2048,96]{2,1,0:T(8,128)(2,1)} %pad_maximum_fusion.q_ref, bf16[4,2,512,96]{3,2,1,0:T(8,128)(2,1)} %get-tuple-element.7.kc_ref, bf16[4,2,512,96]{3,2,1,0:T(8,128)(2,1)} %get-tuple-element.8.vc_ref, bf16[2,1024,96]{2,1,0:T(8,128)(2,1)} %pad_maximum_fusion.1.kn_ref, ...), custom_call_target="tpu_custom_call" | custom-call | flops 4831838208 | bytes 3932160 | tf_op jit(solution)/shard_map/pallas_call | solution.py:282
  150.5 2.2 %copy.78 = bf16[2,2,4,256,96]{3,4,1,0,2:T(8,128)(2,1)} copy(bf16[2,2,4,256,96]{4,3,2,1,0:T(8,128)(2,1)} %bitcast.82) | data formatting | bytes 1572864 | tf_op jit(solution)/shard_map/reshape | solution.py:377
  152.7 4.6 %all-to-all-start = ((bf16[2,2,4,256,96]{3,4,1,0,2:T(8,128)(2,1)}), bf16[2,2,4,256,96]{3,4,1,0,2:T(8,128)(2,1)S(1)}, u32[]{:S(2)}, u32[]{:S(2)}) async-start(bf16[2,2,4,256,96]{3,4,1,0,2:T(8,128)(2,1)} %copy.78), calls=%async_computation | async-start | bytes 1572864 | tf_op jit(solution)/shard_map/all_to_all | solution.py:378
  157.2 0.9 copy.84
  158.1 0.9 copy.85
  159.1 11.3 %all-to-all-done = bf16[2,2,4,256,96]{3,4,1,0,2:T(8,128)(2,1)S(1)} async-done(((bf16[2,2,4,256,96]{3,4,1,0,2:T(8,128)(2,1)}), bf16[2,2,4,256,96]{3,4,1,0,2:T(8,128)(2,1)S(1)}, u32[]{:S(2)}, u32[]{:S(2)}) %all-to-all-start) | async-done | bytes 786464 | tf_op jit(solution)/shard_map/all_to_all | solution.py:378
  170.4 4.6 %fusion.14 = bf16[1,256,1536]{2,1,0:T(8,128)(2,1)} fusion(bf16[4,2,2,96,1536]{4,3,2,1,0:T(8,128)(2,1)} %bitcast.84, bf16[2,2,4,256,96]{3,4,1,0,2:T(8,128)(2,1)S(1)} %all-to-all-done), kind=kOutput, calls=%fused_computation.10 | convolution fusion | flops 1208352768 | bytes 6291456 | tf_op jit(solution)/shard_map/cgsth,scghn->tn/dot_general | solution.py:379
  (28 shorter events, 0.1 us)
Async XLA Ops:
  7.2 4.5 %copy-start.6 = (bf16[1,512,768]{2,1,0:T(8,128)(2,1)S(1)}, bf16[1,512,768]{2,1,0:T(8,128)(2,1)}, u32[]{:S(2)}) copy-start(bf16[1,512,768]{2,1,0:T(8,128)(2,1)} %param.11) | copy-start | bytes 2359300
  7.2 79.8 %all-gather.3.cloned.1.call-start = ((), (), s32[]{:S(2)}) async-start(), calls=%async_computation.3 | async-start | bytes 3932160 | tf_op jit(solution)/shard_map/all_gather | solution.py:317
  11.6 1.7 copy-start.7
  11.6 158.7 %all-gather.5.cloned.1.call-start = ((), (), s32[]{:S(2)}) async-start(), calls=%async_computation.4 | async-start | bytes 5898240 | tf_op jit(solution)/shard_map/all_gather | solution.py:333
  13.3 1.7 copy-start.8
  13.3 1.7 copy-start.9
  13.3 1.7 copy-start.10
  13.3 1.7 copy-start.11
  80.2 5.0 %copy-start = (bf16[1536,384]{1,0:T(8,128)(2,1)S(1)}, bf16[1536,384]{1,0:T(8,128)(2,1)}, u32[]{:S(2)}) copy-start(bf16[1536,384]{1,0:T(8,128)(2,1)} %get-tuple-element.20) | copy-start | bytes 3538948
  83.2 3.5 %copy-start.2 = (bf16[1536,192]{1,0:T(8,128)(2,1)S(1)}, bf16[1536,192]{1,0:T(8,128)(2,1)}, u32[]{:S(2)}) copy-start(bf16[1536,192]{1,0:T(8,128)(2,1)} %get-tuple-element.18) | copy-start | bytes 1769476
  87.0 3.6 %copy-start.4 = (f32[1024,48]{1,0:T(8,128)S(1)}, f32[1024,48]{1,0:T(8,128)}, u32[]{:S(2)}) copy-start(f32[1024,48]{1,0:T(8,128)} %copy.75) | copy-start | bytes 589828
  92.2 16.9 %all-to-all-start.1 = ((bf16[2,4,256,96]{2,3,0,1:T(8,128)(2,1)}), bf16[2,4,256,96]{2,3,0,1:T(8,128)(2,1)S(1)}, u32[]{:S(2)}, u32[]{:S(2)}) async-start(bf16[2,4,256,96]{2,3,0,1:T(8,128)(2,1)} %pad_maximum_fusion.2), calls=%async_computation.1 | async-start | bytes 786432 | tf_op jit(solution)/shard_map/all_to_all | solution.py:368
  95.6 4.8 %copy-start.1 = (bf16[1024,1536]{1,0:T(8,128)(2,1)S(1)}, bf16[1024,1536]{1,0:T(8,128)(2,1)}, u32[]{:S(2)}) copy-start(bf16[1024,1536]{1,0:T(8,128)(2,1)} %all-gather.3.cloned.1.call-done) | copy-start | bytes 9437188
  101.6 1.6 copy-start.5
  104.0 5.1 %copy-start.3 = (bf16[2,96,1024]{1,2,0:T(8,128)(2,1)}, bf16[2,96,1024]{1,2,0:T(8,128)(2,1)S(1)}, u32[]{:S(2)}) copy-start(bf16[2,96,1024]{1,2,0:T(8,128)(2,1)S(1)} %copy.77) | copy-start | bytes 1179652
  109.1 43.6 %all-to-all-start.2 = ((bf16[2,4,256,96]{2,3,0,1:T(8,128)(2,1)}), bf16[2,4,256,96]{2,3,0,1:T(8,128)(2,1)S(1)}, u32[]{:S(2)}, u32[]{:S(2)}) async-start(bf16[2,4,256,96]{2,3,0,1:T(8,128)(2,1)} %copy.83), calls=%async_computation.2 | async-start | bytes 786432 | tf_op jit(solution)/shard_map/all_to_all | solution.py:368
  152.7 17.7 %all-to-all-start = ((bf16[2,2,4,256,96]{3,4,1,0,2:T(8,128)(2,1)}), bf16[2,2,4,256,96]{3,4,1,0,2:T(8,128)(2,1)S(1)}, u32[]{:S(2)}, u32[]{:S(2)}) async-start(bf16[2,2,4,256,96]{3,4,1,0,2:T(8,128)(2,1)} %copy.78), calls=%async_computation | async-start | bytes 1572864 | tf_op jit(solution)/shard_map/all_to_all | solution.py:378
Sparse Core Ops, SparseCore 0:
  11.8 53.8 all-gather.2
  78.8 49.2 all-gather.4

commit v9 on v8

--- a/solution.py
+++ b/solution.py
@@ -121,17 +121,24 @@
     lax.fori_loop(1, planes, finish, 0)
     local.wait()
 
+    split = 2 if planes % 2 == 0 else 1
+    share = planes // split
+
+    def ring_copy(z_block, h, send, recv, k, z_to):
+        part = out_ref.at[z_block, pl.ds(h * share, share)]
+        return remote(part, part, send.at[k, h], recv.at[k, h], (ring_peer(z_to), kv))
+
     sent = []
-    if right_hops > 0:
-        c = remote(out_ref.at[z_me], out_ref.at[z_me], r_send.at[0], r_recv.at[0],
-                   (ring_peer(z_right), kv))
-        c.start()
-        sent.append(c)
-    if left_hops > 0:
-        c = remote(out_ref.at[z_me], out_ref.at[z_me], l_send.at[0], l_recv.at[0],
-                   (ring_peer(z_left), kv))
-        c.start()
-        sent.append(c)
+    for h in range(split):
+        if right_hops > 0:
+            c = ring_copy(z_me, h, r_send, r_recv, 0, z_right)
+            c.start()
+            sent.append(c)
+        if left_hops > 0:
+            c = ring_copy(z_me, h, l_send, l_recv, 0, z_left)
+            c.start()
+            sent.append(c)
+
     def send_kv(step, carry):
         peer = lax.rem(kv + step, kv_count)
         for which, (cache_src, cache_dst) in enumerate(caches):
@@ -141,24 +148,21 @@
 
     lax.fori_loop(1, kv_count, send_kv, 0)
     for k in range(1, max(right_hops, left_hops) + 1):
-        if k <= right_hops:
-            z_from = lax.rem(z_me + runs - k, runs)
-            remote(out_ref.at[z_from], out_ref.at[z_from], r_send.at[k - 1], r_recv.at[k - 1],
-                   (ring_peer(z_right), kv)).wait_recv()
-            if k < right_hops:
-                c = remote(out_ref.at[z_from], out_ref.at[z_from], r_send.at[k], r_recv.at[k],
-                           (ring_peer(z_right), kv))
-                c.start()
-                sent.append(c)
-        if k <= left_hops:
-            z_from = lax.rem(z_me + k, runs)
-            remote(out_ref.at[z_from], out_ref.at[z_from], l_send.at[k - 1], l_recv.at[k - 1],
-                   (ring_peer(z_left), kv)).wait_recv()
-            if k < left_hops:
-                c = remote(out_ref.at[z_from], out_ref.at[z_from], l_send.at[k], l_recv.at[k],
-                           (ring_peer(z_left), kv))
-                c.start()
-                sent.append(c)
+        for h in range(split):
+            if k <= right_hops:
+                z_from = lax.rem(z_me + runs - k, runs)
+                ring_copy(z_from, h, r_send, r_recv, k - 1, z_right).wait_recv()
+                if k < right_hops:
+                    c = ring_copy(z_from, h, r_send, r_recv, k, z_right)
+                    c.start()
+                    sent.append(c)
+            if k <= left_hops:
+                z_from = lax.rem(z_me + k, runs)
+                ring_copy(z_from, h, l_send, l_recv, k - 1, z_left).wait_recv()
+                if k < left_hops:
+                    c = ring_copy(z_from, h, l_send, l_recv, k, z_left)
+                    c.start()
+                    sent.append(c)
     for c in sent:
         c.wait_send()
 
@@ -197,10 +201,10 @@
         scratch_shapes=[
             pltpu.SemaphoreType.DMA((planes - 1,)),
             pltpu.SemaphoreType.DMA((planes - 1,)),
-            pltpu.SemaphoreType.DMA((hops,)),
-            pltpu.SemaphoreType.DMA((hops,)),
-            pltpu.SemaphoreType.DMA((hops,)),
-            pltpu.SemaphoreType.DMA((hops,)),
+            pltpu.SemaphoreType.DMA((hops, 2)),
+            pltpu.SemaphoreType.DMA((hops, 2)),
+            pltpu.SemaphoreType.DMA((hops, 2)),
+            pltpu.SemaphoreType.DMA((hops, 2)),
             pltpu.SemaphoreType.DMA,
             pltpu.SemaphoreType.DMA((2, kv_count - 1)),
             pltpu.SemaphoreType.DMA((2, kv_count - 1)),

time: 182 us -> 180 us (0.989)
  the two profiles are of different devices: /device:TPU:6 before, /device:TPU:1 now
where the time goes in v9:
time: 180 us
  Pallas kernels  95.3 us (53%)
  local copies, waits for them, and re-layouts  21.3 us (12%)
  between operations  14.9 us (8%)
  matrix products  13 us (7%)
  starting transfers between devices  12.9 us (7%)
  waiting for transfers between devices  12.3 us (7%)
  other arithmetic  10 us (6%)
    pallas_call x1, Pallas kernels, gather_req(): pl.pallas_call(functools.partial(plane_ring_kernel, planes, runs), out_sh...  57.6 us
    pallas_call x1, Pallas kernels, flash_attention(): pl.pallas_call(functools.partial(flash_kernel, tokens, scale), out_shape=...  37.7 us
    all_to_all x1, waiting for transfers between devices, body(): got = lax.all_to_all(parts, 'kv', split_axis=2, concat_axis=2, tiled=True)  10.5 us
    all_to_all x2, starting transfers between devices, to_tokens(): got = lax.all_to_all(parts, 'kv', split_axis=1, concat_axis=1, tiled=True)  8.02 us
    all_to_all x1, starting transfers between devices, body(): got = lax.all_to_all(parts, 'kv', split_axis=2, concat_axis=2, tiled=True)  4.8 us
    dot_general x1, matrix products, body(): jnp.einsum('cgsth,scghn->tn', got, wo_full.reshape(kv_count, kv_heads_her...  4.62 us
    dot_general x1, matrix products, body(): jnp.einsum('td,dcgh->cgth', normed_all, wq.reshape(width, kv_heads_here,...  3.8 us
  transfers between devices with their start and end apart: 5, of which 2 were waited for; matrix products, arithmetic and copies ran while one was open for 20% of the time, Pallas kernels for 53%

profile of v9, /device:TPU:1, one launch (start us, length us, event | category | flops | bytes accessed | tf_op | source)
XLA Modules:
  0.0 179.8 jit_solution(14962504240031890720)
XLA Ops:
  7.2 0.0 all-gather.3.cloned.1.call-start
  7.2 0.8 convert_element_type.32
  8.0 1.4 fusion.17
  9.3 2.3 %fusion.19 = bf16[256,1536]{1,0:T(8,128)(2,1)} fusion(bf16[1,256,1536]{2,1,0:T(8,128)(2,1)} %param.9, f32[1536]{0:T(1024)S(1)} %convert_element_type.32, f32[256]{0:T(256)S(1)} %add_rsqrt_fusion), kind=kLoop, calls=%fused_computation.15 | loop fusion | flops 1572864 | bytes 1580032 | tf_op jit(solution)/shard_map/convert_element_type | solution.py:22
  11.6 0.0 all-gather.3.cloned.1.call-update
  11.6 0.0 all-gather.5.cloned.1.call-start
  11.7 0.3 copy.64
  12.0 1.3 copy.65
  13.3 0.0 copy-start.11
  13.3 0.3 copy.66
  13.6 1.4 copy.67
  15.0 0.7 concatenate.24.src_ref
  15.7 57.6 %shard_map.112 = (bf16[8,8,24,1152]{3,2,1,0:T(8,128)(2,1)}, bf16[4,2,512,96]{3,2,1,0:T(8,128)(2,1)}, bf16[4,2,512,96]{3,2,1,0:T(8,128)(2,1)}) custom-call(bf16[24,1152]{1,0:T(8,128)(2,1)} %concatenate.24.src_ref, bf16[4,2,512,96]{3,2,1,0:T(8,128)(2,1)} %bitcast.69, bf16[4,2,512,96]{3,2,1,0:T(8,128)(2,1)} %bitcast.71), custom_call_target="tpu_custom_call" | custom-call | tf_op jit(solution)/shard_map/pallas_call | solution.py:192
  73.4 2.3 %copy.68 = bf16[8,4,2,24,1152]{4,3,2,0,1:T(8,128)(2,1)S(1)} copy(bf16[8,4,2,24,1152]{4,3,2,1,0:T(8,128)(2,1)} %bitcast.73) | data formatting | bytes 7077888 | tf_op jit(solution)/shard_map/reshape | solution.py:217
  75.6 1.7 fusion.31
  77.4 0.0 all-gather.5.cloned.1.call-update
  77.4 1.5 fusion.30
  78.9 2.3 %copy.72 = bf16[1536,192]{0,1:T(8,128)(2,1)} copy(bf16[1536,192]{1,0:T(8,128)(2,1)} %get-tuple-element.19) | data formatting | bytes 1179648 | tf_op jit(solution)/shard_map/slice | solution.py:333
  81.9 0.8 multiply_cosine_fusion
  82.7 0.2 copy.74
  82.9 1.0 copy.75
  83.9 1.5 copy.69
  85.3 0.3 copy.76
  85.6 0.0 all-gather.3.cloned.1.call-done
  85.6 3.4 %fusion.23 = f32[2,1024,96]{2,1,0:T(8,128)S(1)} fusion(bf16[1536,2,96]{0,2,1:T(8,128)(2,1)} %bitcast.83, bf16[1024,1536]{1,0:T(8,128)(2,1)} %all-gather.3.cloned.1.call-done), kind=kOutput, calls=%fused_computation.17 | convolution fusion | flops 603979776 | bytes 4521984 | tf_op jit(solution)/shard_map/td,dch->cth/dot_general | solution.py:358
  89.0 0.5 subtract_convert_fusion
  89.5 0.2 copy.81
  89.7 0.2 copy.82
  89.9 0.8 pad_maximum_fusion.2
  90.7 3.8 %all-to-all-start.1 = ((bf16[2,4,256,96]{2,3,0,1:T(8,128)(2,1)}), bf16[2,4,256,96]{2,3,0,1:T(8,128)(2,1)S(1)}, u32[]{:S(2)}, u32[]{:S(2)}) async-start(bf16[2,4,256,96]{2,3,0,1:T(8,128)(2,1)} %pad_maximum_fusion.2), calls=%async_computation.1 | async-start | bytes 786432 | tf_op jit(solution)/shard_map/all_to_all | solution.py:372
  94.5 3.8 %fusion.20 = f32[2,2,1024,96]{2,3,1,0:T(8,128)S(1)} fusion(bf16[1536,2,2,96]{0,3,2,1:T(8,128)(2,1)} %bitcast.81, bf16[1024,1536]{1,0:T(8,128)(2,1)} %all-gather.3.cloned.1.call-done), kind=kOutput, calls=%fused_computation.16 | convolution fusion | flops 1207959552 | bytes 5898240 | tf_op jit(solution)/shard_map/td,dcgh->cgth/dot_general | solution.py:354
  98.3 1.0 subtract_convert_fusion.1
  99.3 1.2 fusion.26
  100.5 1.1 pad_maximum_fusion.1.kn_ref
  101.5 0.5 copy.70
  102.0 0.5 copy.71
  102.5 0.3 copy.77
  102.8 1.0 copy.83
  103.8 1.5 pad_maximum_fusion.q_ref
  105.3 1.8 %all-to-all-done.1 = bf16[2,4,256,96]{2,3,0,1:T(8,128)(2,1)S(1)} async-done(((bf16[2,4,256,96]{2,3,0,1:T(8,128)(2,1)}), bf16[2,4,256,96]{2,3,0,1:T(8,128)(2,1)S(1)}, u32[]{:S(2)}, u32[]{:S(2)}) %all-to-all-start.1) | async-done | bytes 393248 | tf_op jit(solution)/shard_map/all_to_all | solution.py:372
  107.1 4.2 %all-to-all-start.2 = ((bf16[2,4,256,96]{2,3,0,1:T(8,128)(2,1)}), bf16[2,4,256,96]{2,3,0,1:T(8,128)(2,1)S(1)}, u32[]{:S(2)}, u32[]{:S(2)}) async-start(bf16[2,4,256,96]{2,3,0,1:T(8,128)(2,1)} %copy.83), calls=%async_computation.2 | async-start | bytes 786432 | tf_op jit(solution)/shard_map/all_to_all | solution.py:372
  111.4 37.7 %shard_map.113 = bf16[2,2048,96]{2,1,0:T(8,128)(2,1)} custom-call(s32[1]{0:T(128)} %copy.99.len_ref, bf16[2,2048,96]{2,1,0:T(8,128)(2,1)} %pad_maximum_fusion.q_ref, bf16[4,2,512,96]{3,2,1,0:T(8,128)(2,1)} %get-tuple-element.7.kc_ref, bf16[4,2,512,96]{3,2,1,0:T(8,128)(2,1)} %get-tuple-element.8.vc_ref, bf16[2,1024,96]{2,1,0:T(8,128)(2,1)} %pad_maximum_fusion.1.kn_ref, ...), custom_call_target="tpu_custom_call" | custom-call | flops 4831838208 | bytes 3932160 | tf_op jit(solution)/shard_map/pallas_call | solution.py:286
  149.1 2.2 %copy.78 = bf16[2,2,4,256,96]{3,4,1,0,2:T(8,128)(2,1)} copy(bf16[2,2,4,256,96]{4,3,2,1,0:T(8,128)(2,1)} %bitcast.82) | data formatting | bytes 1572864 | tf_op jit(solution)/shard_map/reshape | solution.py:381
  151.3 4.8 %all-to-all-start = ((bf16[2,2,4,256,96]{3,4,1,0,2:T(8,128)(2,1)}), bf16[2,2,4,256,96]{3,4,1,0,2:T(8,128)(2,1)S(1)}, u32[]{:S(2)}, u32[]{:S(2)}) async-start(bf16[2,2,4,256,96]{3,4,1,0,2:T(8,128)(2,1)} %copy.78), calls=%async_computation | async-start | bytes 1572864 | tf_op jit(solution)/shard_map/all_to_all | solution.py:382
  156.1 0.9 copy.84
  157.0 0.9 copy.85
  157.9 10.5 %all-to-all-done = bf16[2,2,4,256,96]{3,4,1,0,2:T(8,128)(2,1)S(1)} async-done(((bf16[2,2,4,256,96]{3,4,1,0,2:T(8,128)(2,1)}), bf16[2,2,4,256,96]{3,4,1,0,2:T(8,128)(2,1)S(1)}, u32[]{:S(2)}, u32[]{:S(2)}) %all-to-all-start) | async-done | bytes 786464 | tf_op jit(solution)/shard_map/all_to_all | solution.py:382
  168.4 4.6 %fusion.14 = bf16[1,256,1536]{2,1,0:T(8,128)(2,1)} fusion(bf16[4,2,2,96,1536]{4,3,2,1,0:T(8,128)(2,1)} %bitcast.84, bf16[2,2,4,256,96]{3,4,1,0,2:T(8,128)(2,1)S(1)} %all-to-all-done), kind=kOutput, calls=%fused_computation.10 | convolution fusion | flops 1208352768 | bytes 6291456 | tf_op jit(solution)/shard_map/cgsth,scghn->tn/dot_general | solution.py:383
  (28 shorter events, 0.1 us)
Async XLA Ops:
  7.2 4.5 %copy-start.6 = (bf16[1,512,768]{2,1,0:T(8,128)(2,1)S(1)}, bf16[1,512,768]{2,1,0:T(8,128)(2,1)}, u32[]{:S(2)}) copy-start(bf16[1,512,768]{2,1,0:T(8,128)(2,1)} %param.11) | copy-start | bytes 2359300
  7.2 78.4 %all-gather.3.cloned.1.call-start = ((), (), s32[]{:S(2)}) async-start(), calls=%async_computation.3 | async-start | bytes 3932160 | tf_op jit(solution)/shard_map/all_gather | solution.py:321
  11.6 1.7 copy-start.7
  11.6 156.7 %all-gather.5.cloned.1.call-start = ((), (), s32[]{:S(2)}) async-start(), calls=%async_computation.4 | async-start | bytes 5898240 | tf_op jit(solution)/shard_map/all_gather | solution.py:337
  13.3 1.7 copy-start.8
  13.3 1.7 copy-start.9
  13.3 1.7 copy-start.10
  13.3 1.7 copy-start.11
  78.9 5.0 %copy-start = (bf16[1536,384]{1,0:T(8,128)(2,1)S(1)}, bf16[1536,384]{1,0:T(8,128)(2,1)}, u32[]{:S(2)}) copy-start(bf16[1536,384]{1,0:T(8,128)(2,1)} %get-tuple-element.20) | copy-start | bytes 3538948
  81.9 3.5 %copy-start.2 = (bf16[1536,192]{1,0:T(8,128)(2,1)S(1)}, bf16[1536,192]{1,0:T(8,128)(2,1)}, u32[]{:S(2)}) copy-start(bf16[1536,192]{1,0:T(8,128)(2,1)} %get-tuple-element.18) | copy-start | bytes 1769476
  85.6 3.4 %copy-start.4 = (f32[1024,48]{1,0:T(8,128)S(1)}, f32[1024,48]{1,0:T(8,128)}, u32[]{:S(2)}) copy-start(f32[1024,48]{1,0:T(8,128)} %copy.75) | copy-start | bytes 589828
  90.7 16.4 %all-to-all-start.1 = ((bf16[2,4,256,96]{2,3,0,1:T(8,128)(2,1)}), bf16[2,4,256,96]{2,3,0,1:T(8,128)(2,1)S(1)}, u32[]{:S(2)}, u32[]{:S(2)}) async-start(bf16[2,4,256,96]{2,3,0,1:T(8,128)(2,1)} %pad_maximum_fusion.2), calls=%async_computation.1 | async-start | bytes 786432 | tf_op jit(solution)/shard_map/all_to_all | solution.py:372
  94.5 4.8 %copy-start.1 = (bf16[1024,1536]{1,0:T(8,128)(2,1)S(1)}, bf16[1024,1536]{1,0:T(8,128)(2,1)}, u32[]{:S(2)}) copy-start(bf16[1024,1536]{1,0:T(8,128)(2,1)} %all-gather.3.cloned.1.call-done) | copy-start | bytes 9437188
  100.4 1.6 copy-start.5
  102.8 4.3 %copy-start.3 = (bf16[2,96,1024]{1,2,0:T(8,128)(2,1)}, bf16[2,96,1024]{1,2,0:T(8,128)(2,1)S(1)}, u32[]{:S(2)}) copy-start(bf16[2,96,1024]{1,2,0:T(8,128)(2,1)S(1)} %copy.77) | copy-start | bytes 1179652
  107.1 44.1 %all-to-all-start.2 = ((bf16[2,4,256,96]{2,3,0,1:T(8,128)(2,1)}), bf16[2,4,256,96]{2,3,0,1:T(8,128)(2,1)S(1)}, u32[]{:S(2)}, u32[]{:S(2)}) async-start(bf16[2,4,256,96]{2,3,0,1:T(8,128)(2,1)} %copy.83), calls=%async_computation.2 | async-start | bytes 786432 | tf_op jit(solution)/shard_map/all_to_all | solution.py:372
  151.3 17.1 %all-to-all-start = ((bf16[2,2,4,256,96]{3,4,1,0,2:T(8,128)(2,1)}), bf16[2,2,4,256,96]{3,4,1,0,2:T(8,128)(2,1)S(1)}, u32[]{:S(2)}, u32[]{:S(2)}) async-start(bf16[2,2,4,256,96]{3,4,1,0,2:T(8,128)(2,1)} %copy.78), calls=%async_computation | async-start | bytes 1572864 | tf_op jit(solution)/shard_map/all_to_all | solution.py:382
Sparse Core Ops, SparseCore 0:
  11.8 56.0 all-gather.2
  77.5 50.8 all-gather.4

commit v10 on v9

--- a/solution.py
+++ b/solution.py
@@ -227,7 +227,7 @@
     block_q = q_ref.shape[1]
     block_k = kc_ref.shape[2]
     width = q_ref.shape[2]
-    i = pl.program_id(1)
+    i = pl.program_id(0)
     length = len_ref[0]
     first = lax.rem(i * block_q, tokens)
     q = q_ref[0]
@@ -239,24 +239,34 @@
         score = lax.dot_general(
             q, keys, (((1,), (1,)), ((), ())), preferred_element_type=jnp.float32
         ) * scale
-        score = jnp.where(visible, score, masked_score)
+        if visible is not None:
+            score = jnp.where(visible, score, masked_score)
         new_peak = jnp.maximum(peak, jnp.max(score, axis=1, keepdims=True))
         alpha = jnp.exp(peak - new_peak)
-        weights = jnp.where(visible, jnp.exp(score - new_peak), 0.0)
+        weights = jnp.exp(score - new_peak)
+        if visible is not None:
+            weights = jnp.where(visible, weights, 0.0)
         total = alpha * total + jnp.sum(weights, axis=1, keepdims=True)
         acc = alpha * acc + jnp.dot(
             weights.astype(jnp.bfloat16), values, preferred_element_type=jnp.float32
         )
         return new_peak, total, acc
 
-    def cache_step(block, carry):
+    def cache_full(block, carry):
+        return step(kc_ref[block, 0], vc_ref[block, 0], None, carry)
+
+    def cache_part(block, carry):
+        start = block * block_k
+        visible = start + key_offset < length
+        return step(kc_ref[block, 0], vc_ref[block, 0], visible, carry)
+
+    def new_full(block, carry):
         start = pl.multiple_of(block * block_k, block_k)
-        keys = kc_ref[block, 0]
-        values = vc_ref[block, 0]
-        visible = start + key_offset < length
-        return step(keys, values, visible, carry)
-
-    def new_step(block, carry):
+        keys = kn_ref[0, pl.ds(start, block_k), :]
+        values = vn_ref[0, pl.ds(start, block_k), :]
+        return step(keys, values, None, carry)
+
+    def new_part(block, carry):
         start = pl.multiple_of(block * block_k, block_k)
         keys = kn_ref[0, pl.ds(start, block_k), :]
         values = vn_ref[0, pl.ds(start, block_k), :]
@@ -268,37 +278,42 @@
         jnp.zeros((block_q, 1), jnp.float32),
         jnp.zeros((block_q, width), jnp.float32),
     )
+    full_blocks = length // block_k
     live_blocks = (length + block_k - 1) // block_k
-    carry = lax.fori_loop(0, live_blocks, cache_step, carry)
+    carry = lax.fori_loop(0, full_blocks, cache_full, carry)
+    carry = lax.fori_loop(full_blocks, live_blocks, cache_part, carry)
+    clear_blocks = first // block_k
     new_blocks = (first + block_q - 1) // block_k + 1
-    peak, total, acc = lax.fori_loop(0, new_blocks, new_step, carry)
-    o_ref[0] = (acc / total).astype(o_ref.dtype)
-
-
-def flash_attention(lengths, queries, keys_old, values_old, keys_new, values_new, tokens, scale):
+    carry = lax.fori_loop(0, clear_blocks, new_full, carry)
+    peak, total, acc = lax.fori_loop(clear_blocks, new_blocks, new_part, carry)
+    o_ref[...] = (acc / total).astype(o_ref.dtype)
+
+
+def flash_attention(lengths, queries, keys_old, values_old, keys_new, values_new, tokens, scale,
+                    head):
     heads, rows, width = queries.shape
     blocks, _, block_k, _ = keys_old.shape
     slots = blocks * block_k
     block_q = min(BLOCK_Q, tokens)
-    grid = (heads, rows // block_q)
-    whole_cache = pl.BlockSpec((blocks, 1, block_k, width), lambda c, i, n: (0, c, 0, 0))
-    whole_new = pl.BlockSpec((1, tokens, width), lambda c, i, n: (c, 0, 0))
+    grid = (rows // block_q,)
+    whole_cache = pl.BlockSpec((blocks, 1, block_k, width), lambda i, n: (0, head, 0, 0))
+    whole_new = pl.BlockSpec((1, tokens, width), lambda i, n: (head, 0, 0))
     return pl.pallas_call(
         functools.partial(flash_kernel, tokens, scale),
-        out_shape=jax.ShapeDtypeStruct((heads, rows, width), jnp.bfloat16),
+        out_shape=jax.ShapeDtypeStruct((rows, width), jnp.bfloat16),
         grid_spec=pltpu.PrefetchScalarGridSpec(
             num_scalar_prefetch=1,
             grid=grid,
             in_specs=[
-                pl.BlockSpec((1, block_q, width), lambda c, i, n: (c, i, 0)),
+                pl.BlockSpec((1, block_q, width), lambda i, n: (head, i, 0)),
                 whole_cache, whole_cache, whole_new, whole_new,
             ],
-            out_specs=pl.BlockSpec((1, block_q, width), lambda c, i, n: (c, i, 0)),
+            out_specs=pl.BlockSpec((block_q, width), lambda i, n: (i, 0)),
         ),
         cost_estimate=pl.CostEstimate(
-            flops=4 * heads * rows * (slots + tokens) * width,
-            transcendentals=heads * rows * (slots + tokens),
-            bytes_accessed=2 * width * heads * (2 * rows + 2 * slots + 2 * tokens),
+            flops=4 * rows * (slots + tokens) * width,
+            transcendentals=rows * (slots + tokens),
+            bytes_accessed=2 * width * (2 * rows + 2 * slots + 2 * tokens),
         ),
     )(lengths, queries, keys_old, values_old, keys_new, values_new)
 
@@ -375,16 +390,20 @@
     new_keys = to_tokens(keys_new)
     new_values = to_tokens(values_new)
 
-    contexts = flash_attention(
-        lengths, query_heads, keys_old, values_old, keys_new, values_new, appended, scale,
-    )
-    parts = contexts.reshape(kv_heads_here, groups, kv_count, rows_here, HD)
-    got = lax.all_to_all(parts, "kv", split_axis=2, concat_axis=2, tiled=True)
-    attended = jnp.einsum(
-        "cgsth,scghn->tn", got,
-        wo_full.reshape(kv_count, kv_heads_here, groups, HD, wo_full.shape[1]),
-        preferred_element_type=jnp.float32,
-    ).astype(jnp.bfloat16)
+    wo_heads = wo_full.reshape(kv_count, kv_heads_here, groups, HD, wo_full.shape[1])
+    attended = None
+    for head in range(kv_heads_here):
+        context = flash_attention(
+            lengths, query_heads, keys_old, values_old, keys_new, values_new, appended, scale,
+            head,
+        )
+        parts = context.reshape(groups, kv_count, rows_here, HD)
+        got = lax.all_to_all(parts, "kv", split_axis=1, concat_axis=1, tiled=True)
+        partial = jnp.einsum(
+            "gsth,sghn->tn", got, wo_heads[:, head], preferred_element_type=jnp.float32
+        )
+        attended = partial if attended is None else attended + partial
+    attended = attended.astype(jnp.bfloat16)
     return (attended[None], new_keys[None], new_values[None])
 
 

time: 180 us -> 192 us (1.067)
  the two profiles are of different devices: /device:TPU:1 before, /device:TPU:12 now
where the time goes in v10:
time: 192 us
  Pallas kernels  97.4 us (51%)
  local copies, waits for them, and re-layouts  27.4 us (14%)
  starting transfers between devices  15.2 us (8%)
  matrix products  15 us (8%)
  between operations  15 us (8%)
  waiting for transfers between devices  11.7 us (6%)
  other arithmetic  10 us (5%)
    pallas_call x1, Pallas kernels, gather_req(): pl.pallas_call(functools.partial(plane_ring_kernel, planes, runs), out_sh...  55.9 us
    pallas_call x2, Pallas kernels, flash_attention(): pl.pallas_call(functools.partial(flash_kernel, tokens, scale), out_shape=...  41.4 us
    all_to_all x2, waiting for transfers between devices, body(): got = lax.all_to_all(parts, 'kv', split_axis=1, concat_axis=1, tiled=True)  9.02 us
    all_to_all x2, starting transfers between devices, body(): got = lax.all_to_all(parts, 'kv', split_axis=1, concat_axis=1, tiled=True)  8.01 us
    all_to_all x2, starting transfers between devices, to_tokens(): got = lax.all_to_all(parts, 'kv', split_axis=1, concat_axis=1, tiled=True)  7.1 us
    dot_general x2, matrix products, body(): jnp.einsum('gsth,sghn->tn', got, wo_heads[:, head], preferred_element_typ...  6.74 us
    slice x1, local copies, waits for them, and re-layouts, body(): wo_heads[:, head]  4.25 us
    reshape x2, local copies, waits for them, and re-layouts, body(): parts = context.reshape(groups, kv_count, rows_here, HD)  3.97 us
  transfers between devices with their start and end apart: 6, of which 3 were waited for; matrix products, arithmetic and copies ran while one was open for 23% of the time, Pallas kernels for 51%

profile of v10, /device:TPU:12, one launch (start us, length us, event | category | flops | bytes accessed | tf_op | source)
XLA Modules:
  0.0 191.7 jit_solution(5774225084607169)
XLA Ops:
  7.2 0.8 convert_element_type.32
  8.0 1.4 fusion.9
  9.3 2.3 %fusion.11 = bf16[256,1536]{1,0:T(8,128)(2,1)} fusion(bf16[1,256,1536]{2,1,0:T(8,128)(2,1)} %param.9, f32[1536]{0:T(1024)S(1)} %convert_element_type.32, f32[256]{0:T(256)S(1)} %add_rsqrt_fusion), kind=kLoop, calls=%fused_computation.17 | loop fusion | flops 1572864 | bytes 1580032 | tf_op jit(solution)/shard_map/convert_element_type | solution.py:22
  11.7 0.3 copy.70
  12.0 1.3 copy.71
  13.4 0.3 copy.72
  13.6 1.4 copy.73
  15.1 0.7 concatenate.24.src_ref
  15.8 55.9 %shard_map.112 = (bf16[8,8,24,1152]{3,2,1,0:T(8,128)(2,1)}, bf16[4,2,512,96]{3,2,1,0:T(8,128)(2,1)}, bf16[4,2,512,96]{3,2,1,0:T(8,128)(2,1)}) custom-call(bf16[24,1152]{1,0:T(8,128)(2,1)} %concatenate.24.src_ref, bf16[4,2,512,96]{3,2,1,0:T(8,128)(2,1)} %bitcast.83, bf16[4,2,512,96]{3,2,1,0:T(8,128)(2,1)} %bitcast.85), custom_call_target="tpu_custom_call" | custom-call | tf_op jit(solution)/shard_map/pallas_call | solution.py:192
  71.7 2.3 %copy.74 = bf16[8,4,2,24,1152]{4,3,2,0,1:T(8,128)(2,1)S(1)} copy(bf16[8,4,2,24,1152]{4,3,2,1,0:T(8,128)(2,1)} %bitcast.87) | data formatting | bytes 7077888 | tf_op jit(solution)/shard_map/reshape | solution.py:217
  74.0 1.7 fusion.25
  75.7 1.5 fusion.24
  77.3 2.3 %copy.78 = bf16[1536,192]{0,1:T(8,128)(2,1)} copy(bf16[1536,192]{1,0:T(8,128)(2,1)} %get-tuple-element.21) | data formatting | bytes 1179648 | tf_op jit(solution)/shard_map/slice | solution.py:348
  80.4 0.8 multiply_cosine_fusion
  81.1 0.2 copy.80
  81.3 1.0 copy.81
  82.3 1.5 copy.75
  83.8 0.3 copy.82
  84.1 3.2 %fusion.15 = f32[2,1024,96]{2,1,0:T(8,128)S(1)} fusion(bf16[1536,2,96]{0,2,1:T(8,128)(2,1)} %bitcast.97, bf16[1024,1536]{1,0:T(8,128)(2,1)} %all-gather.3.cloned.1.call-done), kind=kOutput, calls=%fused_computation.19 | convolution fusion | flops 603979776 | bytes 4521984 | tf_op jit(solution)/shard_map/td,dch->cth/dot_general | solution.py:373
  87.4 0.5 subtract_convert_fusion
  87.8 0.2 copy.90
  88.0 0.2 copy.91
  88.2 0.8 pad_maximum_fusion.2
  89.0 3.5 %all-to-all-start.2 = ((bf16[2,4,256,96]{2,3,0,1:T(8,128)(2,1)}), bf16[2,4,256,96]{2,3,0,1:T(8,128)(2,1)S(1)}, u32[]{:S(2)}, u32[]{:S(2)}) async-start(bf16[2,4,256,96]{2,3,0,1:T(8,128)(2,1)} %pad_maximum_fusion.2), calls=%async_computation.2 | async-start | bytes 786432 | tf_op jit(solution)/shard_map/all_to_all | solution.py:387
  92.5 3.8 %fusion.12 = f32[2,2,1024,96]{2,3,1,0:T(8,128)S(1)} fusion(bf16[1536,2,2,96]{0,3,2,1:T(8,128)(2,1)} %bitcast.96, bf16[1024,1536]{1,0:T(8,128)(2,1)} %all-gather.3.cloned.1.call-done), kind=kOutput, calls=%fused_computation.18 | convolution fusion | flops 1207959552 | bytes 5898240 | tf_op jit(solution)/shard_map/td,dcgh->cgth/dot_general | solution.py:369
  96.3 1.0 subtract_convert_fusion.1
  97.3 1.2 fusion.18
  98.5 1.1 pad_maximum_fusion.1.kn_ref
  99.6 0.5 copy.76
  100.1 0.5 copy.77
  100.5 0.3 copy.83
  100.8 1.0 copy.92
  101.8 1.5 pad_maximum_fusion.q_ref
  103.3 2.6 %all-to-all-done.2 = bf16[2,4,256,96]{2,3,0,1:T(8,128)(2,1)S(1)} async-done(((bf16[2,4,256,96]{2,3,0,1:T(8,128)(2,1)}), bf16[2,4,256,96]{2,3,0,1:T(8,128)(2,1)S(1)}, u32[]{:S(2)}, u32[]{:S(2)}) %all-to-all-start.2) | async-done | bytes 393248 | tf_op jit(solution)/shard_map/all_to_all | solution.py:387
  105.9 3.6 %all-to-all-start.3 = ((bf16[2,4,256,96]{2,3,0,1:T(8,128)(2,1)}), bf16[2,4,256,96]{2,3,0,1:T(8,128)(2,1)S(1)}, u32[]{:S(2)}, u32[]{:S(2)}) async-start(bf16[2,4,256,96]{2,3,0,1:T(8,128)(2,1)} %copy.92), calls=%async_computation.3 | async-start | bytes 786432 | tf_op jit(solution)/shard_map/all_to_all | solution.py:387
  109.6 20.7 %shard_map.114 = bf16[2048,96]{1,0:T(8,128)(2,1)} custom-call(s32[1]{0:T(128)} %copy.109.len_ref, bf16[2,2048,96]{2,1,0:T(8,128)(2,1)} %pad_maximum_fusion.q_ref, bf16[4,2,512,96]{3,2,1,0:T(8,128)(2,1)} %get-tuple-element.7.kc_ref, bf16[4,2,512,96]{3,2,1,0:T(8,128)(2,1)} %get-tuple-element.8.vc_ref, bf16[2,1024,96]{2,1,0:T(8,128)(2,1)} %pad_maximum_fusion.1.kn_ref, ...), custom_call_target="tpu_custom_call" | custom-call | flops 2415919104 | bytes 1966080 | tf_op jit(solution)/shard_map/pallas_call | solution.py:301
  130.3 2.0 %copy.87 = bf16[2,4,256,96]{2,3,0,1:T(8,128)(2,1)} copy(bf16[2,4,256,96]{3,2,1,0:T(8,128)(2,1)} %bitcast.99) | data formatting | bytes 786432 | tf_op jit(solution)/shard_map/reshape | solution.py:400
  132.3 20.7 %shard_map.113 = bf16[2048,96]{1,0:T(8,128)(2,1)} custom-call(s32[1]{0:T(128)} %copy.109.len_ref, bf16[2,2048,96]{2,1,0:T(8,128)(2,1)} %pad_maximum_fusion.q_ref, bf16[4,2,512,96]{3,2,1,0:T(8,128)(2,1)} %get-tuple-element.7.kc_ref, bf16[4,2,512,96]{3,2,1,0:T(8,128)(2,1)} %get-tuple-element.8.vc_ref, bf16[2,1024,96]{2,1,0:T(8,128)(2,1)} %pad_maximum_fusion.1.kn_ref, ...), custom_call_target="tpu_custom_call" | custom-call | flops 2415919104 | bytes 1966080 | tf_op jit(solution)/shard_map/pallas_call | solution.py:301
  153.0 2.0 %copy.84 = bf16[2,4,256,96]{2,3,0,1:T(8,128)(2,1)} copy(bf16[2,4,256,96]{3,2,1,0:T(8,128)(2,1)} %bitcast.98) | data formatting | bytes 786432 | tf_op jit(solution)/shard_map/reshape | solution.py:400
  155.0 0.9 copy.93
  155.9 4.6 %all-to-all-start.1 = ((bf16[2,4,256,96]{2,3,0,1:T(8,128)(2,1)}), bf16[2,4,256,96]{2,3,0,1:T(8,128)(2,1)S(1)}, u32[]{:S(2)}, u32[]{:S(2)}) async-start(bf16[2,4,256,96]{2,3,0,1:T(8,128)(2,1)} %copy.87), calls=%async_computation.1 | async-start | bytes 786432 | tf_op jit(solution)/shard_map/all_to_all | solution.py:401
  160.4 0.9 copy.94
  161.4 4.3 %fusion.23 = (bf16[4,1,2,96,1536]{4,3,2,1,0:T(8,128)(2,1)S(1)}, bf16[4,1,2,96,1536]{4,3,2,1,0:T(8,128)(2,1)}) fusion(bf16[4,2,2,96,1536]{4,3,2,1,0:T(8,128)(2,1)} %bitcast.80), kind=kLoop, calls=%fused_computation.35 | loop fusion | bytes 9437184 | tf_op jit(solution)/shard_map/slice | solution.py:403
  165.6 3.8 %all-to-all-done.1 = bf16[2,4,256,96]{2,3,0,1:T(8,128)(2,1)S(1)} async-done(((bf16[2,4,256,96]{2,3,0,1:T(8,128)(2,1)}), bf16[2,4,256,96]{2,3,0,1:T(8,128)(2,1)S(1)}, u32[]{:S(2)}, u32[]{:S(2)}) %all-to-all-start.1) | async-done | bytes 393248 | tf_op jit(solution)/shard_map/all_to_all | solution.py:401
  169.4 3.5 %all-to-all-start = ((bf16[2,4,256,96]{2,3,0,1:T(8,128)(2,1)}), bf16[2,4,256,96]{2,3,0,1:T(8,128)(2,1)S(1)}, u32[]{:S(2)}, u32[]{:S(2)}) async-start(bf16[2,4,256,96]{2,3,0,1:T(8,128)(2,1)} %copy.84), calls=%async_computation | async-start | bytes 786432 | tf_op jit(solution)/shard_map/all_to_all | solution.py:401
  172.9 3.7 %convolution_bitcast_fusion = f32[256,1536]{1,0:T(8,128)} fusion(bf16[4,1,2,96,1536]{4,3,2,1,0:T(8,128)(2,1)} %get-tuple-element.19, bf16[2,4,256,96]{2,3,0,1:T(8,128)(2,1)S(1)} %all-to-all-done.1), kind=kOutput, calls=%fused_computation.6 | convolution fusion | flops 603979776 | bytes 4325376 | tf_op jit(solution)/shard_map/gsth,sghn->tn/dot_general | solution.py:402
  176.5 5.2 %all-to-all-done = bf16[2,4,256,96]{2,3,0,1:T(8,128)(2,1)S(1)} async-done(((bf16[2,4,256,96]{2,3,0,1:T(8,128)(2,1)}), bf16[2,4,256,96]{2,3,0,1:T(8,128)(2,1)S(1)}, u32[]{:S(2)}, u32[]{:S(2)}) %all-to-all-start) | async-done | bytes 393248 | tf_op jit(solution)/shard_map/all_to_all | solution.py:401
  181.8 3.1 %fusion.8 = bf16[1,256,1536]{2,1,0:T(8,128)(2,1)} fusion(f32[256,1536]{1,0:T(8,128)} %convolution_bitcast_fusion, bf16[4,1,2,96,1536]{4,3,2,1,0:T(8,128)(2,1)S(1)} %get-tuple-element.18, bf16[2,4,256,96]{2,3,0,1:T(8,128)(2,1)S(1)} %all-to-all-done), kind=kOutput, calls=%fused_computation.10 | convolution fusion | flops 604766208 | bytes 5111808 | tf_op jit(solution)/shard_map/gsth,sghn->tn/dot_general | solution.py:402
  (34 shorter events, 0.2 us)
Async XLA Ops:
  7.2 4.5 %copy-start.6 = (bf16[1,512,768]{2,1,0:T(8,128)(2,1)S(1)}, bf16[1,512,768]{2,1,0:T(8,128)(2,1)}, u32[]{:S(2)}) copy-start(bf16[1,512,768]{2,1,0:T(8,128)(2,1)} %param.11) | copy-start | bytes 2359300
  7.2 76.9 %all-gather.3.cloned.1.call-start = ((), (), s32[]{:S(2)}) async-start(), calls=%async_computation.4 | async-start | bytes 3932160 | tf_op jit(solution)/shard_map/all_gather | solution.py:336
  11.6 1.7 copy-start.7
  11.6 149.7 %all-gather.5.cloned.1.call-start = ((), (), s32[]{:S(2)}) async-start(), calls=%async_computation.5 | async-start | bytes 5898240 | tf_op jit(solution)/shard_map/all_gather | solution.py:352
  12.0 3.0 %copy-start.8 = (bf16[24,384]{1,0:T(8,128)(2,1)S(1)}, bf16[24,384]{1,0:T(8,128)(2,1)}, u32[]{:S(2)}) copy-start(bf16[24,384]{1,0:T(8,128)(2,1)} %param.14) | copy-start | bytes 55300
  12.0 3.0 %copy-start.9 = (bf16[24,384]{1,0:T(8,128)(2,1)S(1)}, bf16[24,384]{1,0:T(8,128)(2,1)}, u32[]{:S(2)}) copy-start(bf16[24,384]{1,0:T(8,128)(2,1)} %param.17) | copy-start | bytes 55300
  12.0 3.0 %copy-start.10 = (bf16[24,192]{1,0:T(8,128)(2,1)S(1)}, bf16[24,192]{1,0:T(8,128)(2,1)}, u32[]{:S(2)}) copy-start(bf16[24,192]{1,0:T(8,128)(2,1)} %param.15) | copy-start | bytes 27652
  12.0 3.0 %copy-start.11 = (bf16[24,192]{1,0:T(8,128)(2,1)S(1)}, bf16[24,192]{1,0:T(8,128)(2,1)}, u32[]{:S(2)}) copy-start(bf16[24,192]{1,0:T(8,128)(2,1)} %param.16) | copy-start | bytes 27652
  77.3 5.0 %copy-start = (bf16[1536,384]{1,0:T(8,128)(2,1)S(1)}, bf16[1536,384]{1,0:T(8,128)(2,1)}, u32[]{:S(2)}) copy-start(bf16[1536,384]{1,0:T(8,128)(2,1)} %get-tuple-element.22) | copy-start | bytes 3538948
  79.6 4.2 %copy-start.2 = (bf16[1536,192]{1,0:T(8,128)(2,1)S(1)}, bf16[1536,192]{1,0:T(8,128)(2,1)}, u32[]{:S(2)}) copy-start(bf16[1536,192]{1,0:T(8,128)(2,1)} %get-tuple-element.20) | copy-start | bytes 1769476
  84.1 3.3 %copy-start.4 = (f32[1024,48]{1,0:T(8,128)S(1)}, f32[1024,48]{1,0:T(8,128)}, u32[]{:S(2)}) copy-start(f32[1024,48]{1,0:T(8,128)} %copy.81) | copy-start | bytes 589828
  89.0 16.9 %all-to-all-start.2 = ((bf16[2,4,256,96]{2,3,0,1:T(8,128)(2,1)}), bf16[2,4,256,96]{2,3,0,1:T(8,128)(2,1)S(1)}, u32[]{:S(2)}, u32[]{:S(2)}) async-start(bf16[2,4,256,96]{2,3,0,1:T(8,128)(2,1)} %pad_maximum_fusion.2), calls=%async_computation.2 | async-start | bytes 786432 | tf_op jit(solution)/shard_map/all_to_all | solution.py:387
  92.5 4.8 %copy-start.1 = (bf16[1024,1536]{1,0:T(8,128)(2,1)S(1)}, bf16[1024,1536]{1,0:T(8,128)(2,1)}, u32[]{:S(2)}) copy-start(bf16[1024,1536]{1,0:T(8,128)(2,1)} %all-gather.3.cloned.1.call-done) | copy-start | bytes 9437188
  98.5 1.6 copy-start.5
  100.8 5.1 %copy-start.3 = (bf16[2,96,1024]{1,2,0:T(8,128)(2,1)}, bf16[2,96,1024]{1,2,0:T(8,128)(2,1)S(1)}, u32[]{:S(2)}) copy-start(bf16[2,96,1024]{1,2,0:T(8,128)(2,1)S(1)} %copy.83) | copy-start | bytes 1179652
  105.9 50.0 %all-to-all-start.3 = ((bf16[2,4,256,96]{2,3,0,1:T(8,128)(2,1)}), bf16[2,4,256,96]{2,3,0,1:T(8,128)(2,1)S(1)}, u32[]{:S(2)}, u32[]{:S(2)}) async-start(bf16[2,4,256,96]{2,3,0,1:T(8,128)(2,1)} %copy.92), calls=%async_computation.3 | async-start | bytes 786432 | tf_op jit(solution)/shard_map/all_to_all | solution.py:387
  155.9 13.5 %all-to-all-start.1 = ((bf16[2,4,256,96]{2,3,0,1:T(8,128)(2,1)}), bf16[2,4,256,96]{2,3,0,1:T(8,128)(2,1)S(1)}, u32[]{:S(2)}, u32[]{:S(2)}) async-start(bf16[2,4,256,96]{2,3,0,1:T(8,128)(2,1)} %copy.87), calls=%async_computation.1 | async-start | bytes 786432 | tf_op jit(solution)/shard_map/all_to_all | solution.py:401
  169.4 12.4 %all-to-all-start = ((bf16[2,4,256,96]{2,3,0,1:T(8,128)(2,1)}), bf16[2,4,256,96]{2,3,0,1:T(8,128)(2,1)S(1)}, u32[]{:S(2)}, u32[]{:S(2)}) async-start(bf16[2,4,256,96]{2,3,0,1:T(8,128)(2,1)} %copy.84), calls=%async_computation | async-start | bytes 786432 | tf_op jit(solution)/shard_map/all_to_all | solution.py:401
Sparse Core Ops, SparseCore 0:
  11.8 53.2 all-gather.2
  75.9 50.2 all-gather.4

commit v11 on v9

--- a/solution.py
+++ b/solution.py
@@ -256,12 +256,13 @@
         visible = start + key_offset < length
         return step(keys, values, visible, carry)
 
+    block_n = kn_ref.shape[2]
+    query_new = first + lax.broadcasted_iota(jnp.int32, (block_q, block_n), 0)
+    offset_new = lax.broadcasted_iota(jnp.int32, (block_q, block_n), 1)
+
     def new_step(block, carry):
-        start = pl.multiple_of(block * block_k, block_k)
-        keys = kn_ref[0, pl.ds(start, block_k), :]
-        values = vn_ref[0, pl.ds(start, block_k), :]
-        visible = start + key_offset <= query_index
-        return step(keys, values, visible, carry)
+        visible = block * block_n + offset_new <= query_new
+        return step(kn_ref[block, 0], vn_ref[block, 0], visible, carry)
 
     carry = (
         jnp.full((block_q, 1), -jnp.inf, jnp.float32),
@@ -270,9 +271,9 @@
     )
     live_blocks = (length + block_k - 1) // block_k
     carry = lax.fori_loop(0, live_blocks, cache_step, carry)
-    new_blocks = (first + block_q - 1) // block_k + 1
+    new_blocks = (first + block_q - 1) // block_n + 1
     peak, total, acc = lax.fori_loop(0, new_blocks, new_step, carry)
-    o_ref[0] = (acc / total).astype(o_ref.dtype)
+    o_ref[...] = (acc / total).astype(o_ref.dtype).reshape(o_ref.shape)
 
 
 def flash_attention(lengths, queries, keys_old, values_old, keys_new, values_new, tokens, scale):
@@ -282,10 +283,14 @@
     block_q = min(BLOCK_Q, tokens)
     grid = (heads, rows // block_q)
     whole_cache = pl.BlockSpec((blocks, 1, block_k, width), lambda c, i, n: (0, c, 0, 0))
-    whole_new = pl.BlockSpec((1, tokens, width), lambda c, i, n: (c, 0, 0))
+    peers, _, block_n, _ = keys_new.shape
+    whole_new = pl.BlockSpec((peers, 1, block_n, width), lambda c, i, n: (0, c, 0, 0))
+    per_q = block_q // block_n
+    halves = tokens // block_q
+    groups = rows // tokens
     return pl.pallas_call(
         functools.partial(flash_kernel, tokens, scale),
-        out_shape=jax.ShapeDtypeStruct((heads, rows, width), jnp.bfloat16),
+        out_shape=jax.ShapeDtypeStruct((peers, heads, groups, block_n, width), jnp.bfloat16),
         grid_spec=pltpu.PrefetchScalarGridSpec(
             num_scalar_prefetch=1,
             grid=grid,
@@ -293,7 +298,10 @@
                 pl.BlockSpec((1, block_q, width), lambda c, i, n: (c, i, 0)),
                 whole_cache, whole_cache, whole_new, whole_new,
             ],
-            out_specs=pl.BlockSpec((1, block_q, width), lambda c, i, n: (c, i, 0)),
+            out_specs=pl.BlockSpec(
+                (per_q, 1, 1, block_n, width),
+                lambda c, i, n: (lax.rem(i, halves), c, i // halves, 0, 0),
+            ),
         ),
         cost_estimate=pl.CostEstimate(
             flops=4 * heads * rows * (slots + tokens) * width,
@@ -301,6 +309,67 @@
             bytes_accessed=2 * width * heads * (2 * rows + 2 * slots + 2 * tokens),
         ),
     )(lengths, queries, keys_old, values_old, keys_new, values_new)
+
+
+def exchange_kernel(k_ref, v_ref, c_ref, k_out, v_out, c_out, send_sem, recv_sem, local_sem):
+    me = lax.axis_index("kv")
+    req = lax.axis_index("req")
+    count = lax.axis_size("kv")
+    arrays = ((k_ref, k_out), (v_ref, v_out), (c_ref, c_out))
+    barrier = pltpu.get_barrier_semaphore()
+
+    def greet(step, carry):
+        peer = lax.rem(me + step, count)
+        pl.semaphore_signal(barrier, inc=1, device_id=(req, peer), device_id_type=MESH)
+        return carry
+
+    lax.fori_loop(1, count, greet, 0)
+    pl.semaphore_wait(barrier, count - 1)
+    local = []
+    for which, (src, dst) in enumerate(arrays):
+        c = pltpu.make_async_copy(src.at[me], dst.at[me], local_sem.at[which])
+        c.start()
+        local.append(c)
+
+    def send(step, carry):
+        peer = lax.rem(me + step, count)
+        for which, (src, dst) in enumerate(arrays):
+            remote(src.at[peer], dst.at[me], send_sem.at[which, step - 1],
+                   recv_sem.at[which, step - 1], (req, peer)).start()
+        return carry
+
+    lax.fori_loop(1, count, send, 0)
+
+    def finish(step, carry):
+        peer = lax.rem(me + step, count)
+        source = lax.rem(me + count - step, count)
+        for which, (src, dst) in enumerate(arrays):
+            remote(src.at[peer], dst.at[me], send_sem.at[which, step - 1],
+                   recv_sem.at[which, step - 1], (req, peer)).wait_send()
+            remote(src.at[me], dst.at[source], send_sem.at[which, step - 1],
+                   recv_sem.at[which, step - 1], (req, source)).wait_recv()
+        return carry
+
+    lax.fori_loop(1, count, finish, 0)
+    for c in local:
+        c.wait()
+
+
+def exchange_kv(keys, values, context):
+    count = lax.axis_size("kv")
+    anywhere = pl.BlockSpec(memory_space=pl.ANY)
+    return pl.pallas_call(
+        exchange_kernel,
+        out_shape=tuple(jax.ShapeDtypeStruct(a.shape, a.dtype) for a in (keys, values, context)),
+        in_specs=[anywhere, anywhere, anywhere],
+        out_specs=(anywhere, anywhere, anywhere),
+        scratch_shapes=[
+            pltpu.SemaphoreType.DMA((3, count - 1)),
+            pltpu.SemaphoreType.DMA((3, count - 1)),
+            pltpu.SemaphoreType.DMA((3,)),
+        ],
+        compiler_params=pltpu.CompilerParams(collective_id=1, has_side_effects=True),
+    )(keys, values, context)
 
 
 def body(hidden, lengths, key_cache, value_cache, norm_gain, w_query, w_key, w_value, w_out):
@@ -355,33 +424,38 @@
         "td,dcgh->cgth", normed_all, wq.reshape(width, kv_heads_here, groups, HD),
         preferred_element_type=jnp.float32,
     )
+    normed_blocks = normed_all.reshape(kv_count, rows_here, width)
     proj_k = jnp.einsum(
-        "td,dch->cth", normed_all, wk.reshape(width, kv_heads_here, HD),
+        "std,dch->scth", normed_blocks, wk.reshape(width, kv_heads_here, HD),
         preferred_element_type=jnp.float32,
     )
     proj_v = jnp.einsum(
-        "td,dch->cth", normed_all, wv.reshape(width, kv_heads_here, HD),
+        "std,dch->scth", normed_blocks, wv.reshape(width, kv_heads_here, HD),
         preferred_element_type=jnp.float32,
     )
+    cosine_blocks = cosine.reshape(kv_count, 1, rows_here, half)
+    sine_blocks = sine.reshape(kv_count, 1, rows_here, half)
     query_heads = turn(proj_q).astype(jnp.bfloat16).reshape(kv_heads_here, groups * appended, HD)
-    keys_new = turn(proj_k).astype(jnp.bfloat16)
+    first_k = proj_k[..., :half]
+    second_k = proj_k[..., half:]
+    keys_new = jnp.concatenate(
+        [first_k * cosine_blocks - second_k * sine_blocks,
+         second_k * cosine_blocks + first_k * sine_blocks], axis=-1,
+    ).astype(jnp.bfloat16)
     values_new = proj_v.astype(jnp.bfloat16)
-
-    def to_tokens(values):
-        parts = values.reshape(kv_heads_here, kv_count, rows_here, HD)
-        got = lax.all_to_all(parts, "kv", split_axis=1, concat_axis=1, tiled=True)
-        return jnp.transpose(got, (2, 1, 0, 3)).reshape(rows_here, kv_count * kv_heads_here * HD)
-
-    new_keys = to_tokens(keys_new)
-    new_values = to_tokens(values_new)
 
     contexts = flash_attention(
         lengths, query_heads, keys_old, values_old, keys_new, values_new, appended, scale,
     )
-    parts = contexts.reshape(kv_heads_here, groups, kv_count, rows_here, HD)
-    got = lax.all_to_all(parts, "kv", split_axis=2, concat_axis=2, tiled=True)
+    keys_got, values_got, got = exchange_kv(keys_new, values_new, contexts)
+
+    def to_tokens(values):
+        return jnp.transpose(values, (2, 0, 1, 3)).reshape(rows_here, kv_count * kv_heads_here * HD)
+
+    new_keys = to_tokens(keys_got)
+    new_values = to_tokens(values_got)
     attended = jnp.einsum(
-        "cgsth,scghn->tn", got,
+        "scgth,scghn->tn", got,
         wo_full.reshape(kv_count, kv_heads_here, groups, HD, wo_full.shape[1]),
         preferred_element_type=jnp.float32,
     ).astype(jnp.bfloat16)

time: 180 us -> 191 us (1.061)
  the two profiles are of different devices: /device:TPU:1 before, /device:TPU:11 now
where the time goes in v11:
time: 191 us
  Pallas kernels  126 us (66%)
  local copies, waits for them, and re-layouts  22 us (12%)
  matrix products  15.1 us (8%)
  between operations  14.9 us (8%)
  other arithmetic  12.3 us (6%)
    pallas_call x1, Pallas kernels, gather_req(): pl.pallas_call(functools.partial(plane_ring_kernel, planes, runs), out_sh...  55.4 us
    pallas_call x1, Pallas kernels, flash_attention(): pl.pallas_call(functools.partial(flash_kernel, tokens, scale), out_shape=...  42.8 us
    pallas_call x1, Pallas kernels, exchange_kv(): pl.pallas_call(exchange_kernel, out_shape=tuple((jax.ShapeDtypeStruct(a.s...  28.3 us
    dot_general x1, matrix products, body(): jnp.einsum('scgth,scghn->tn', got, wo_full.reshape(kv_count, kv_heads_her...  4.65 us
  transfers between devices with their start and end apart: 2, of which 0 were waited for; matrix products, arithmetic and copies ran while one was open for 21% of the time, Pallas kernels for 66%

profile of v11, /device:TPU:11, one launch (start us, length us, event | category | flops | bytes accessed | tf_op | source)
XLA Modules:
  0.0 190.9 jit_solution(8775396159657911697)
XLA Ops:
  7.2 0.0 copy-start.4
  7.2 0.0 all-gather.3.cloned.1.call-start
  7.2 0.8 convert_element_type.35
  8.0 1.4 fusion.13
  9.3 2.3 %fusion.15 = bf16[256,1536]{1,0:T(8,128)(2,1)} fusion(bf16[1,256,1536]{2,1,0:T(8,128)(2,1)} %param.9, f32[1536]{0:T(1024)S(1)} %convert_element_type.35, f32[256]{0:T(256)S(1)} %add_rsqrt_fusion), kind=kLoop, calls=%fused_computation.11 | loop fusion | flops 1572864 | bytes 1580032 | tf_op jit(solution)/shard_map/convert_element_type | solution.py:22
  11.7 0.0 all-gather.3.cloned.1.call-update
  11.7 0.0 all-gather.5.cloned.1.call-start
  11.8 0.0 copy-done.4
  11.8 0.3 copy.35
  12.1 1.3 copy.36
  13.4 0.0 copy-done.5
  13.4 0.0 copy-start.9
  13.4 0.3 copy.37
  13.7 1.4 copy.38
  15.1 0.0 copy-done.6
  15.1 0.0 copy-done.7
  15.1 0.0 copy-done.8
  15.1 0.7 concatenate.16.src_ref
  15.8 55.4 %shard_map.112 = (bf16[8,8,24,1152]{3,2,1,0:T(8,128)(2,1)}, bf16[4,2,512,96]{3,2,1,0:T(8,128)(2,1)}, bf16[4,2,512,96]{3,2,1,0:T(8,128)(2,1)}) custom-call(bf16[24,1152]{1,0:T(8,128)(2,1)} %concatenate.16.src_ref, bf16[4,2,512,96]{3,2,1,0:T(8,128)(2,1)} %bitcast.67, bf16[4,2,512,96]{3,2,1,0:T(8,128)(2,1)} %bitcast.68), custom_call_target="tpu_custom_call" | custom-call | tf_op jit(solution)/shard_map/pallas_call | solution.py:192
  71.2 2.3 %copy.39 = bf16[8,4,2,24,1152]{4,3,2,0,1:T(8,128)(2,1)S(1)} copy(bf16[8,4,2,24,1152]{4,3,2,1,0:T(8,128)(2,1)} %bitcast.69) | data formatting | bytes 7077888 | tf_op jit(solution)/shard_map/reshape | solution.py:217
  73.5 1.7 fusion.20
  75.2 0.0 all-gather.5.cloned.1.call-update
  75.2 1.5 fusion.21
  76.7 2.3 %copy.40 = bf16[1536,192]{0,1:T(8,128)(2,1)} copy(bf16[1536,192]{1,0:T(8,128)(2,1)} %get-tuple-element.24) | data formatting | bytes 1179648 | tf_op jit(solution)/shard_map/slice | solution.py:402
  79.7 1.5 copy.44
  81.2 0.3 copy.42
  81.5 0.8 multiply_cosine_fusion.1
  82.3 3.0 %multiply_cosine_fusion = (f32[4,256,48]{2,1,0:T(8,128)S(1)}, f32[4,256,48]{2,1,0:T(8,128)}) fusion(f32[48]{0:T(128)S(1)} %negate_power_fusion, f32[4,256]{1,0:T(4,128)S(1)} %add_convert_fusion.3), kind=kLoop, calls=%fused_computation.22 | loop fusion | flops 49152 | bytes 397504 | tf_op jit(solution)/shard_map/cos | solution.py:412
  85.3 3.6 %fusion.16 = f32[2,2,1024,96]{2,3,1,0:T(8,128)S(1)} fusion(bf16[1536,2,2,96]{0,3,2,1:T(8,128)(2,1)S(1)} %bitcast.79, bf16[1024,1536]{1,0:T(8,128)(2,1)} %all-gather.3.cloned.1.call-done), kind=kOutput, calls=%fused_computation.12 | convolution fusion | flops 1207959552 | bytes 5898240 | tf_op jit(solution)/shard_map/td,dcgh->cgth/dot_general | solution.py:423
  88.8 1.0 subtract_convert_fusion.1
  89.8 0.5 copy.45
  90.3 1.5 copy.46
  91.8 3.8 %convolution_convert_fusion = bf16[2,96,4,256]{3,1,2,0:T(8,128)(2,1)} fusion(bf16[1536,2,96,1]{0,2,3,1:T(8,128)(2,1)S(1)} %bitcast.74, bf16[4,256,1536,1]{2,1,0,3:T(8,128)(2,1)} %bitcast.72), kind=kOutput, calls=%fused_computation.14 | convolution fusion | flops 604176384 | bytes 4128768 | tf_op jit(solution)/shard_map/std,dch->scth/dot_general | solution.py:432
  95.6 2.1 %copy.43 = bf16[2,96,4,256]{1,3,0,2:T(8,128)(2,1)} copy(bf16[2,96,4,256]{3,1,2,0:T(8,128)(2,1)} %convolution_convert_fusion) | data formatting | bytes 786432 | tf_op jit(solution)/shard_map/convert_element_type | solution.py:445
  97.7 3.1 %convolution_bitcast_fusion = f32[4,2,256,96]{3,2,1,0:T(8,128)S(1)} fusion(bf16[1536,2,96,1]{0,2,1,3:T(8,128)(2,1)} %bitcast.80, bf16[4,256,1536,1]{2,1,3,0:T(8,128)(2,1)} %bitcast.73), kind=kOutput, calls=%fused_computation.13 | convolution fusion | flops 603979776 | bytes 4521984 | tf_op jit(solution)/shard_map/std,dch->scth/dot_general | solution.py:428
  100.8 0.0 copy-done.2
  100.8 0.5 subtract_convert_fusion
  101.3 1.1 pad_maximum_fusion.1.kn_ref.k_ref
  102.4 1.6 pad_maximum_fusion.q_ref
  104.0 42.8 %shard_map.113.c_ref = bf16[4,2,2,256,96]{4,3,2,1,0:T(8,128)(2,1)} custom-call(s32[1]{0:T(128)} %copy.70.len_ref, bf16[2,2048,96]{2,1,0:T(8,128)(2,1)} %pad_maximum_fusion.q_ref, bf16[4,2,512,96]{3,2,1,0:T(8,128)(2,1)} %get-tuple-element.10.kc_ref, bf16[4,2,512,96]{3,2,1,0:T(8,128)(2,1)} %get-tuple-element.11.vc_ref, ...), custom_call_target="tpu_custom_call" | custom-call | flops 4831838208 | bytes 3932160 | tf_op jit(solution)/shard_map/pallas_call | solution.py:291
  146.8 28.3 %shard_map.114 = (bf16[4,2,256,96]{3,2,1,0:T(8,128)(2,1)}, bf16[4,2,256,96]{3,2,1,0:T(8,128)(2,1)}, bf16[4,2,2,256,96]{4,3,2,1,0:T(8,128)(2,1)}) custom-call(bf16[4,2,256,96]{3,2,1,0:T(8,128)(2,1)} %pad_maximum_fusion.1.kn_ref.k_ref, bf16[4,2,256,96]{3,2,1,0:T(8,128)(2,1)} %bitcast.76, bf16[4,2,2,256,96]{4,3,2,1,0:T(8,128)(2,1)} %shard_map.113.c_ref), custom_call_target="tpu_custom_call" | custom-call | tf_op jit(solution)/shard_map/pallas_call | solution.py:361
  175.0 0.0 copy-start.10
  175.0 1.3 copy.49
  176.4 0.9 copy.51
  177.3 1.2 copy.50
  178.5 0.9 copy.52
  179.4 0.0 copy-done.10
  179.5 4.7 %fusion.10 = bf16[1,256,1536]{2,1,0:T(8,128)(2,1)} fusion(bf16[4,2,2,96,1536]{4,3,2,1,0:T(8,128)(2,1)} %bitcast.83, bf16[4,2,2,256,96]{4,3,2,1,0:T(8,128)(2,1)S(1)} %copy-done.10), kind=kOutput, calls=%fused_computation.6 | convolution fusion | flops 1208352768 | bytes 6291456 | tf_op jit(solution)/shard_map/scgth,scghn->tn/dot_general | solution.py:457
  (18 shorter events, 0.1 us)
Async XLA Ops:
  7.2 4.6 %copy-start.4 = (bf16[1,512,768]{2,1,0:T(8,128)(2,1)S(1)}, bf16[1,512,768]{2,1,0:T(8,128)(2,1)}, u32[]{:S(2)}) copy-start(bf16[1,512,768]{2,1,0:T(8,128)(2,1)} %param.11) | copy-start | bytes 2359300
  7.2 78.1 %all-gather.3.cloned.1.call-start = ((), (), s32[]{:S(2)}) async-start(), calls=%async_computation | async-start | bytes 3932160 | tf_op jit(solution)/shard_map/all_gather | solution.py:390
  11.7 1.7 copy-start.5
  11.7 167.7 %all-gather.5.cloned.1.call-start = ((), (), s32[]{:S(2)}) async-start(), calls=%async_computation.1 | async-start | bytes 5898240 | tf_op jit(solution)/shard_map/all_gather | solution.py:406
  13.4 1.7 copy-start.6
  13.4 1.7 copy-start.7
  13.4 1.7 copy-start.8
  13.4 1.7 copy-start.9
  76.7 3.0 %copy-start = (bf16[1536,384]{1,0:T(8,128)(2,1)S(1)}, bf16[1536,384]{1,0:T(8,128)(2,1)}, u32[]{:S(2)}) copy-start(bf16[1536,384]{1,0:T(8,128)(2,1)} %get-tuple-element.21) | copy-start | bytes 3538948
  76.7 4.5 %copy-start.1 = (bf16[1536,192]{1,0:T(8,128)(2,1)S(1)}, bf16[1536,192]{1,0:T(8,128)(2,1)}, u32[]{:S(2)}) copy-start(bf16[1536,192]{1,0:T(8,128)(2,1)} %get-tuple-element.23) | copy-start | bytes 1769476
  81.2 4.0 %copy-start.3 = (bf16[1536,384]{0,1:T(8,128)(2,1)S(1)}, bf16[1536,384]{0,1:T(8,128)(2,1)}, u32[]{:S(2)}) copy-start(bf16[1536,384]{0,1:T(8,128)(2,1)} %copy.44) | copy-start | bytes 3538948
  97.7 3.1 %copy-start.2 = (f32[4,256,48]{2,1,0:T(8,128)S(1)}, f32[4,256,48]{2,1,0:T(8,128)}, u32[]{:S(2)}) copy-start(f32[4,256,48]{2,1,0:T(8,128)} %get-tuple-element.32) | copy-start | bytes 589828
  175.0 4.4 %copy-start.10 = (bf16[4,2,2,256,96]{4,3,2,1,0:T(8,128)(2,1)S(1)}, bf16[4,2,2,256,96]{4,3,2,1,0:T(8,128)(2,1)}, u32[]{:S(2)}) copy-start(bf16[4,2,2,256,96]{4,3,2,1,0:T(8,128)(2,1)} %get-tuple-element.12) | copy-start | bytes 2359300
Sparse Core Ops, SparseCore 0:
  11.8 53.1 all-gather.2
  75.3 42.8 all-gather.4

commit v12 on v9

--- a/solution.py
+++ b/solution.py
@@ -239,24 +239,33 @@
         score = lax.dot_general(
             q, keys, (((1,), (1,)), ((), ())), preferred_element_type=jnp.float32
         ) * scale
-        score = jnp.where(visible, score, masked_score)
+        if visible is not None:
+            score = jnp.where(visible, score, masked_score)
         new_peak = jnp.maximum(peak, jnp.max(score, axis=1, keepdims=True))
         alpha = jnp.exp(peak - new_peak)
-        weights = jnp.where(visible, jnp.exp(score - new_peak), 0.0)
+        weights = jnp.exp(score - new_peak)
+        if visible is not None:
+            weights = jnp.where(visible, weights, 0.0)
         total = alpha * total + jnp.sum(weights, axis=1, keepdims=True)
         acc = alpha * acc + jnp.dot(
             weights.astype(jnp.bfloat16), values, preferred_element_type=jnp.float32
         )
         return new_peak, total, acc
 
-    def cache_step(block, carry):
+    def cache_full(block, carry):
+        return step(kc_ref[block, 0], vc_ref[block, 0], None, carry)
+
+    def cache_part(block, carry):
+        visible = block * block_k + key_offset < length
+        return step(kc_ref[block, 0], vc_ref[block, 0], visible, carry)
+
+    def new_full(block, carry):
         start = pl.multiple_of(block * block_k, block_k)
-        keys = kc_ref[block, 0]
-        values = vc_ref[block, 0]
-        visible = start + key_offset < length
-        return step(keys, values, visible, carry)
-
-    def new_step(block, carry):
+        keys = kn_ref[0, pl.ds(start, block_k), :]
+        values = vn_ref[0, pl.ds(start, block_k), :]
+        return step(keys, values, None, carry)
+
+    def new_part(block, carry):
         start = pl.multiple_of(block * block_k, block_k)
         keys = kn_ref[0, pl.ds(start, block_k), :]
         values = vn_ref[0, pl.ds(start, block_k), :]
@@ -268,10 +277,14 @@
         jnp.zeros((block_q, 1), jnp.float32),
         jnp.zeros((block_q, width), jnp.float32),
     )
+    full_blocks = length // block_k
     live_blocks = (length + block_k - 1) // block_k
-    carry = lax.fori_loop(0, live_blocks, cache_step, carry)
+    carry = lax.fori_loop(0, full_blocks, cache_full, carry)
+    carry = lax.fori_loop(full_blocks, live_blocks, cache_part, carry)
+    clear_blocks = first // block_k
     new_blocks = (first + block_q - 1) // block_k + 1
-    peak, total, acc = lax.fori_loop(0, new_blocks, new_step, carry)
+    carry = lax.fori_loop(0, clear_blocks, new_full, carry)
+    peak, total, acc = lax.fori_loop(clear_blocks, new_blocks, new_part, carry)
     o_ref[0] = (acc / total).astype(o_ref.dtype)
 
 

time: 180 us -> 180 us (level)
  the two profiles are of different devices: /device:TPU:1 before, /device:TPU:2 now
where the time goes in v12:
time: 180 us; the launch traced here: 179 us
  Pallas kernels  94.8 us (53%)
  local copies, waits for them, and re-layouts  21.3 us (12%)
  between operations  14.9 us (8%)
  waiting for transfers between devices  14 us (8%)
  matrix products  12.7 us (7%)
  starting transfers between devices  11.7 us (6%)
  other arithmetic  10 us (6%)
    pallas_call x1, Pallas kernels, gather_req(): pl.pallas_call(functools.partial(plane_ring_kernel, planes, runs), out_sh...  55.5 us
    pallas_call x1, Pallas kernels, flash_attention(): pl.pallas_call(functools.partial(flash_kernel, tokens, scale), out_shape=...  39.2 us
    all_to_all x1, waiting for transfers between devices, body(): got = lax.all_to_all(parts, 'kv', split_axis=2, concat_axis=2, tiled=True)  11.3 us
    all_to_all x2, starting transfers between devices, to_tokens(): got = lax.all_to_all(parts, 'kv', split_axis=1, concat_axis=1, tiled=True)  7.11 us
    dot_general x1, matrix products, body(): jnp.einsum('cgsth,scghn->tn', got, wo_full.reshape(kv_count, kv_heads_her...  4.62 us
    all_to_all x1, starting transfers between devices, body(): got = lax.all_to_all(parts, 'kv', split_axis=2, concat_axis=2, tiled=True)  4.53 us
    dot_general x1, matrix products, body(): jnp.einsum('td,dcgh->cgth', normed_all, wq.reshape(width, kv_heads_here,...  3.8 us
  transfers between devices with their start and end apart: 5, of which 2 were waited for; matrix products, arithmetic and copies ran while one was open for 19% of the time, Pallas kernels for 53%

profile of v12, /device:TPU:2, one launch (start us, length us, event | category | flops | bytes accessed | tf_op | source)
XLA Modules:
  0.0 179.5 jit_solution(11432330619791641111)
XLA Ops:
  7.2 0.0 all-gather.3.cloned.1.call-start
  7.2 0.8 convert_element_type.32
  8.0 1.4 fusion.17
  9.3 2.3 %fusion.19 = bf16[256,1536]{1,0:T(8,128)(2,1)} fusion(bf16[1,256,1536]{2,1,0:T(8,128)(2,1)} %param.9, f32[1536]{0:T(1024)S(1)} %convert_element_type.32, f32[256]{0:T(256)S(1)} %add_rsqrt_fusion), kind=kLoop, calls=%fused_computation.15 | loop fusion | flops 1572864 | bytes 1580032 | tf_op jit(solution)/shard_map/convert_element_type | solution.py:22
  11.6 0.0 all-gather.3.cloned.1.call-update
  11.6 0.0 all-gather.5.cloned.1.call-start
  11.7 0.3 copy.64
  12.0 1.3 copy.65
  13.3 0.0 copy-start.11
  13.3 0.3 copy.66
  13.6 1.4 copy.67
  15.0 0.7 concatenate.24.src_ref
  15.7 55.5 %shard_map.112 = (bf16[8,8,24,1152]{3,2,1,0:T(8,128)(2,1)}, bf16[4,2,512,96]{3,2,1,0:T(8,128)(2,1)}, bf16[4,2,512,96]{3,2,1,0:T(8,128)(2,1)}) custom-call(bf16[24,1152]{1,0:T(8,128)(2,1)} %concatenate.24.src_ref, bf16[4,2,512,96]{3,2,1,0:T(8,128)(2,1)} %bitcast.69, bf16[4,2,512,96]{3,2,1,0:T(8,128)(2,1)} %bitcast.71), custom_call_target="tpu_custom_call" | custom-call | tf_op jit(solution)/shard_map/pallas_call | solution.py:192
  71.2 2.3 %copy.68 = bf16[8,4,2,24,1152]{4,3,2,0,1:T(8,128)(2,1)S(1)} copy(bf16[8,4,2,24,1152]{4,3,2,1,0:T(8,128)(2,1)} %bitcast.73) | data formatting | bytes 7077888 | tf_op jit(solution)/shard_map/reshape | solution.py:217
  73.5 1.7 fusion.31
  75.2 0.0 all-gather.5.cloned.1.call-update
  75.3 1.5 fusion.30
  76.8 2.3 %copy.72 = bf16[1536,192]{0,1:T(8,128)(2,1)} copy(bf16[1536,192]{1,0:T(8,128)(2,1)} %get-tuple-element.19) | data formatting | bytes 1179648 | tf_op jit(solution)/shard_map/slice | solution.py:346
  79.8 0.8 multiply_cosine_fusion
  80.5 0.2 copy.74
  80.7 1.0 copy.75
  81.8 1.5 copy.69
  83.2 0.3 copy.76
  83.5 0.0 all-gather.3.cloned.1.call-done
  83.5 3.1 %fusion.23 = f32[2,1024,96]{2,1,0:T(8,128)S(1)} fusion(bf16[1536,2,96]{0,2,1:T(8,128)(2,1)} %bitcast.83, bf16[1024,1536]{1,0:T(8,128)(2,1)} %all-gather.3.cloned.1.call-done), kind=kOutput, calls=%fused_computation.17 | convolution fusion | flops 603979776 | bytes 4521984 | tf_op jit(solution)/shard_map/td,dch->cth/dot_general | solution.py:371
  86.7 0.5 subtract_convert_fusion
  87.1 0.2 copy.81
  87.3 0.2 copy.82
  87.5 0.8 pad_maximum_fusion.2
  88.3 3.5 %all-to-all-start.1 = ((bf16[2,4,256,96]{2,3,0,1:T(8,128)(2,1)}), bf16[2,4,256,96]{2,3,0,1:T(8,128)(2,1)S(1)}, u32[]{:S(2)}, u32[]{:S(2)}) async-start(bf16[2,4,256,96]{2,3,0,1:T(8,128)(2,1)} %pad_maximum_fusion.2), calls=%async_computation.1 | async-start | bytes 786432 | tf_op jit(solution)/shard_map/all_to_all | solution.py:385
  91.8 3.8 %fusion.20 = f32[2,2,1024,96]{2,3,1,0:T(8,128)S(1)} fusion(bf16[1536,2,2,96]{0,3,2,1:T(8,128)(2,1)} %bitcast.81, bf16[1024,1536]{1,0:T(8,128)(2,1)} %all-gather.3.cloned.1.call-done), kind=kOutput, calls=%fused_computation.16 | convolution fusion | flops 1207959552 | bytes 5898240 | tf_op jit(solution)/shard_map/td,dcgh->cgth/dot_general | solution.py:367
  95.6 1.0 subtract_convert_fusion.1
  96.6 1.2 fusion.26
  97.8 1.1 pad_maximum_fusion.1.kn_ref
  98.9 0.5 copy.70
  99.4 0.5 copy.71
  99.8 0.3 copy.77
  100.1 1.0 copy.83
  101.1 1.5 pad_maximum_fusion.q_ref
  102.6 2.6 %all-to-all-done.1 = bf16[2,4,256,96]{2,3,0,1:T(8,128)(2,1)S(1)} async-done(((bf16[2,4,256,96]{2,3,0,1:T(8,128)(2,1)}), bf16[2,4,256,96]{2,3,0,1:T(8,128)(2,1)S(1)}, u32[]{:S(2)}, u32[]{:S(2)}) %all-to-all-start.1) | async-done | bytes 393248 | tf_op jit(solution)/shard_map/all_to_all | solution.py:385
  105.2 3.6 %all-to-all-start.2 = ((bf16[2,4,256,96]{2,3,0,1:T(8,128)(2,1)}), bf16[2,4,256,96]{2,3,0,1:T(8,128)(2,1)S(1)}, u32[]{:S(2)}, u32[]{:S(2)}) async-start(bf16[2,4,256,96]{2,3,0,1:T(8,128)(2,1)} %copy.83), calls=%async_computation.2 | async-start | bytes 786432 | tf_op jit(solution)/shard_map/all_to_all | solution.py:385
  108.9 39.2 %shard_map.113 = bf16[2,2048,96]{2,1,0:T(8,128)(2,1)} custom-call(s32[1]{0:T(128)} %copy.99.len_ref, bf16[2,2048,96]{2,1,0:T(8,128)(2,1)} %pad_maximum_fusion.q_ref, bf16[4,2,512,96]{3,2,1,0:T(8,128)(2,1)} %get-tuple-element.7.kc_ref, bf16[4,2,512,96]{3,2,1,0:T(8,128)(2,1)} %get-tuple-element.8.vc_ref, bf16[2,1024,96]{2,1,0:T(8,128)(2,1)} %pad_maximum_fusion.1.kn_ref, ...), custom_call_target="tpu_custom_call" | custom-call | flops 4831838208 | bytes 3932160 | tf_op jit(solution)/shard_map/pallas_call | solution.py:299
  148.1 2.2 %copy.78 = bf16[2,2,4,256,96]{3,4,1,0,2:T(8,128)(2,1)} copy(bf16[2,2,4,256,96]{4,3,2,1,0:T(8,128)(2,1)} %bitcast.82) | data formatting | bytes 1572864 | tf_op jit(solution)/shard_map/reshape | solution.py:394
  150.3 4.5 %all-to-all-start = ((bf16[2,2,4,256,96]{3,4,1,0,2:T(8,128)(2,1)}), bf16[2,2,4,256,96]{3,4,1,0,2:T(8,128)(2,1)S(1)}, u32[]{:S(2)}, u32[]{:S(2)}) async-start(bf16[2,2,4,256,96]{3,4,1,0,2:T(8,128)(2,1)} %copy.78), calls=%async_computation | async-start | bytes 1572864 | tf_op jit(solution)/shard_map/all_to_all | solution.py:395
  154.8 0.9 copy.84
  155.8 0.9 copy.85
  156.7 11.3 %all-to-all-done = bf16[2,2,4,256,96]{3,4,1,0,2:T(8,128)(2,1)S(1)} async-done(((bf16[2,2,4,256,96]{3,4,1,0,2:T(8,128)(2,1)}), bf16[2,2,4,256,96]{3,4,1,0,2:T(8,128)(2,1)S(1)}, u32[]{:S(2)}, u32[]{:S(2)}) %all-to-all-start) | async-done | bytes 786464 | tf_op jit(solution)/shard_map/all_to_all | solution.py:395
  168.0 4.6 %fusion.14 = bf16[1,256,1536]{2,1,0:T(8,128)(2,1)} fusion(bf16[4,2,2,96,1536]{4,3,2,1,0:T(8,128)(2,1)} %bitcast.84, bf16[2,2,4,256,96]{3,4,1,0,2:T(8,128)(2,1)S(1)} %all-to-all-done), kind=kOutput, calls=%fused_computation.10 | convolution fusion | flops 1208352768 | bytes 6291456 | tf_op jit(solution)/shard_map/cgsth,scghn->tn/dot_general | solution.py:396
  (28 shorter events, 0.1 us)
Async XLA Ops:
  7.2 4.5 %copy-start.6 = (bf16[1,512,768]{2,1,0:T(8,128)(2,1)S(1)}, bf16[1,512,768]{2,1,0:T(8,128)(2,1)}, u32[]{:S(2)}) copy-start(bf16[1,512,768]{2,1,0:T(8,128)(2,1)} %param.11) | copy-start | bytes 2359300
  7.2 76.3 %all-gather.3.cloned.1.call-start = ((), (), s32[]{:S(2)}) async-start(), calls=%async_computation.3 | async-start | bytes 3932160 | tf_op jit(solution)/shard_map/all_gather | solution.py:334
  11.6 1.7 copy-start.7
  11.6 156.4 %all-gather.5.cloned.1.call-start = ((), (), s32[]{:S(2)}) async-start(), calls=%async_computation.4 | async-start | bytes 5898240 | tf_op jit(solution)/shard_map/all_gather | solution.py:350
  13.3 1.7 copy-start.8
  13.3 1.7 copy-start.9
  13.3 1.7 copy-start.10
  13.3 1.7 copy-start.11
  76.8 5.0 %copy-start = (bf16[1536,384]{1,0:T(8,128)(2,1)S(1)}, bf16[1536,384]{1,0:T(8,128)(2,1)}, u32[]{:S(2)}) copy-start(bf16[1536,384]{1,0:T(8,128)(2,1)} %get-tuple-element.20) | copy-start | bytes 3538948
  79.8 3.5 %copy-start.2 = (bf16[1536,192]{1,0:T(8,128)(2,1)S(1)}, bf16[1536,192]{1,0:T(8,128)(2,1)}, u32[]{:S(2)}) copy-start(bf16[1536,192]{1,0:T(8,128)(2,1)} %get-tuple-element.18) | copy-start | bytes 1769476
  83.5 3.1 %copy-start.4 = (f32[1024,48]{1,0:T(8,128)S(1)}, f32[1024,48]{1,0:T(8,128)}, u32[]{:S(2)}) copy-start(f32[1024,48]{1,0:T(8,128)} %copy.75) | copy-start | bytes 589828
  88.3 16.9 %all-to-all-start.1 = ((bf16[2,4,256,96]{2,3,0,1:T(8,128)(2,1)}), bf16[2,4,256,96]{2,3,0,1:T(8,128)(2,1)S(1)}, u32[]{:S(2)}, u32[]{:S(2)}) async-start(bf16[2,4,256,96]{2,3,0,1:T(8,128)(2,1)} %pad_maximum_fusion.2), calls=%async_computation.1 | async-start | bytes 786432 | tf_op jit(solution)/shard_map/all_to_all | solution.py:385
  91.8 4.8 %copy-start.1 = (bf16[1024,1536]{1,0:T(8,128)(2,1)S(1)}, bf16[1024,1536]{1,0:T(8,128)(2,1)}, u32[]{:S(2)}) copy-start(bf16[1024,1536]{1,0:T(8,128)(2,1)} %all-gather.3.cloned.1.call-done) | copy-start | bytes 9437188
  97.8 1.6 copy-start.5
  100.1 5.1 %copy-start.3 = (bf16[2,96,1024]{1,2,0:T(8,128)(2,1)}, bf16[2,96,1024]{1,2,0:T(8,128)(2,1)S(1)}, u32[]{:S(2)}) copy-start(bf16[2,96,1024]{1,2,0:T(8,128)(2,1)S(1)} %copy.77) | copy-start | bytes 1179652
  105.2 45.1 %all-to-all-start.2 = ((bf16[2,4,256,96]{2,3,0,1:T(8,128)(2,1)}), bf16[2,4,256,96]{2,3,0,1:T(8,128)(2,1)S(1)}, u32[]{:S(2)}, u32[]{:S(2)}) async-start(bf16[2,4,256,96]{2,3,0,1:T(8,128)(2,1)} %copy.83), calls=%async_computation.2 | async-start | bytes 786432 | tf_op jit(solution)/shard_map/all_to_all | solution.py:385
  150.3 17.7 %all-to-all-start = ((bf16[2,2,4,256,96]{3,4,1,0,2:T(8,128)(2,1)}), bf16[2,2,4,256,96]{3,4,1,0,2:T(8,128)(2,1)S(1)}, u32[]{:S(2)}, u32[]{:S(2)}) async-start(bf16[2,2,4,256,96]{3,4,1,0,2:T(8,128)(2,1)} %copy.78), calls=%async_computation | async-start | bytes 1572864 | tf_op jit(solution)/shard_map/all_to_all | solution.py:395
Sparse Core Ops, SparseCore 0:
  11.8 54.2 all-gather.2
  75.4 51.7 all-gather.4

commit v13 on v9

--- a/solution.py
+++ b/solution.py
@@ -212,11 +212,22 @@
         ],
         compiler_params=pltpu.CompilerParams(collective_id=0, has_side_effects=True),
     )(piece, keys_send, values_send)
-    x_count = planes // Y_RUN
-    ordered = jnp.transpose(
-        gathered.reshape(runs, x_count, Y_RUN, rows, width), (1, 0, 2, 3, 4)
-    )
-    return ordered.reshape(count * rows, width), keys_old, values_old
+    return gathered.reshape(count * rows, width), keys_old, values_old
+
+
+def req_order(block, count, piece_rows):
+    runs = min(Z_RUN, count // Y_RUN)
+    x_count = count // (runs * Y_RUN)
+    shaped = block.reshape(runs, x_count, Y_RUN, piece_rows, block.shape[1])
+    return jnp.transpose(shaped, (1, 0, 2, 3, 4)).reshape(block.shape)
+
+
+def gathered_order(normed, count, piece_rows):
+    runs = min(Z_RUN, count // Y_RUN)
+    x_count = count // (runs * Y_RUN)
+    rows = normed.shape[0]
+    shaped = normed.reshape(rows, x_count, runs, Y_RUN, piece_rows)
+    return jnp.transpose(shaped, (0, 2, 1, 3, 4)).reshape(rows, -1)
 
 
 BLOCK_Q = 512
@@ -318,6 +329,7 @@
     kv_heads_here = k_cols // HD
 
     normed = rms_norm(hidden[0].astype(jnp.float32), norm_gain)
+    normed = gathered_order(normed, lax.axis_size("req"), w_query.shape[0])
     normed_all = lax.all_gather(normed, "kv", axis=0, tiled=True)
 
     pieces = jnp.concatenate([w_query, w_key, w_value, w_out], axis=1)
@@ -332,7 +344,7 @@
     wq = cols[:, :q_cols]
     wk = cols[:, q_cols:q_cols + k_cols]
     wv = cols[:, q_cols + k_cols:q_cols + k_cols + v_cols]
-    wo = cols[:, q_cols + k_cols + v_cols:]
+    wo = req_order(cols[:, q_cols + k_cols + v_cols:], lax.axis_size("req"), w_query.shape[0])
 
     wo_full = lax.all_gather(wo, "kv", axis=1, tiled=True)
 

time: 180 us -> 176 us (0.978)
  the two profiles are of different devices: /device:TPU:1 before, /device:TPU:10 now
where the time goes in v13:
time: 176 us
  Pallas kernels  93.9 us (53%)
  local copies, waits for them, and re-layouts  22.3 us (13%)
  between operations  15 us (9%)
  waiting for transfers between devices  13.9 us (8%)
  matrix products  12.7 us (7%)
  starting transfers between devices  11.7 us (7%)
  other arithmetic  6.18 us (4%)
    pallas_call x1, Pallas kernels, gather_req(): pl.pallas_call(functools.partial(plane_ring_kernel, planes, runs), out_sh...  56.2 us
    pallas_call x1, Pallas kernels, flash_attention(): pl.pallas_call(functools.partial(flash_kernel, tokens, scale), out_shape=...  37.7 us
    all_to_all x1, waiting for transfers between devices, body(): got = lax.all_to_all(parts, 'kv', split_axis=2, concat_axis=2, tiled=True)  11.3 us
    all_to_all x2, starting transfers between devices, to_tokens(): got = lax.all_to_all(parts, 'kv', split_axis=1, concat_axis=1, tiled=True)  7.11 us
    dot_general x1, matrix products, body(): jnp.einsum('cgsth,scghn->tn', got, wo_full.reshape(kv_count, kv_heads_her...  4.62 us
    all_to_all x1, starting transfers between devices, body(): got = lax.all_to_all(parts, 'kv', split_axis=2, concat_axis=2, tiled=True)  4.56 us
    unnamed x27, local copies, waits for them, and re-layouts  3.85 us
    dot_general x1, matrix products, body(): jnp.einsum('td,dcgh->cgth', normed_all, wq.reshape(width, kv_heads_here,...  3.8 us
  transfers between devices with their start and end apart: 5, of which 2 were waited for; matrix products, arithmetic and copies ran while one was open for 19% of the time, Pallas kernels for 53%

profile of v13, /device:TPU:10, one launch (start us, length us, event | category | flops | bytes accessed | tf_op | source)
XLA Modules:
  0.0 175.7 jit_solution(12970335948410677810)
XLA Ops:
  7.2 0.0 all-gather.3.cloned.1.call-start
  7.2 1.4 copy.102
  8.6 0.2 multiply_reduce_fusion
  8.9 0.1 reshape.204
  9.0 0.3 fusion.26
  9.3 0.1 copy.103
  9.4 1.2 copy.104
  10.5 0.0 all-gather.5.cloned.1.call-start
  10.6 0.3 copy.97
  10.9 1.3 copy.98
  12.2 0.3 copy.99
  12.5 1.3 copy.100
  13.9 0.7 concatenate.24.src_ref
  14.6 56.2 %shard_map.112 = (bf16[8,8,24,1152]{3,2,1,0:T(8,128)(2,1)}, bf16[4,2,512,96]{3,2,1,0:T(8,128)(2,1)}, bf16[4,2,512,96]{3,2,1,0:T(8,128)(2,1)}) custom-call(bf16[24,1152]{1,0:T(8,128)(2,1)} %concatenate.24.src_ref, bf16[4,2,512,96]{3,2,1,0:T(8,128)(2,1)} %bitcast.74, bf16[4,2,512,96]{3,2,1,0:T(8,128)(2,1)} %bitcast.76), custom_call_target="tpu_custom_call" | custom-call | tf_op jit(solution)/shard_map/pallas_call | solution.py:192
  70.8 1.9 %fusion.29 = (bf16[1536,384]{1,0:T(8,128)(2,1)S(1)}, bf16[1536,384]{1,0:T(8,128)(2,1)S(1)}) fusion(bf16[1536,1152]{1,0:T(8,128)(2,1)} %bitcast.72), kind=kLoop, calls=%fused_computation.31 | loop fusion | bytes 4718592 | tf_op jit(solution)/shard_map/slice | solution.py:344
  72.6 1.2 copy.114
  73.8 1.9 %fusion.28 = (bf16[1536,192]{1,0:T(8,128)(2,1)S(1)}, bf16[1536,192]{1,0:T(8,128)(2,1)S(1)}) fusion(bf16[1536,1152]{1,0:T(8,128)(2,1)} %bitcast.73), kind=kLoop, calls=%fused_computation.30 | loop fusion | bytes 2359296 | tf_op jit(solution)/shard_map/slice | solution.py:346
  75.7 1.1 copy.107
  77.5 0.8 multiply_cosine_fusion
  78.2 0.2 copy.109
  78.4 1.0 copy.110
  79.5 1.5 copy.101
  81.0 0.3 copy.111
  81.2 0.0 all-gather.3.cloned.1.call-done
  81.3 3.1 %fusion.20 = f32[2,1024,96]{2,1,0:T(8,128)S(1)} fusion(bf16[1536,2,96]{0,2,1:T(8,128)(2,1)} %bitcast.88, bf16[1024,1536]{1,0:T(8,128)(2,1)} %all-gather.3.cloned.1.call-done), kind=kOutput, calls=%fused_computation.14 | convolution fusion | flops 603979776 | bytes 4521984 | tf_op jit(solution)/shard_map/td,dch->cth/dot_general | solution.py:370
  84.4 0.5 subtract_convert_fusion
  84.9 0.2 copy.117
  85.1 0.2 copy.118
  85.3 0.8 pad_maximum_fusion.2
  86.0 3.5 %all-to-all-start.1 = ((bf16[2,4,256,96]{2,3,0,1:T(8,128)(2,1)}), bf16[2,4,256,96]{2,3,0,1:T(8,128)(2,1)S(1)}, u32[]{:S(2)}, u32[]{:S(2)}) async-start(bf16[2,4,256,96]{2,3,0,1:T(8,128)(2,1)} %pad_maximum_fusion.2), calls=%async_computation.1 | async-start | bytes 786432 | tf_op jit(solution)/shard_map/all_to_all | solution.py:384
  89.5 3.8 %fusion.17 = f32[2,2,1024,96]{2,3,1,0:T(8,128)S(1)} fusion(bf16[1536,2,2,96]{0,3,2,1:T(8,128)(2,1)} %bitcast.86, bf16[1024,1536]{1,0:T(8,128)(2,1)} %all-gather.3.cloned.1.call-done), kind=kOutput, calls=%fused_computation.13 | convolution fusion | flops 1207959552 | bytes 5898240 | tf_op jit(solution)/shard_map/td,dcgh->cgth/dot_general | solution.py:366
  93.3 1.0 subtract_convert_fusion.1
  94.3 1.2 fusion.23
  95.5 1.1 pad_maximum_fusion.1.kn_ref
  96.6 0.5 copy.105
  97.1 0.5 copy.106
  97.6 0.3 copy.112
  97.9 1.0 copy.119
  98.8 1.6 pad_maximum_fusion.q_ref
  100.4 2.6 %all-to-all-done.1 = bf16[2,4,256,96]{2,3,0,1:T(8,128)(2,1)S(1)} async-done(((bf16[2,4,256,96]{2,3,0,1:T(8,128)(2,1)}), bf16[2,4,256,96]{2,3,0,1:T(8,128)(2,1)S(1)}, u32[]{:S(2)}, u32[]{:S(2)}) %all-to-all-start.1) | async-done | bytes 393248 | tf_op jit(solution)/shard_map/all_to_all | solution.py:384
  103.0 3.6 %all-to-all-start.2 = ((bf16[2,4,256,96]{2,3,0,1:T(8,128)(2,1)}), bf16[2,4,256,96]{2,3,0,1:T(8,128)(2,1)S(1)}, u32[]{:S(2)}, u32[]{:S(2)}) async-start(bf16[2,4,256,96]{2,3,0,1:T(8,128)(2,1)} %copy.119), calls=%async_computation.2 | async-start | bytes 786432 | tf_op jit(solution)/shard_map/all_to_all | solution.py:384
  106.6 37.7 %shard_map.113 = bf16[2,2048,96]{2,1,0:T(8,128)(2,1)} custom-call(s32[1]{0:T(128)} %copy.135.len_ref, bf16[2,2048,96]{2,1,0:T(8,128)(2,1)} %pad_maximum_fusion.q_ref, bf16[4,2,512,96]{3,2,1,0:T(8,128)(2,1)} %get-tuple-element.7.kc_ref, bf16[4,2,512,96]{3,2,1,0:T(8,128)(2,1)} %get-tuple-element.8.vc_ref, bf16[2,1024,96]{2,1,0:T(8,128)(2,1)} %pad_maximum_fusion.1.kn_ref, ...), custom_call_target="tpu_custom_call" | custom-call | flops 4831838208 | bytes 3932160 | tf_op jit(solution)/shard_map/pallas_call | solution.py:297
  144.3 2.2 %copy.113 = bf16[2,2,4,256,96]{3,4,1,0,2:T(8,128)(2,1)} copy(bf16[2,2,4,256,96]{4,3,2,1,0:T(8,128)(2,1)} %bitcast.87) | data formatting | bytes 1572864 | tf_op jit(solution)/shard_map/reshape | solution.py:393
  146.5 4.6 %all-to-all-start = ((bf16[2,2,4,256,96]{3,4,1,0,2:T(8,128)(2,1)}), bf16[2,2,4,256,96]{3,4,1,0,2:T(8,128)(2,1)S(1)}, u32[]{:S(2)}, u32[]{:S(2)}) async-start(bf16[2,2,4,256,96]{3,4,1,0,2:T(8,128)(2,1)} %copy.113), calls=%async_computation | async-start | bytes 1572864 | tf_op jit(solution)/shard_map/all_to_all | solution.py:394
  151.1 0.9 copy.120
  152.0 0.9 copy.121
  152.9 11.3 %all-to-all-done = bf16[2,2,4,256,96]{3,4,1,0,2:T(8,128)(2,1)S(1)} async-done(((bf16[2,2,4,256,96]{3,4,1,0,2:T(8,128)(2,1)}), bf16[2,2,4,256,96]{3,4,1,0,2:T(8,128)(2,1)S(1)}, u32[]{:S(2)}, u32[]{:S(2)}) %all-to-all-start) | async-done | bytes 786464 | tf_op jit(solution)/shard_map/all_to_all | solution.py:394
  164.2 4.6 %fusion.14 = bf16[1,256,1536]{2,1,0:T(8,128)(2,1)} fusion(bf16[4,2,2,96,1536]{4,3,2,1,0:T(8,128)(2,1)} %bitcast.89, bf16[2,2,4,256,96]{3,4,1,0,2:T(8,128)(2,1)S(1)} %all-to-all-done), kind=kOutput, calls=%fused_computation.10 | convolution fusion | flops 1208352768 | bytes 6291456 | tf_op jit(solution)/shard_map/cgsth,scghn->tn/dot_general | solution.py:395
  (29 shorter events, 0.1 us)
Async XLA Ops:
  7.2 1.7 copy-start.10
  7.2 74.1 %all-gather.3.cloned.1.call-start = ((), (), s32[]{:S(2)}) async-start(), calls=%async_computation.3 | async-start | bytes 3932160 | tf_op jit(solution)/shard_map/all_gather | solution.py:333
  9.3 1.3 copy-start.4
  10.5 1.7 copy-start.5
  10.5 153.7 %all-gather.5.cloned.1.call-start = ((), (), s32[]{:S(2)}) async-start(), calls=%async_computation.4 | async-start | bytes 5898240 | tf_op jit(solution)/shard_map/all_gather | solution.py:349
  12.2 1.6 copy-start.6
  12.2 1.6 copy-start.7
  12.2 1.6 copy-start.8
  12.2 1.6 copy-start.9
  81.3 3.1 %copy-start.2 = (f32[1024,48]{1,0:T(8,128)S(1)}, f32[1024,48]{1,0:T(8,128)}, u32[]{:S(2)}) copy-start(f32[1024,48]{1,0:T(8,128)} %copy.110) | copy-start | bytes 589828
  86.0 16.9 %all-to-all-start.1 = ((bf16[2,4,256,96]{2,3,0,1:T(8,128)(2,1)}), bf16[2,4,256,96]{2,3,0,1:T(8,128)(2,1)S(1)}, u32[]{:S(2)}, u32[]{:S(2)}) async-start(bf16[2,4,256,96]{2,3,0,1:T(8,128)(2,1)} %pad_maximum_fusion.2), calls=%async_computation.1 | async-start | bytes 786432 | tf_op jit(solution)/shard_map/all_to_all | solution.py:384
  89.5 4.8 %copy-start = (bf16[1024,1536]{1,0:T(8,128)(2,1)S(1)}, bf16[1024,1536]{1,0:T(8,128)(2,1)}, u32[]{:S(2)}) copy-start(bf16[1024,1536]{1,0:T(8,128)(2,1)} %all-gather.3.cloned.1.call-done) | copy-start | bytes 9437188
  95.5 1.6 copy-start.3
  97.9 5.1 %copy-start.1 = (bf16[2,96,1024]{1,2,0:T(8,128)(2,1)}, bf16[2,96,1024]{1,2,0:T(8,128)(2,1)S(1)}, u32[]{:S(2)}) copy-start(bf16[2,96,1024]{1,2,0:T(8,128)(2,1)S(1)} %copy.112) | copy-start | bytes 1179652
  103.0 43.6 %all-to-all-start.2 = ((bf16[2,4,256,96]{2,3,0,1:T(8,128)(2,1)}), bf16[2,4,256,96]{2,3,0,1:T(8,128)(2,1)S(1)}, u32[]{:S(2)}, u32[]{:S(2)}) async-start(bf16[2,4,256,96]{2,3,0,1:T(8,128)(2,1)} %copy.119), calls=%async_computation.2 | async-start | bytes 786432 | tf_op jit(solution)/shard_map/all_to_all | solution.py:384
  146.5 17.7 %all-to-all-start = ((bf16[2,2,4,256,96]{3,4,1,0,2:T(8,128)(2,1)}), bf16[2,2,4,256,96]{3,4,1,0,2:T(8,128)(2,1)S(1)}, u32[]{:S(2)}, u32[]{:S(2)}) async-start(bf16[2,2,4,256,96]{3,4,1,0,2:T(8,128)(2,1)} %copy.113), calls=%async_computation | async-start | bytes 1572864 | tf_op jit(solution)/shard_map/all_to_all | solution.py:394
Sparse Core Ops, SparseCore 0:
  10.7 52.8 all-gather.2
  74.0 50.1 all-gather.4

commit v14 on v13

--- a/solution.py
+++ b/solution.py
@@ -128,13 +128,19 @@
         part = out_ref.at[z_block, pl.ds(h * share, share)]
         return remote(part, part, send.at[k, h], recv.at[k, h], (ring_peer(z_to), kv))
 
+    if split == 2:
+        right_of = (right_hops, left_hops)
+        left_of = (left_hops, right_hops)
+    else:
+        right_of = (right_hops,)
+        left_of = (left_hops,)
     sent = []
     for h in range(split):
-        if right_hops > 0:
+        if right_of[h] > 0:
             c = ring_copy(z_me, h, r_send, r_recv, 0, z_right)
             c.start()
             sent.append(c)
-        if left_hops > 0:
+        if left_of[h] > 0:
             c = ring_copy(z_me, h, l_send, l_recv, 0, z_left)
             c.start()
             sent.append(c)
@@ -147,19 +153,19 @@
         return carry
 
     lax.fori_loop(1, kv_count, send_kv, 0)
-    for k in range(1, max(right_hops, left_hops) + 1):
+    for k in range(1, max(right_of + left_of) + 1):
         for h in range(split):
-            if k <= right_hops:
+            if k <= right_of[h]:
                 z_from = lax.rem(z_me + runs - k, runs)
                 ring_copy(z_from, h, r_send, r_recv, k - 1, z_right).wait_recv()
-                if k < right_hops:
+                if k < right_of[h]:
                     c = ring_copy(z_from, h, r_send, r_recv, k, z_right)
                     c.start()
                     sent.append(c)
-            if k <= left_hops:
+            if k <= left_of[h]:
                 z_from = lax.rem(z_me + k, runs)
                 ring_copy(z_from, h, l_send, l_recv, k - 1, z_left).wait_recv()
-                if k < left_hops:
+                if k < left_of[h]:
                     c = ring_copy(z_from, h, l_send, l_recv, k, z_left)
                     c.start()
                     sent.append(c)

time: 176 us -> 174 us (0.989)
  the two profiles are of different devices: /device:TPU:10 before, /device:TPU:72 now
where the time goes in v14:
time: 174 us; the launch traced here: 173 us
  Pallas kernels  89.9 us (52%)
  local copies, waits for them, and re-layouts  22.3 us (13%)
  between operations  15 us (9%)
  waiting for transfers between devices  13.8 us (8%)
  matrix products  12.9 us (7%)
  starting transfers between devices  12.5 us (7%)
  other arithmetic  6.18 us (4%)
    pallas_call x1, Pallas kernels, gather_req(): pl.pallas_call(functools.partial(plane_ring_kernel, planes, runs), out_sh...  52.3 us
    pallas_call x1, Pallas kernels, flash_attention(): pl.pallas_call(functools.partial(flash_kernel, tokens, scale), out_shape=...  37.7 us
    all_to_all x1, waiting for transfers between devices, body(): got = lax.all_to_all(parts, 'kv', split_axis=2, concat_axis=2, tiled=True)  11.3 us
    all_to_all x2, starting transfers between devices, to_tokens(): got = lax.all_to_all(parts, 'kv', split_axis=1, concat_axis=1, tiled=True)  7.81 us
    all_to_all x1, starting transfers between devices, body(): got = lax.all_to_all(parts, 'kv', split_axis=2, concat_axis=2, tiled=True)  4.63 us
    dot_general x1, matrix products, body(): jnp.einsum('cgsth,scghn->tn', got, wo_full.reshape(kv_count, kv_heads_her...  4.62 us
    dot_general x1, matrix products, body(): jnp.einsum('td,dcgh->cgth', normed_all, wq.reshape(width, kv_heads_here,...  4 us
    unnamed x27, local copies, waits for them, and re-layouts  3.85 us
  transfers between devices with their start and end apart: 5, of which 2 were waited for; matrix products, arithmetic and copies ran while one was open for 19% of the time, Pallas kernels for 52%

profile of v14, /device:TPU:72, one launch (start us, length us, event | category | flops | bytes accessed | tf_op | source)
XLA Modules:
  0.0 172.6 jit_solution(7932076711051389922)
XLA Ops:
  7.2 0.0 all-gather.3.cloned.1.call-start
  7.2 1.4 copy.102
  8.6 0.2 multiply_reduce_fusion
  8.9 0.1 reshape.204
  9.0 0.3 fusion.26
  9.3 0.1 copy.103
  9.4 1.2 copy.104
  10.5 0.0 all-gather.5.cloned.1.call-start
  10.6 0.3 copy.97
  10.9 1.3 copy.98
  12.2 0.3 copy.99
  12.5 1.3 copy.100
  13.9 0.7 concatenate.24.src_ref
  14.6 52.3 %shard_map.112 = (bf16[8,8,24,1152]{3,2,1,0:T(8,128)(2,1)}, bf16[4,2,512,96]{3,2,1,0:T(8,128)(2,1)}, bf16[4,2,512,96]{3,2,1,0:T(8,128)(2,1)}) custom-call(bf16[24,1152]{1,0:T(8,128)(2,1)} %concatenate.24.src_ref, bf16[4,2,512,96]{3,2,1,0:T(8,128)(2,1)} %bitcast.74, bf16[4,2,512,96]{3,2,1,0:T(8,128)(2,1)} %bitcast.76), custom_call_target="tpu_custom_call" | custom-call | tf_op jit(solution)/shard_map/pallas_call | solution.py:198
  66.8 1.9 %fusion.29 = (bf16[1536,384]{1,0:T(8,128)(2,1)S(1)}, bf16[1536,384]{1,0:T(8,128)(2,1)S(1)}) fusion(bf16[1536,1152]{1,0:T(8,128)(2,1)} %bitcast.72), kind=kLoop, calls=%fused_computation.31 | loop fusion | bytes 4718592 | tf_op jit(solution)/shard_map/slice | solution.py:350
  68.7 1.2 copy.114
  69.9 1.9 %fusion.28 = (bf16[1536,192]{1,0:T(8,128)(2,1)S(1)}, bf16[1536,192]{1,0:T(8,128)(2,1)S(1)}) fusion(bf16[1536,1152]{1,0:T(8,128)(2,1)} %bitcast.73), kind=kLoop, calls=%fused_computation.30 | loop fusion | bytes 2359296 | tf_op jit(solution)/shard_map/slice | solution.py:352
  71.8 1.1 copy.107
  73.5 0.8 multiply_cosine_fusion
  74.3 0.2 copy.109
  74.5 1.0 copy.110
  75.5 1.5 copy.101
  77.0 0.3 copy.111
  77.3 0.0 all-gather.3.cloned.1.call-done
  77.3 3.1 %fusion.20 = f32[2,1024,96]{2,1,0:T(8,128)S(1)} fusion(bf16[1536,2,96]{0,2,1:T(8,128)(2,1)} %bitcast.88, bf16[1024,1536]{1,0:T(8,128)(2,1)} %all-gather.3.cloned.1.call-done), kind=kOutput, calls=%fused_computation.14 | convolution fusion | flops 603979776 | bytes 4521984 | tf_op jit(solution)/shard_map/td,dch->cth/dot_general | solution.py:376
  80.5 0.5 subtract_convert_fusion
  81.0 0.2 copy.117
  81.2 0.2 copy.118
  81.3 0.8 pad_maximum_fusion.2
  82.1 4.2 %all-to-all-start.1 = ((bf16[2,4,256,96]{2,3,0,1:T(8,128)(2,1)}), bf16[2,4,256,96]{2,3,0,1:T(8,128)(2,1)S(1)}, u32[]{:S(2)}, u32[]{:S(2)}) async-start(bf16[2,4,256,96]{2,3,0,1:T(8,128)(2,1)} %pad_maximum_fusion.2), calls=%async_computation.1 | async-start | bytes 786432 | tf_op jit(solution)/shard_map/all_to_all | solution.py:390
  86.3 4.0 %fusion.17 = f32[2,2,1024,96]{2,3,1,0:T(8,128)S(1)} fusion(bf16[1536,2,2,96]{0,3,2,1:T(8,128)(2,1)} %bitcast.86, bf16[1024,1536]{1,0:T(8,128)(2,1)} %all-gather.3.cloned.1.call-done), kind=kOutput, calls=%fused_computation.13 | convolution fusion | flops 1207959552 | bytes 5898240 | tf_op jit(solution)/shard_map/td,dcgh->cgth/dot_general | solution.py:372
  90.3 1.0 subtract_convert_fusion.1
  91.3 1.2 fusion.23
  92.5 1.1 pad_maximum_fusion.1.kn_ref
  93.6 0.5 copy.105
  94.1 0.5 copy.106
  94.6 0.3 copy.112
  94.8 1.0 copy.119
  95.8 1.6 pad_maximum_fusion.q_ref
  97.4 2.4 %all-to-all-done.1 = bf16[2,4,256,96]{2,3,0,1:T(8,128)(2,1)S(1)} async-done(((bf16[2,4,256,96]{2,3,0,1:T(8,128)(2,1)}), bf16[2,4,256,96]{2,3,0,1:T(8,128)(2,1)S(1)}, u32[]{:S(2)}, u32[]{:S(2)}) %all-to-all-start.1) | async-done | bytes 393248 | tf_op jit(solution)/shard_map/all_to_all | solution.py:390
  99.8 3.6 %all-to-all-start.2 = ((bf16[2,4,256,96]{2,3,0,1:T(8,128)(2,1)}), bf16[2,4,256,96]{2,3,0,1:T(8,128)(2,1)S(1)}, u32[]{:S(2)}, u32[]{:S(2)}) async-start(bf16[2,4,256,96]{2,3,0,1:T(8,128)(2,1)} %copy.119), calls=%async_computation.2 | async-start | bytes 786432 | tf_op jit(solution)/shard_map/all_to_all | solution.py:390
  103.4 37.7 %shard_map.113 = bf16[2,2048,96]{2,1,0:T(8,128)(2,1)} custom-call(s32[1]{0:T(128)} %copy.135.len_ref, bf16[2,2048,96]{2,1,0:T(8,128)(2,1)} %pad_maximum_fusion.q_ref, bf16[4,2,512,96]{3,2,1,0:T(8,128)(2,1)} %get-tuple-element.7.kc_ref, bf16[4,2,512,96]{3,2,1,0:T(8,128)(2,1)} %get-tuple-element.8.vc_ref, bf16[2,1024,96]{2,1,0:T(8,128)(2,1)} %pad_maximum_fusion.1.kn_ref, ...), custom_call_target="tpu_custom_call" | custom-call | flops 4831838208 | bytes 3932160 | tf_op jit(solution)/shard_map/pallas_call | solution.py:303
  141.1 2.2 %copy.113 = bf16[2,2,4,256,96]{3,4,1,0,2:T(8,128)(2,1)} copy(bf16[2,2,4,256,96]{4,3,2,1,0:T(8,128)(2,1)} %bitcast.87) | data formatting | bytes 1572864 | tf_op jit(solution)/shard_map/reshape | solution.py:399
  143.3 4.6 %all-to-all-start = ((bf16[2,2,4,256,96]{3,4,1,0,2:T(8,128)(2,1)}), bf16[2,2,4,256,96]{3,4,1,0,2:T(8,128)(2,1)S(1)}, u32[]{:S(2)}, u32[]{:S(2)}) async-start(bf16[2,2,4,256,96]{3,4,1,0,2:T(8,128)(2,1)} %copy.113), calls=%async_computation | async-start | bytes 1572864 | tf_op jit(solution)/shard_map/all_to_all | solution.py:400
  148.0 0.9 copy.120
  148.9 0.9 copy.121
  149.8 11.3 %all-to-all-done = bf16[2,2,4,256,96]{3,4,1,0,2:T(8,128)(2,1)S(1)} async-done(((bf16[2,2,4,256,96]{3,4,1,0,2:T(8,128)(2,1)}), bf16[2,2,4,256,96]{3,4,1,0,2:T(8,128)(2,1)S(1)}, u32[]{:S(2)}, u32[]{:S(2)}) %all-to-all-start) | async-done | bytes 786464 | tf_op jit(solution)/shard_map/all_to_all | solution.py:400
  161.1 4.6 %fusion.14 = bf16[1,256,1536]{2,1,0:T(8,128)(2,1)} fusion(bf16[4,2,2,96,1536]{4,3,2,1,0:T(8,128)(2,1)} %bitcast.89, bf16[2,2,4,256,96]{3,4,1,0,2:T(8,128)(2,1)S(1)} %all-to-all-done), kind=kOutput, calls=%fused_computation.10 | convolution fusion | flops 1208352768 | bytes 6291456 | tf_op jit(solution)/shard_map/cgsth,scghn->tn/dot_general | solution.py:401
  (29 shorter events, 0.1 us)
Async XLA Ops:
  7.2 1.7 copy-start.10
  7.2 70.1 %all-gather.3.cloned.1.call-start = ((), (), s32[]{:S(2)}) async-start(), calls=%async_computation.3 | async-start | bytes 3932160 | tf_op jit(solution)/shard_map/all_gather | solution.py:339
  9.3 1.3 copy-start.4
  10.5 1.7 copy-start.5
  10.5 150.6 %all-gather.5.cloned.1.call-start = ((), (), s32[]{:S(2)}) async-start(), calls=%async_computation.4 | async-start | bytes 5898240 | tf_op jit(solution)/shard_map/all_gather | solution.py:355
  12.2 1.6 copy-start.6
  12.2 1.6 copy-start.7
  12.2 1.6 copy-start.8
  12.2 1.6 copy-start.9
  77.3 3.1 %copy-start.2 = (f32[1024,48]{1,0:T(8,128)S(1)}, f32[1024,48]{1,0:T(8,128)}, u32[]{:S(2)}) copy-start(f32[1024,48]{1,0:T(8,128)} %copy.110) | copy-start | bytes 589828
  82.1 17.6 %all-to-all-start.1 = ((bf16[2,4,256,96]{2,3,0,1:T(8,128)(2,1)}), bf16[2,4,256,96]{2,3,0,1:T(8,128)(2,1)S(1)}, u32[]{:S(2)}, u32[]{:S(2)}) async-start(bf16[2,4,256,96]{2,3,0,1:T(8,128)(2,1)} %pad_maximum_fusion.2), calls=%async_computation.1 | async-start | bytes 786432 | tf_op jit(solution)/shard_map/all_to_all | solution.py:390
  86.3 5.0 %copy-start = (bf16[1024,1536]{1,0:T(8,128)(2,1)S(1)}, bf16[1024,1536]{1,0:T(8,128)(2,1)}, u32[]{:S(2)}) copy-start(bf16[1024,1536]{1,0:T(8,128)(2,1)} %all-gather.3.cloned.1.call-done) | copy-start | bytes 9437188
  92.5 1.6 copy-start.3
  94.8 4.9 %copy-start.1 = (bf16[2,96,1024]{1,2,0:T(8,128)(2,1)}, bf16[2,96,1024]{1,2,0:T(8,128)(2,1)S(1)}, u32[]{:S(2)}) copy-start(bf16[2,96,1024]{1,2,0:T(8,128)(2,1)S(1)} %copy.112) | copy-start | bytes 1179652
  99.8 43.6 %all-to-all-start.2 = ((bf16[2,4,256,96]{2,3,0,1:T(8,128)(2,1)}), bf16[2,4,256,96]{2,3,0,1:T(8,128)(2,1)S(1)}, u32[]{:S(2)}, u32[]{:S(2)}) async-start(bf16[2,4,256,96]{2,3,0,1:T(8,128)(2,1)} %copy.119), calls=%async_computation.2 | async-start | bytes 786432 | tf_op jit(solution)/shard_map/all_to_all | solution.py:390
  143.3 17.8 %all-to-all-start = ((bf16[2,2,4,256,96]{3,4,1,0,2:T(8,128)(2,1)}), bf16[2,2,4,256,96]{3,4,1,0,2:T(8,128)(2,1)S(1)}, u32[]{:S(2)}, u32[]{:S(2)}) async-start(bf16[2,2,4,256,96]{3,4,1,0,2:T(8,128)(2,1)} %copy.113), calls=%async_computation | async-start | bytes 1572864 | tf_op jit(solution)/shard_map/all_to_all | solution.py:400
Sparse Core Ops, SparseCore 0:
  10.7 53.1 all-gather.2
  70.0 53.3 all-gather.4

commit v15 on v11

--- a/solution.py
+++ b/solution.py
@@ -128,13 +128,19 @@
         part = out_ref.at[z_block, pl.ds(h * share, share)]
         return remote(part, part, send.at[k, h], recv.at[k, h], (ring_peer(z_to), kv))
 
+    if split == 2:
+        right_of = (right_hops, left_hops)
+        left_of = (left_hops, right_hops)
+    else:
+        right_of = (right_hops,)
+        left_of = (left_hops,)
     sent = []
     for h in range(split):
-        if right_hops > 0:
+        if right_of[h] > 0:
             c = ring_copy(z_me, h, r_send, r_recv, 0, z_right)
             c.start()
             sent.append(c)
-        if left_hops > 0:
+        if left_of[h] > 0:
             c = ring_copy(z_me, h, l_send, l_recv, 0, z_left)
             c.start()
             sent.append(c)
@@ -147,19 +153,19 @@
         return carry
 
     lax.fori_loop(1, kv_count, send_kv, 0)
-    for k in range(1, max(right_hops, left_hops) + 1):
+    for k in range(1, max(right_of + left_of) + 1):
         for h in range(split):
-            if k <= right_hops:
+            if k <= right_of[h]:
                 z_from = lax.rem(z_me + runs - k, runs)
                 ring_copy(z_from, h, r_send, r_recv, k - 1, z_right).wait_recv()
-                if k < right_hops:
+                if k < right_of[h]:
                     c = ring_copy(z_from, h, r_send, r_recv, k, z_right)
                     c.start()
                     sent.append(c)
-            if k <= left_hops:
+            if k <= left_of[h]:
                 z_from = lax.rem(z_me + k, runs)
                 ring_copy(z_from, h, l_send, l_recv, k - 1, z_left).wait_recv()
-                if k < left_hops:
+                if k < left_of[h]:
                     c = ring_copy(z_from, h, l_send, l_recv, k, z_left)
                     c.start()
                     sent.append(c)
@@ -212,11 +218,22 @@
         ],
         compiler_params=pltpu.CompilerParams(collective_id=0, has_side_effects=True),
     )(piece, keys_send, values_send)
-    x_count = planes // Y_RUN
-    ordered = jnp.transpose(
-        gathered.reshape(runs, x_count, Y_RUN, rows, width), (1, 0, 2, 3, 4)
-    )
-    return ordered.reshape(count * rows, width), keys_old, values_old
+    return gathered.reshape(count * rows, width), keys_old, values_old
+
+
+def req_order(block, count, piece_rows):
+    runs = min(Z_RUN, count // Y_RUN)
+    x_count = count // (runs * Y_RUN)
+    shaped = block.reshape(runs, x_count, Y_RUN, piece_rows, block.shape[1])
+    return jnp.transpose(shaped, (1, 0, 2, 3, 4)).reshape(block.shape)
+
+
+def gathered_order(normed, count, piece_rows):
+    runs = min(Z_RUN, count // Y_RUN)
+    x_count = count // (runs * Y_RUN)
+    rows = normed.shape[0]
+    shaped = normed.reshape(rows, x_count, runs, Y_RUN, piece_rows)
+    return jnp.transpose(shaped, (0, 2, 1, 3, 4)).reshape(rows, -1)
 
 
 BLOCK_Q = 512
@@ -273,7 +290,7 @@
     carry = lax.fori_loop(0, live_blocks, cache_step, carry)
     new_blocks = (first + block_q - 1) // block_n + 1
     peak, total, acc = lax.fori_loop(0, new_blocks, new_step, carry)
-    o_ref[...] = (acc / total).astype(o_ref.dtype).reshape(o_ref.shape)
+    o_ref[0] = (acc / total).astype(o_ref.dtype)
 
 
 def flash_attention(lengths, queries, keys_old, values_old, keys_new, values_new, tokens, scale):
@@ -285,12 +302,9 @@
     whole_cache = pl.BlockSpec((blocks, 1, block_k, width), lambda c, i, n: (0, c, 0, 0))
     peers, _, block_n, _ = keys_new.shape
     whole_new = pl.BlockSpec((peers, 1, block_n, width), lambda c, i, n: (0, c, 0, 0))
-    per_q = block_q // block_n
-    halves = tokens // block_q
-    groups = rows // tokens
     return pl.pallas_call(
         functools.partial(flash_kernel, tokens, scale),
-        out_shape=jax.ShapeDtypeStruct((peers, heads, groups, block_n, width), jnp.bfloat16),
+        out_shape=jax.ShapeDtypeStruct((heads, rows, width), jnp.bfloat16),
         grid_spec=pltpu.PrefetchScalarGridSpec(
             num_scalar_prefetch=1,
             grid=grid,
@@ -298,10 +312,7 @@
                 pl.BlockSpec((1, block_q, width), lambda c, i, n: (c, i, 0)),
                 whole_cache, whole_cache, whole_new, whole_new,
             ],
-            out_specs=pl.BlockSpec(
-                (per_q, 1, 1, block_n, width),
-                lambda c, i, n: (lax.rem(i, halves), c, i // halves, 0, 0),
-            ),
+            out_specs=pl.BlockSpec((1, block_q, width), lambda c, i, n: (c, i, 0)),
         ),
         cost_estimate=pl.CostEstimate(
             flops=4 * heads * rows * (slots + tokens) * width,
@@ -311,11 +322,11 @@
     )(lengths, queries, keys_old, values_old, keys_new, values_new)
 
 
-def exchange_kernel(k_ref, v_ref, c_ref, k_out, v_out, c_out, send_sem, recv_sem, local_sem):
+def exchange_kernel(k_ref, v_ref, k_out, v_out, send_sem, recv_sem, local_sem):
     me = lax.axis_index("kv")
     req = lax.axis_index("req")
     count = lax.axis_size("kv")
-    arrays = ((k_ref, k_out), (v_ref, v_out), (c_ref, c_out))
+    arrays = ((k_ref, k_out), (v_ref, v_out))
     barrier = pltpu.get_barrier_semaphore()
 
     def greet(step, carry):
@@ -355,21 +366,21 @@
         c.wait()
 
 
-def exchange_kv(keys, values, context):
+def exchange_kv(keys, values):
     count = lax.axis_size("kv")
     anywhere = pl.BlockSpec(memory_space=pl.ANY)
     return pl.pallas_call(
         exchange_kernel,
-        out_shape=tuple(jax.ShapeDtypeStruct(a.shape, a.dtype) for a in (keys, values, context)),
-        in_specs=[anywhere, anywhere, anywhere],
-        out_specs=(anywhere, anywhere, anywhere),
+        out_shape=tuple(jax.ShapeDtypeStruct(a.shape, a.dtype) for a in (keys, values)),
+        in_specs=[anywhere, anywhere],
+        out_specs=(anywhere, anywhere),
         scratch_shapes=[
-            pltpu.SemaphoreType.DMA((3, count - 1)),
-            pltpu.SemaphoreType.DMA((3, count - 1)),
-            pltpu.SemaphoreType.DMA((3,)),
+            pltpu.SemaphoreType.DMA((2, count - 1)),
+            pltpu.SemaphoreType.DMA((2, count - 1)),
+            pltpu.SemaphoreType.DMA((2,)),
         ],
         compiler_params=pltpu.CompilerParams(collective_id=1, has_side_effects=True),
-    )(keys, values, context)
+    )(keys, values)
 
 
 def body(hidden, lengths, key_cache, value_cache, norm_gain, w_query, w_key, w_value, w_out):
@@ -387,6 +398,7 @@
     kv_heads_here = k_cols // HD
 
     normed = rms_norm(hidden[0].astype(jnp.float32), norm_gain)
+    normed = gathered_order(normed, lax.axis_size("req"), w_query.shape[0])
     normed_all = lax.all_gather(normed, "kv", axis=0, tiled=True)
 
     pieces = jnp.concatenate([w_query, w_key, w_value, w_out], axis=1)
@@ -401,7 +413,7 @@
     wq = cols[:, :q_cols]
     wk = cols[:, q_cols:q_cols + k_cols]
     wv = cols[:, q_cols + k_cols:q_cols + k_cols + v_cols]
-    wo = cols[:, q_cols + k_cols + v_cols:]
+    wo = req_order(cols[:, q_cols + k_cols + v_cols:], lax.axis_size("req"), w_query.shape[0])
 
     wo_full = lax.all_gather(wo, "kv", axis=1, tiled=True)
 
@@ -444,18 +456,21 @@
     ).astype(jnp.bfloat16)
     values_new = proj_v.astype(jnp.bfloat16)
 
+    keys_got, values_got = exchange_kv(keys_new, values_new)
+
+    def to_tokens(values):
+        return jnp.transpose(values, (2, 0, 1, 3)).reshape(rows_here, kv_count * kv_heads_here * HD)
+
+    new_keys = to_tokens(keys_got)
+    new_values = to_tokens(values_got)
+
     contexts = flash_attention(
         lengths, query_heads, keys_old, values_old, keys_new, values_new, appended, scale,
     )
-    keys_got, values_got, got = exchange_kv(keys_new, values_new, contexts)
-
-    def to_tokens(values):
-        return jnp.transpose(values, (2, 0, 1, 3)).reshape(rows_here, kv_count * kv_heads_here * HD)
-
-    new_keys = to_tokens(keys_got)
-    new_values = to_tokens(values_got)
+    parts = contexts.reshape(kv_heads_here, groups, kv_count, rows_here, HD)
+    got = lax.all_to_all(parts, "kv", split_axis=2, concat_axis=2, tiled=True)
     attended = jnp.einsum(
-        "scgth,scghn->tn", got,
+        "cgsth,scghn->tn", got,
         wo_full.reshape(kv_count, kv_heads_here, groups, HD, wo_full.shape[1]),
         preferred_element_type=jnp.float32,
     ).astype(jnp.bfloat16)

time: 191 us -> 188 us (0.984)
  the two profiles are of different devices: /device:TPU:11 before, /device:TPU:9 now
where the time goes in v15:
time: 188 us; the launch traced here: 187 us
  Pallas kernels  122 us (65%)
  local copies, waits for them, and re-layouts  24 us (13%)
  matrix products  15 us (8%)
  between operations  14.9 us (8%)
  other arithmetic  8.4 us (4%)
  starting transfers between devices  3.56 us (2%)
    pallas_call x1, Pallas kernels, gather_req(): pl.pallas_call(functools.partial(plane_ring_kernel, planes, runs), out_sh...  55.6 us
    pallas_call x1, Pallas kernels, flash_attention(): pl.pallas_call(functools.partial(flash_kernel, tokens, scale), out_shape=...  42.5 us
    pallas_call x1, Pallas kernels, exchange_kv(): pl.pallas_call(exchange_kernel, out_shape=tuple((jax.ShapeDtypeStruct(a.s...  23.5 us
    dot_general x1, matrix products, body(): jnp.einsum('cgsth,scghn->tn', got, wo_full.reshape(kv_count, kv_heads_her...  4.62 us
    dot_general x1, matrix products, body(): jnp.einsum('std,dch->scth', normed_blocks, wv.reshape(width, kv_heads_her...  3.95 us
    unnamed x21, local copies, waits for them, and re-layouts  3.84 us
  transfers between devices with their start and end apart: 3, of which 0 were waited for; matrix products, arithmetic and copies ran while one was open for 21% of the time, Pallas kernels for 65%

profile of v15, /device:TPU:9, one launch (start us, length us, event | category | flops | bytes accessed | tf_op | source)
XLA Modules:
  0.0 187.5 jit_solution(14015638163164421606)
XLA Ops:
  7.2 0.0 copy-start.7
  7.2 0.0 all-gather.3.cloned.1.call-start
  7.2 1.4 copy.89
  8.6 0.2 multiply_reduce_fusion
  8.9 0.1 reshape.174
  9.0 0.3 fusion.16
  9.3 0.0 copy-start.1
  9.3 0.1 copy.90
  9.4 1.2 copy.91
  10.5 0.0 all-gather.3.cloned.1.call-update
  10.5 0.0 all-gather.5.cloned.1.call-start
  10.6 0.0 copy-done.1
  10.6 0.3 copy.84
  10.9 1.3 copy.85
  12.2 0.0 copy-start.6
  12.2 0.3 copy.86
  12.5 1.3 copy.87
  13.8 0.7 concatenate.16.src_ref
  14.5 55.6 %shard_map.112 = (bf16[8,8,24,1152]{3,2,1,0:T(8,128)(2,1)}, bf16[4,2,512,96]{3,2,1,0:T(8,128)(2,1)}, bf16[4,2,512,96]{3,2,1,0:T(8,128)(2,1)}) custom-call(bf16[24,1152]{1,0:T(8,128)(2,1)} %concatenate.16.src_ref, bf16[4,2,512,96]{3,2,1,0:T(8,128)(2,1)} %bitcast.73, bf16[4,2,512,96]{3,2,1,0:T(8,128)(2,1)} %bitcast.74), custom_call_target="tpu_custom_call" | custom-call | tf_op jit(solution)/shard_map/pallas_call | solution.py:198
  70.1 1.9 %fusion.19 = (bf16[1536,384]{1,0:T(8,128)(2,1)S(1)}, bf16[1536,384]{1,0:T(8,128)(2,1)S(1)}) fusion(bf16[1536,1152]{1,0:T(8,128)(2,1)} %bitcast.69), kind=kLoop, calls=%fused_computation.29 | loop fusion | bytes 4718592 | tf_op jit(solution)/shard_map/slice | solution.py:413
  72.0 1.2 copy.99
  73.1 0.0 all-gather.5.cloned.1.call-update
  73.2 1.9 fusion.18
  75.0 1.1 copy.94
  76.8 0.6 copy.88
  77.4 0.3 copy.96
  77.7 0.8 multiply_cosine_fusion.1
  78.5 2.9 %multiply_cosine_fusion = (f32[4,256,48]{2,1,0:T(8,128)S(1)}, f32[4,256,48]{2,1,0:T(8,128)}) fusion(f32[48]{0:T(128)S(1)} %negate_power_fusion, f32[4,256]{1,0:T(4,128)S(1)} %add_convert_fusion.2), kind=kLoop, calls=%fused_computation.20 | loop fusion | flops 49152 | bytes 397504 | tf_op jit(solution)/shard_map/cos | solution.py:424
  81.4 3.3 %fusion.13 = f32[2,2,1024,96]{2,3,1,0:T(8,128)S(1)} fusion(bf16[1536,2,2,96]{0,3,2,1:T(8,128)(2,1)S(1)} %bitcast.85, bf16[1024,1536]{1,0:T(8,128)(2,1)} %all-gather.3.cloned.1.call-done), kind=kOutput, calls=%fused_computation.9 | convolution fusion | flops 1207959552 | bytes 5898240 | tf_op jit(solution)/shard_map/td,dcgh->cgth/dot_general | solution.py:435
  84.7 1.0 subtract_convert_fusion.1
  85.7 0.5 copy.92
  86.2 1.5 copy.93
  87.7 4.0 %convolution_convert_fusion = bf16[2,96,4,256]{3,1,2,0:T(8,128)(2,1)} fusion(bf16[1536,2,96,1]{0,2,3,1:T(8,128)(2,1)S(1)} %bitcast.80, bf16[4,256,1536,1]{2,1,0,3:T(8,128)(2,1)} %bitcast.78), kind=kOutput, calls=%fused_computation.11 | convolution fusion | flops 604176384 | bytes 4128768 | tf_op jit(solution)/shard_map/std,dch->scth/dot_general | solution.py:444
  91.7 2.0 %copy.97 = bf16[2,96,4,256]{1,3,0,2:T(8,128)(2,1)} copy(bf16[2,96,4,256]{3,1,2,0:T(8,128)(2,1)} %convolution_convert_fusion) | data formatting | bytes 786432 | tf_op jit(solution)/shard_map/convert_element_type | solution.py:457
  93.7 3.1 %convolution_bitcast_fusion = f32[4,2,256,96]{3,2,1,0:T(8,128)S(1)} fusion(bf16[1536,2,96,1]{0,2,1,3:T(8,128)(2,1)} %bitcast.87, bf16[4,256,1536,1]{2,1,3,0:T(8,128)(2,1)} %bitcast.79), kind=kOutput, calls=%fused_computation.10 | convolution fusion | flops 603979776 | bytes 4521984 | tf_op jit(solution)/shard_map/std,dch->scth/dot_general | solution.py:440
  96.8 0.5 subtract_convert_fusion
  97.3 1.1 pad_maximum_fusion.1.kn_ref.k_ref
  98.4 1.6 pad_maximum_fusion.q_ref
  100.0 42.5 %shard_map.113 = bf16[2,2048,96]{2,1,0:T(8,128)(2,1)} custom-call(s32[1]{0:T(128)} %copy.121.len_ref, bf16[2,2048,96]{2,1,0:T(8,128)(2,1)} %pad_maximum_fusion.q_ref, bf16[4,2,512,96]{3,2,1,0:T(8,128)(2,1)} %get-tuple-element.9.kc_ref, bf16[4,2,512,96]{3,2,1,0:T(8,128)(2,1)} %get-tuple-element.10.vc_ref, ...), custom_call_target="tpu_custom_call" | custom-call | flops 4831838208 | bytes 3932160 | tf_op jit(solution)/shard_map/pallas_call | solution.py:305
  142.5 2.2 %copy.98 = bf16[2,2,4,256,96]{3,4,1,0,2:T(8,128)(2,1)} copy(bf16[2,2,4,256,96]{4,3,2,1,0:T(8,128)(2,1)} %bitcast.86) | data formatting | bytes 1572864 | tf_op jit(solution)/shard_map/reshape | solution.py:470
  144.7 3.5 %all-to-all-start = ((bf16[2,2,4,256,96]{3,4,1,0,2:T(8,128)(2,1)}), bf16[2,2,4,256,96]{3,4,1,0,2:T(8,128)(2,1)S(1)}, u32[]{:S(2)}, u32[]{:S(2)}) async-start(bf16[2,2,4,256,96]{3,4,1,0,2:T(8,128)(2,1)} %copy.98), calls=%async_computation | async-start | bytes 1572864 | tf_op jit(solution)/shard_map/all_to_all | solution.py:471
  148.2 23.5 %shard_map.114 = (bf16[4,2,256,96]{3,2,1,0:T(8,128)(2,1)}, bf16[4,2,256,96]{3,2,1,0:T(8,128)(2,1)}) custom-call(bf16[4,2,256,96]{3,2,1,0:T(8,128)(2,1)} %pad_maximum_fusion.1.kn_ref.k_ref, bf16[4,2,256,96]{3,2,1,0:T(8,128)(2,1)} %bitcast.82), custom_call_target="tpu_custom_call" | custom-call | tf_op jit(solution)/shard_map/pallas_call | solution.py:372
  171.7 1.2 copy.102
  172.9 0.9 copy.104
  173.9 1.2 copy.103
  175.1 0.9 copy.105
  176.0 0.0 all-to-all-done
  176.0 4.6 %fusion.10 = bf16[1,256,1536]{2,1,0:T(8,128)(2,1)} fusion(bf16[4,2,2,96,1536]{4,3,2,1,0:T(8,128)(2,1)} %bitcast.90, bf16[2,2,4,256,96]{3,4,1,0,2:T(8,128)(2,1)S(1)} %all-to-all-done), kind=kOutput, calls=%fused_computation.6 | convolution fusion | flops 1208352768 | bytes 6291456 | tf_op jit(solution)/shard_map/cgsth,scghn->tn/dot_general | solution.py:472
  (18 shorter events, 0.1 us)
Async XLA Ops:
  7.2 1.7 copy-start.7
  7.2 74.2 %all-gather.3.cloned.1.call-start = ((), (), s32[]{:S(2)}) async-start(), calls=%async_computation.1 | async-start | bytes 3932160 | tf_op jit(solution)/shard_map/all_gather | solution.py:402
  9.3 1.3 copy-start.1
  10.5 1.7 copy-start.2
  10.5 165.5 %all-gather.5.cloned.1.call-start = ((), (), s32[]{:S(2)}) async-start(), calls=%async_computation.2 | async-start | bytes 5898240 | tf_op jit(solution)/shard_map/all_gather | solution.py:418
  12.2 1.6 copy-start.3
  12.2 1.6 copy-start.4
  12.2 1.6 copy-start.5
  12.2 1.6 copy-start.6
  93.7 3.1 %copy-start = (f32[4,256,48]{2,1,0:T(8,128)S(1)}, f32[4,256,48]{2,1,0:T(8,128)}, u32[]{:S(2)}) copy-start(f32[4,256,48]{2,1,0:T(8,128)} %get-tuple-element.34) | copy-start | bytes 589828
  144.7 31.3 %all-to-all-start = ((bf16[2,2,4,256,96]{3,4,1,0,2:T(8,128)(2,1)}), bf16[2,2,4,256,96]{3,4,1,0,2:T(8,128)(2,1)S(1)}, u32[]{:S(2)}, u32[]{:S(2)}) async-start(bf16[2,2,4,256,96]{3,4,1,0,2:T(8,128)(2,1)} %copy.98), calls=%async_computation | async-start | bytes 1572864 | tf_op jit(solution)/shard_map/all_to_all | solution.py:471
Sparse Core Ops, SparseCore 0:
  10.7 52.8 all-gather.2
  73.3 42.8 all-gather.4

commit v16 on v14

--- a/solution.py
+++ b/solution.py
@@ -236,7 +236,7 @@
     return jnp.transpose(shaped, (0, 2, 1, 3, 4)).reshape(rows, -1)
 
 
-BLOCK_Q = 512
+BLOCK_Q = 1024
 BLOCK_K = 512
 
 

time: 174 us -> 174 us (level)
  the two profiles are of different devices: /device:TPU:72 before, /device:TPU:1 now
where the time goes in v16:
time: 174 us
  Pallas kernels  94.4 us (54%)
  local copies, waits for them, and re-layouts  22.3 us (13%)
  between operations  15 us (9%)
  matrix products  12.7 us (7%)
  starting transfers between devices  12.6 us (7%)
  waiting for transfers between devices  10.6 us (6%)
  other arithmetic  6.18 us (4%)
    pallas_call x1, Pallas kernels, gather_req(): pl.pallas_call(functools.partial(plane_ring_kernel, planes, runs), out_sh...  57.6 us
    pallas_call x1, Pallas kernels, flash_attention(): pl.pallas_call(functools.partial(flash_kernel, tokens, scale), out_shape=...  36.8 us
    all_to_all x1, waiting for transfers between devices, body(): got = lax.all_to_all(parts, 'kv', split_axis=2, concat_axis=2, tiled=True)  10.5 us
    all_to_all x2, starting transfers between devices, to_tokens(): got = lax.all_to_all(parts, 'kv', split_axis=1, concat_axis=1, tiled=True)  7.72 us
    all_to_all x1, starting transfers between devices, body(): got = lax.all_to_all(parts, 'kv', split_axis=2, concat_axis=2, tiled=True)  4.85 us
    dot_general x1, matrix products, body(): jnp.einsum('cgsth,scghn->tn', got, wo_full.reshape(kv_count, kv_heads_her...  4.62 us
    unnamed x27, local copies, waits for them, and re-layouts  3.85 us
    dot_general x1, matrix products, body(): jnp.einsum('td,dcgh->cgth', normed_all, wq.reshape(width, kv_heads_here,...  3.8 us
  transfers between devices with their start and end apart: 5, of which 2 were waited for; matrix products, arithmetic and copies ran while one was open for 19% of the time, Pallas kernels for 54%

profile of v16, /device:TPU:1, one launch (start us, length us, event | category | flops | bytes accessed | tf_op | source)
XLA Modules:
  0.0 173.8 jit_solution(1220968635006018898)
XLA Ops:
  7.2 0.0 all-gather.3.cloned.1.call-start
  7.2 1.4 copy.102
  8.6 0.2 multiply_reduce_fusion
  8.9 0.1 reshape.204
  9.0 0.3 fusion.26
  9.3 0.1 copy.103
  9.4 1.2 copy.104
  10.5 0.0 all-gather.5.cloned.1.call-start
  10.6 0.3 copy.97
  10.9 1.3 copy.98
  12.2 0.3 copy.99
  12.5 1.3 copy.100
  13.9 0.7 concatenate.24.src_ref
  14.6 57.6 %shard_map.112 = (bf16[8,8,24,1152]{3,2,1,0:T(8,128)(2,1)}, bf16[4,2,512,96]{3,2,1,0:T(8,128)(2,1)}, bf16[4,2,512,96]{3,2,1,0:T(8,128)(2,1)}) custom-call(bf16[24,1152]{1,0:T(8,128)(2,1)} %concatenate.24.src_ref, bf16[4,2,512,96]{3,2,1,0:T(8,128)(2,1)} %bitcast.74, bf16[4,2,512,96]{3,2,1,0:T(8,128)(2,1)} %bitcast.76), custom_call_target="tpu_custom_call" | custom-call | tf_op jit(solution)/shard_map/pallas_call | solution.py:198
  72.2 1.9 %fusion.29 = (bf16[1536,384]{1,0:T(8,128)(2,1)S(1)}, bf16[1536,384]{1,0:T(8,128)(2,1)S(1)}) fusion(bf16[1536,1152]{1,0:T(8,128)(2,1)} %bitcast.72), kind=kLoop, calls=%fused_computation.31 | loop fusion | bytes 4718592 | tf_op jit(solution)/shard_map/slice | solution.py:350
  74.1 1.2 copy.114
  75.3 1.9 %fusion.28 = (bf16[1536,192]{1,0:T(8,128)(2,1)S(1)}, bf16[1536,192]{1,0:T(8,128)(2,1)S(1)}) fusion(bf16[1536,1152]{1,0:T(8,128)(2,1)} %bitcast.73), kind=kLoop, calls=%fused_computation.30 | loop fusion | bytes 2359296 | tf_op jit(solution)/shard_map/slice | solution.py:352
  77.2 1.1 copy.107
  78.9 0.8 multiply_cosine_fusion
  79.7 0.2 copy.109
  79.9 1.0 copy.110
  80.9 1.5 copy.101
  82.4 0.3 copy.111
  82.7 0.0 all-gather.3.cloned.1.call-done
  82.7 3.1 %fusion.20 = f32[2,1024,96]{2,1,0:T(8,128)S(1)} fusion(bf16[1536,2,96]{0,2,1:T(8,128)(2,1)} %bitcast.88, bf16[1024,1536]{1,0:T(8,128)(2,1)} %all-gather.3.cloned.1.call-done), kind=kOutput, calls=%fused_computation.14 | convolution fusion | flops 603979776 | bytes 4521984 | tf_op jit(solution)/shard_map/td,dch->cth/dot_general | solution.py:376
  85.9 0.5 subtract_convert_fusion
  86.3 0.2 copy.117
  86.5 0.2 copy.118
  86.7 0.8 pad_maximum_fusion.2
  87.5 3.5 %all-to-all-start.1 = ((bf16[2,4,256,96]{2,3,0,1:T(8,128)(2,1)}), bf16[2,4,256,96]{2,3,0,1:T(8,128)(2,1)S(1)}, u32[]{:S(2)}, u32[]{:S(2)}) async-start(bf16[2,4,256,96]{2,3,0,1:T(8,128)(2,1)} %pad_maximum_fusion.2), calls=%async_computation.1 | async-start | bytes 786432 | tf_op jit(solution)/shard_map/all_to_all | solution.py:390
  91.0 3.8 %fusion.17 = f32[2,2,1024,96]{2,3,1,0:T(8,128)S(1)} fusion(bf16[1536,2,2,96]{0,3,2,1:T(8,128)(2,1)} %bitcast.86, bf16[1024,1536]{1,0:T(8,128)(2,1)} %all-gather.3.cloned.1.call-done), kind=kOutput, calls=%fused_computation.13 | convolution fusion | flops 1207959552 | bytes 5898240 | tf_op jit(solution)/shard_map/td,dcgh->cgth/dot_general | solution.py:372
  94.8 1.0 subtract_convert_fusion.1
  95.8 1.2 fusion.23
  97.0 1.1 pad_maximum_fusion.1.kn_ref
  98.1 0.5 copy.105
  98.6 0.5 copy.106
  99.0 0.3 copy.112
  99.3 1.0 copy.119
  100.3 1.6 pad_maximum_fusion.q_ref
  101.9 0.1 all-to-all-done.1
  102.0 4.3 %all-to-all-start.2 = ((bf16[2,4,256,96]{2,3,0,1:T(8,128)(2,1)}), bf16[2,4,256,96]{2,3,0,1:T(8,128)(2,1)S(1)}, u32[]{:S(2)}, u32[]{:S(2)}) async-start(bf16[2,4,256,96]{2,3,0,1:T(8,128)(2,1)} %copy.119), calls=%async_computation.2 | async-start | bytes 786432 | tf_op jit(solution)/shard_map/all_to_all | solution.py:390
  106.2 36.8 %shard_map.113 = bf16[2,2048,96]{2,1,0:T(8,128)(2,1)} custom-call(s32[1]{0:T(128)} %copy.135.len_ref, bf16[2,2048,96]{2,1,0:T(8,128)(2,1)} %pad_maximum_fusion.q_ref, bf16[4,2,512,96]{3,2,1,0:T(8,128)(2,1)} %get-tuple-element.7.kc_ref, bf16[4,2,512,96]{3,2,1,0:T(8,128)(2,1)} %get-tuple-element.8.vc_ref, bf16[2,1024,96]{2,1,0:T(8,128)(2,1)} %pad_maximum_fusion.1.kn_ref, ...), custom_call_target="tpu_custom_call" | custom-call | flops 4831838208 | bytes 3932160 | tf_op jit(solution)/shard_map/pallas_call | solution.py:303
  143.0 2.2 %copy.113 = bf16[2,2,4,256,96]{3,4,1,0,2:T(8,128)(2,1)} copy(bf16[2,2,4,256,96]{4,3,2,1,0:T(8,128)(2,1)} %bitcast.87) | data formatting | bytes 1572864 | tf_op jit(solution)/shard_map/reshape | solution.py:399
  145.2 4.9 %all-to-all-start = ((bf16[2,2,4,256,96]{3,4,1,0,2:T(8,128)(2,1)}), bf16[2,2,4,256,96]{3,4,1,0,2:T(8,128)(2,1)S(1)}, u32[]{:S(2)}, u32[]{:S(2)}) async-start(bf16[2,2,4,256,96]{3,4,1,0,2:T(8,128)(2,1)} %copy.113), calls=%async_computation | async-start | bytes 1572864 | tf_op jit(solution)/shard_map/all_to_all | solution.py:400
  150.0 0.9 copy.120
  150.9 0.9 copy.121
  151.9 10.5 %all-to-all-done = bf16[2,2,4,256,96]{3,4,1,0,2:T(8,128)(2,1)S(1)} async-done(((bf16[2,2,4,256,96]{3,4,1,0,2:T(8,128)(2,1)}), bf16[2,2,4,256,96]{3,4,1,0,2:T(8,128)(2,1)S(1)}, u32[]{:S(2)}, u32[]{:S(2)}) %all-to-all-start) | async-done | bytes 786464 | tf_op jit(solution)/shard_map/all_to_all | solution.py:400
  162.3 4.6 %fusion.14 = bf16[1,256,1536]{2,1,0:T(8,128)(2,1)} fusion(bf16[4,2,2,96,1536]{4,3,2,1,0:T(8,128)(2,1)} %bitcast.89, bf16[2,2,4,256,96]{3,4,1,0,2:T(8,128)(2,1)S(1)} %all-to-all-done), kind=kOutput, calls=%fused_computation.10 | convolution fusion | flops 1208352768 | bytes 6291456 | tf_op jit(solution)/shard_map/cgsth,scghn->tn/dot_general | solution.py:401
  (29 shorter events, 0.1 us)
Async XLA Ops:
  7.2 1.7 copy-start.10
  7.2 75.5 %all-gather.3.cloned.1.call-start = ((), (), s32[]{:S(2)}) async-start(), calls=%async_computation.3 | async-start | bytes 3932160 | tf_op jit(solution)/shard_map/all_gather | solution.py:339
  9.3 1.3 copy-start.4
  10.5 1.7 copy-start.5
  10.5 151.8 %all-gather.5.cloned.1.call-start = ((), (), s32[]{:S(2)}) async-start(), calls=%async_computation.4 | async-start | bytes 5898240 | tf_op jit(solution)/shard_map/all_gather | solution.py:355
  12.2 1.6 copy-start.6
  12.2 1.6 copy-start.7
  12.2 1.6 copy-start.8
  12.2 1.6 copy-start.9
  82.7 3.1 %copy-start.2 = (f32[1024,48]{1,0:T(8,128)S(1)}, f32[1024,48]{1,0:T(8,128)}, u32[]{:S(2)}) copy-start(f32[1024,48]{1,0:T(8,128)} %copy.110) | copy-start | bytes 589828
  87.5 14.4 %all-to-all-start.1 = ((bf16[2,4,256,96]{2,3,0,1:T(8,128)(2,1)}), bf16[2,4,256,96]{2,3,0,1:T(8,128)(2,1)S(1)}, u32[]{:S(2)}, u32[]{:S(2)}) async-start(bf16[2,4,256,96]{2,3,0,1:T(8,128)(2,1)} %pad_maximum_fusion.2), calls=%async_computation.1 | async-start | bytes 786432 | tf_op jit(solution)/shard_map/all_to_all | solution.py:390
  91.0 4.8 %copy-start = (bf16[1024,1536]{1,0:T(8,128)(2,1)S(1)}, bf16[1024,1536]{1,0:T(8,128)(2,1)}, u32[]{:S(2)}) copy-start(bf16[1024,1536]{1,0:T(8,128)(2,1)} %all-gather.3.cloned.1.call-done) | copy-start | bytes 9437188
  97.0 1.6 copy-start.3
  99.3 2.6 %copy-start.1 = (bf16[2,96,1024]{1,2,0:T(8,128)(2,1)}, bf16[2,96,1024]{1,2,0:T(8,128)(2,1)S(1)}, u32[]{:S(2)}) copy-start(bf16[2,96,1024]{1,2,0:T(8,128)(2,1)S(1)} %copy.112) | copy-start | bytes 1179652
  102.0 43.2 %all-to-all-start.2 = ((bf16[2,4,256,96]{2,3,0,1:T(8,128)(2,1)}), bf16[2,4,256,96]{2,3,0,1:T(8,128)(2,1)S(1)}, u32[]{:S(2)}, u32[]{:S(2)}) async-start(bf16[2,4,256,96]{2,3,0,1:T(8,128)(2,1)} %copy.119), calls=%async_computation.2 | async-start | bytes 786432 | tf_op jit(solution)/shard_map/all_to_all | solution.py:390
  145.2 17.1 %all-to-all-start = ((bf16[2,2,4,256,96]{3,4,1,0,2:T(8,128)(2,1)}), bf16[2,2,4,256,96]{3,4,1,0,2:T(8,128)(2,1)S(1)}, u32[]{:S(2)}, u32[]{:S(2)}) async-start(bf16[2,2,4,256,96]{3,4,1,0,2:T(8,128)(2,1)} %copy.113), calls=%async_computation | async-start | bytes 1572864 | tf_op jit(solution)/shard_map/all_to_all | solution.py:400
Sparse Core Ops, SparseCore 0:
  10.7 56.0 all-gather.2
  75.4 50.9 all-gather.4

commit v17 on v14

--- a/solution.py
+++ b/solution.py
@@ -369,18 +369,14 @@
         )
 
     width = normed_all.shape[1]
-    proj_q = jnp.einsum(
-        "td,dcgh->cgth", normed_all, wq.reshape(width, kv_heads_here, groups, HD),
+    heads_qkv = (q_cols + k_cols + v_cols) // HD
+    proj = jnp.einsum(
+        "td,dnh->nth", normed_all, cols[:, :q_cols + k_cols + v_cols].reshape(width, heads_qkv, HD),
         preferred_element_type=jnp.float32,
     )
-    proj_k = jnp.einsum(
-        "td,dch->cth", normed_all, wk.reshape(width, kv_heads_here, HD),
-        preferred_element_type=jnp.float32,
-    )
-    proj_v = jnp.einsum(
-        "td,dch->cth", normed_all, wv.reshape(width, kv_heads_here, HD),
-        preferred_element_type=jnp.float32,
-    )
+    proj_q = proj[:heads_here].reshape(kv_heads_here, groups, appended, HD)
+    proj_k = proj[heads_here:heads_here + kv_heads_here]
+    proj_v = proj[heads_here + kv_heads_here:]
     query_heads = turn(proj_q).astype(jnp.bfloat16).reshape(kv_heads_here, groups * appended, HD)
     keys_new = turn(proj_k).astype(jnp.bfloat16)
     values_new = proj_v.astype(jnp.bfloat16)

time: 174 us -> 180 us (1.034)
  the two profiles are of different devices: /device:TPU:72 before, /device:TPU:1 now
where the time goes in v17:
time: 180 us; the launch traced here: 179 us
  Pallas kernels  95.3 us (53%)
  local copies, waits for them, and re-layouts  25.6 us (14%)
  between operations  14.9 us (8%)
  starting transfers between devices  11.4 us (6%)
  other arithmetic  10.8 us (6%)
  matrix products  10.6 us (6%)
  waiting for transfers between devices  10.5 us (6%)
    pallas_call x1, Pallas kernels, gather_req(): pl.pallas_call(functools.partial(plane_ring_kernel, planes, runs), out_sh...  57.6 us
    pallas_call x1, Pallas kernels, flash_attention(): pl.pallas_call(functools.partial(flash_kernel, tokens, scale), out_shape=...  37.7 us
    all_to_all x1, waiting for transfers between devices, body(): got = lax.all_to_all(parts, 'kv', split_axis=2, concat_axis=2, tiled=True)  10.5 us
    all_to_all x2, starting transfers between devices, to_tokens(): got = lax.all_to_all(parts, 'kv', split_axis=1, concat_axis=1, tiled=True)  7.08 us
    unnamed x25, local copies, waits for them, and re-layouts  6.21 us
    dot_general x1, matrix products, body(): jnp.einsum('td,dnh->nth', normed_all, cols[:, :q_cols + k_cols + v_cols]....  6.03 us
    concatenate x3, other arithmetic, turn(): jnp.concatenate([first * cosine - second * sine, second * cosine + first...  4.62 us
    dot_general x1, matrix products, body(): jnp.einsum('cgsth,scghn->tn', got, wo_full.reshape(kv_count, kv_heads_her...  4.62 us
  transfers between devices with their start and end apart: 5, of which 1 were waited for; matrix products, arithmetic and copies ran while one was open for 20% of the time, Pallas kernels for 53%

profile of v17, /device:TPU:1, one launch (start us, length us, event | category | flops | bytes accessed | tf_op | source)
XLA Modules:
  0.0 179.2 jit_solution(7608843967422849502)
XLA Ops:
  7.2 0.0 all-gather.3.cloned.1.call-start
  7.2 0.8 reshape.200
  8.0 1.4 copy.56
  9.4 0.2 multiply_reduce_fusion
  9.7 0.3 fusion.16
  10.0 0.0 copy-start.2
  10.0 0.1 copy.57
  10.0 1.2 copy.58
  11.2 0.0 all-gather.3.cloned.1.call-update
  11.2 0.0 all-gather.5.cloned.1.call-start
  11.3 0.3 copy.51
  11.6 1.3 copy.52
  12.9 0.0 copy-start.9
  12.9 0.3 copy.53
  13.2 1.3 copy.54
  14.5 0.7 concatenate.24.src_ref
  15.2 57.6 %shard_map.112 = (bf16[8,8,24,1152]{3,2,1,0:T(8,128)(2,1)}, bf16[4,2,512,96]{3,2,1,0:T(8,128)(2,1)}, bf16[4,2,512,96]{3,2,1,0:T(8,128)(2,1)}) custom-call(bf16[24,1152]{1,0:T(8,128)(2,1)} %concatenate.24.src_ref, bf16[4,2,512,96]{3,2,1,0:T(8,128)(2,1)} %bitcast.57, bf16[4,2,512,96]{3,2,1,0:T(8,128)(2,1)} %bitcast.58), custom_call_target="tpu_custom_call" | custom-call | tf_op jit(solution)/shard_map/pallas_call | solution.py:198
  72.9 1.4 slice.43
  74.3 1.2 copy.61
  75.4 0.0 all-gather.5.cloned.1.call-update
  75.5 1.8 %slice.36 = bf16[1536,768]{1,0:T(8,128)(2,1)S(1)} slice(bf16[1536,1152]{1,0:T(8,128)(2,1)} %bitcast.60), slice={[0:1536], [0:768]} | slice | bytes 4718592 | tf_op jit(solution)/shard_map/slice | solution.py:374
  77.9 2.5 %copy.55 = bf16[1536,768]{0,1:T(8,128)(2,1)} copy(bf16[1536,768]{1,0:T(8,128)(2,1)S(1)} %slice.36) | data formatting | bytes 4718592 | tf_op jit(solution)/shard_map/slice | solution.py:374
  80.4 1.9 %multiply_cosine_fusion = (f32[1024,48]{1,0:T(8,128)S(1)}, f32[1024,48]{1,0:T(8,128)S(1)}) fusion(f32[48]{0:T(128)S(1)} %negate_power_fusion, f32[1024]{0:T(1024)S(1)} %add_convert_fusion.2), kind=kLoop, calls=%fused_computation.19 | loop fusion | flops 49152 | bytes 397504 | tf_op jit(solution)/shard_map/cos | solution.py:361
  82.3 0.0 all-gather.3.cloned.1.call-done
  82.4 6.0 %fusion.13 = f32[8,1024,96]{2,1,0:T(8,128)S(1)} fusion(bf16[1536,8,96]{0,2,1:T(8,128)(2,1)} %bitcast.64, bf16[1024,1536]{1,0:T(8,128)(2,1)} %all-gather.3.cloned.1.call-done), kind=kOutput, calls=%fused_computation.7 | convolution fusion | flops 2415919104 | bytes 8650752 | tf_op jit(solution)/shard_map/td,dnh->nth/dot_general | solution.py:373
  88.4 0.1 slice.53.vn_ref
  88.5 1.9 %copy-done = f32[8,1024,96]{2,1,0:T(8,128)} copy-done((f32[8,1024,96]{2,1,0:T(8,128)}, f32[8,1024,96]{2,1,0:T(8,128)S(1)}, u32[]{:S(2)}) %copy-start) | copy-done | bytes 3145752
  90.4 0.2 copy-done.1
  90.6 1.0 copy.66
  91.6 3.4 %all-to-all-start.2 = ((bf16[2,4,256,96]{2,3,0,1:T(8,128)(2,1)}), bf16[2,4,256,96]{2,3,0,1:T(8,128)(2,1)S(1)}, u32[]{:S(2)}, u32[]{:S(2)}) async-start(bf16[2,4,256,96]{2,3,0,1:T(8,128)(2,1)} %copy.66), calls=%async_computation.2 | async-start | bytes 786432 | tf_op jit(solution)/shard_map/all_to_all | solution.py:386
  95.0 3.0 %subtract_convert_fusion.1 = (bf16[2,1024,48]{2,1,0:T(8,128)(2,1)}, bf16[2,1024,48]{2,1,0:T(8,128)(2,1)}) fusion(f32[8,1024,96]{2,1,0:T(8,128)} %copy-done, f32[1024,48]{1,0:T(8,128)S(1)} %get-tuple-element.23, f32[1024,48]{1,0:T(8,128)S(1)} %get-tuple-element.22), kind=kLoop, calls=%fused_computation.15 | loop fusion | flops 786432 | bytes 1572864 | tf_op jit(solution)/shard_map/convert.7
  98.0 2.1 %copy.65 = bf16[2,4,256,48]{2,3,0,1:T(8,128)(2,1)} copy(bf16[2,4,256,48]{3,2,1,0:T(8,128)(2,1)} %bitcast.54) | data formatting | bytes 393216 | tf_op jit(solution)/shard_map/concatenate | solution.py:367
  100.1 1.9 %copy.64 = bf16[2,4,256,48]{2,3,0,1:T(8,128)(2,1)} copy(bf16[2,4,256,48]{3,2,1,0:T(8,128)(2,1)} %bitcast.53) | data formatting | bytes 393216 | tf_op jit(solution)/shard_map/concatenate | solution.py:367
  102.0 2.3 %pad_maximum_fusion.1.kn_ref = bf16[2,1024,96]{2,1,0:T(8,128)(2,1)} fusion(bf16[2,1024,48]{2,1,0:T(8,128)(2,1)} %get-tuple-element.19, bf16[2,1024,48]{2,1,0:T(8,128)(2,1)} %get-tuple-element.18), kind=kLoop, calls=%fused_computation.20 | loop fusion | flops 786432 | bytes 786432 | tf_op jit(solution)/shard_map/concatenate | solution.py:367
  104.3 0.7 subtract_convert_fusion
  105.0 0.2 copy-done.4
  105.2 0.1 copy-done.5
  105.3 0.8 pad_maximum_fusion.2
  106.1 1.6 pad_maximum_fusion.q_ref
  107.6 0.0 all-to-all-done.2
  107.6 3.6 %all-to-all-start.1 = ((bf16[2,4,256,96]{2,3,0,1:T(8,128)(2,1)}), bf16[2,4,256,96]{2,3,0,1:T(8,128)(2,1)S(1)}, u32[]{:S(2)}, u32[]{:S(2)}) async-start(bf16[2,4,256,96]{2,3,0,1:T(8,128)(2,1)} %pad_maximum_fusion.2), calls=%async_computation.1 | async-start | bytes 786432 | tf_op jit(solution)/shard_map/all_to_all | solution.py:386
  111.3 37.7 %shard_map.113 = bf16[2,2048,96]{2,1,0:T(8,128)(2,1)} custom-call(s32[1]{0:T(128)} %copy.81.len_ref, bf16[2,2048,96]{2,1,0:T(8,128)(2,1)} %pad_maximum_fusion.q_ref, bf16[4,2,512,96]{3,2,1,0:T(8,128)(2,1)} %get-tuple-element.7.kc_ref, bf16[4,2,512,96]{3,2,1,0:T(8,128)(2,1)} %get-tuple-element.8.vc_ref, bf16[2,1024,96]{2,1,0:T(8,128)(2,1)} %pad_maximum_fusion.1.kn_ref, ...), custom_call_target="tpu_custom_call" | custom-call | flops 4831838208 | bytes 3932160 | tf_op jit(solution)/shard_map/pallas_call | solution.py:303
  149.0 2.2 %copy.60 = bf16[2,2,4,256,96]{3,4,1,0,2:T(8,128)(2,1)} copy(bf16[2,2,4,256,96]{4,3,2,1,0:T(8,128)(2,1)} %bitcast.68) | data formatting | bytes 1572864 | tf_op jit(solution)/shard_map/reshape | solution.py:395
  151.2 4.3 %all-to-all-start = ((bf16[2,2,4,256,96]{3,4,1,0,2:T(8,128)(2,1)}), bf16[2,2,4,256,96]{3,4,1,0,2:T(8,128)(2,1)S(1)}, u32[]{:S(2)}, u32[]{:S(2)}) async-start(bf16[2,2,4,256,96]{3,4,1,0,2:T(8,128)(2,1)} %copy.60), calls=%async_computation | async-start | bytes 1572864 | tf_op jit(solution)/shard_map/all_to_all | solution.py:396
  155.5 0.9 copy.68
  156.4 0.9 copy.67
  157.3 10.5 %all-to-all-done = bf16[2,2,4,256,96]{3,4,1,0,2:T(8,128)(2,1)S(1)} async-done(((bf16[2,2,4,256,96]{3,4,1,0,2:T(8,128)(2,1)}), bf16[2,2,4,256,96]{3,4,1,0,2:T(8,128)(2,1)S(1)}, u32[]{:S(2)}, u32[]{:S(2)}) %all-to-all-start) | async-done | bytes 786464 | tf_op jit(solution)/shard_map/all_to_all | solution.py:396
  167.7 4.6 %fusion.10 = bf16[1,256,1536]{2,1,0:T(8,128)(2,1)} fusion(bf16[4,2,2,96,1536]{4,3,2,1,0:T(8,128)(2,1)} %bitcast.69, bf16[2,2,4,256,96]{3,4,1,0,2:T(8,128)(2,1)S(1)} %all-to-all-done), kind=kOutput, calls=%fused_computation.6 | convolution fusion | flops 1208352768 | bytes 6291456 | tf_op jit(solution)/shard_map/cgsth,scghn->tn/dot_general | solution.py:397
  (21 shorter events, 0.1 us)
Async XLA Ops:
  7.2 75.2 %all-gather.3.cloned.1.call-start = ((), (), s32[]{:S(2)}) async-start(), calls=%async_computation.3 | async-start | bytes 3932160 | tf_op jit(solution)/shard_map/all_gather | solution.py:339
  10.0 1.3 copy-start.2
  11.2 1.7 copy-start.3
  11.2 156.5 %all-gather.5.cloned.1.call-start = ((), (), s32[]{:S(2)}) async-start(), calls=%async_computation.4 | async-start | bytes 5898240 | tf_op jit(solution)/shard_map/all_gather | solution.py:355
  12.9 1.6 copy-start.6
  12.9 1.6 copy-start.7
  12.9 1.6 copy-start.8
  12.9 1.6 copy-start.9
  88.4 2.0 %copy-start = (f32[8,1024,96]{2,1,0:T(8,128)}, f32[8,1024,96]{2,1,0:T(8,128)S(1)}, u32[]{:S(2)}) copy-start(f32[8,1024,96]{2,1,0:T(8,128)S(1)} %fusion.13) | copy-start | bytes 9437188
  88.5 2.1 %copy-start.1 = (bf16[2,1024,96]{2,1,0:T(8,128)(2,1)}, bf16[2,1024,96]{2,1,0:T(8,128)(2,1)S(1)}, u32[]{:S(2)}) copy-start(bf16[2,1024,96]{2,1,0:T(8,128)(2,1)S(1)} %slice.53.vn_ref) | copy-start | bytes 1179652
  91.6 16.1 %all-to-all-start.2 = ((bf16[2,4,256,96]{2,3,0,1:T(8,128)(2,1)}), bf16[2,4,256,96]{2,3,0,1:T(8,128)(2,1)S(1)}, u32[]{:S(2)}, u32[]{:S(2)}) async-start(bf16[2,4,256,96]{2,3,0,1:T(8,128)(2,1)} %copy.66), calls=%async_computation.2 | async-start | bytes 786432 | tf_op jit(solution)/shard_map/all_to_all | solution.py:386
  98.0 6.2 %slice-start = ((f32[8,1024,96]{2,1,0:T(8,128)}), f32[4,1024,96]{2,1,0:T(8,128)S(1)}, s32[]{:S(2)}) async-start(f32[8,1024,96]{2,1,0:T(8,128)} %copy-done), calls=%async_computation.5 | async-start | bytes 4194304 | tf_op jit(solution)/shard_map/slice | solution.py:377
  104.3 0.9 copy-start.4
  104.3 1.0 copy-start.5
  107.6 43.5 %all-to-all-start.1 = ((bf16[2,4,256,96]{2,3,0,1:T(8,128)(2,1)}), bf16[2,4,256,96]{2,3,0,1:T(8,128)(2,1)S(1)}, u32[]{:S(2)}, u32[]{:S(2)}) async-start(bf16[2,4,256,96]{2,3,0,1:T(8,128)(2,1)} %pad_maximum_fusion.2), calls=%async_computation.1 | async-start | bytes 786432 | tf_op jit(solution)/shard_map/all_to_all | solution.py:386
  151.2 16.6 %all-to-all-start = ((bf16[2,2,4,256,96]{3,4,1,0,2:T(8,128)(2,1)}), bf16[2,2,4,256,96]{3,4,1,0,2:T(8,128)(2,1)S(1)}, u32[]{:S(2)}, u32[]{:S(2)}) async-start(bf16[2,2,4,256,96]{3,4,1,0,2:T(8,128)(2,1)} %copy.60), calls=%async_computation | async-start | bytes 1572864 | tf_op jit(solution)/shard_map/all_to_all | solution.py:396
Sparse Core Ops, SparseCore 0:
  11.3 56.0 all-gather.2
  75.6 50.9 all-gather.4

commit v18 on v14

--- a/solution.py
+++ b/solution.py
@@ -152,8 +152,9 @@
                    kv_recv.at[which, step - 1], (me, peer)).start()
         return carry
 
-    lax.fori_loop(1, kv_count, send_kv, 0)
     for k in range(1, max(right_of + left_of) + 1):
+        if k == 2:
+            lax.fori_loop(1, kv_count, send_kv, 0)
         for h in range(split):
             if k <= right_of[h]:
                 z_from = lax.rem(z_me + runs - k, runs)

time: 174 us -> 175 us (level)
  the two profiles are of different devices: /device:TPU:72 before, /device:TPU:1 now
where the time goes in v18:
time: 175 us
  Pallas kernels  95.3 us (54%)
  local copies, waits for them, and re-layouts  22.3 us (13%)
  between operations  15 us (9%)
  matrix products  12.7 us (7%)
  starting transfers between devices  12.6 us (7%)
  waiting for transfers between devices  10.6 us (6%)
  other arithmetic  6.18 us (4%)
    pallas_call x1, Pallas kernels, gather_req(): pl.pallas_call(functools.partial(plane_ring_kernel, planes, runs), out_sh...  57.6 us
    pallas_call x1, Pallas kernels, flash_attention(): pl.pallas_call(functools.partial(flash_kernel, tokens, scale), out_shape=...  37.7 us
    all_to_all x1, waiting for transfers between devices, body(): got = lax.all_to_all(parts, 'kv', split_axis=2, concat_axis=2, tiled=True)  10.5 us
    all_to_all x2, starting transfers between devices, to_tokens(): got = lax.all_to_all(parts, 'kv', split_axis=1, concat_axis=1, tiled=True)  7.72 us
    all_to_all x1, starting transfers between devices, body(): got = lax.all_to_all(parts, 'kv', split_axis=2, concat_axis=2, tiled=True)  4.85 us
    dot_general x1, matrix products, body(): jnp.einsum('cgsth,scghn->tn', got, wo_full.reshape(kv_count, kv_heads_her...  4.62 us
    unnamed x27, local copies, waits for them, and re-layouts  3.85 us
    dot_general x1, matrix products, body(): jnp.einsum('td,dcgh->cgth', normed_all, wq.reshape(width, kv_heads_here,...  3.8 us
  transfers between devices with their start and end apart: 5, of which 2 were waited for; matrix products, arithmetic and copies ran while one was open for 19% of the time, Pallas kernels for 55%

profile of v18, /device:TPU:1, one launch (start us, length us, event | category | flops | bytes accessed | tf_op | source)
XLA Modules:
  0.0 174.7 jit_solution(5943582067050002916)
XLA Ops:
  7.2 0.0 all-gather.3.cloned.1.call-start
  7.2 1.4 copy.102
  8.6 0.2 multiply_reduce_fusion
  8.9 0.1 reshape.204
  9.0 0.3 fusion.26
  9.3 0.1 copy.103
  9.4 1.2 copy.104
  10.5 0.0 all-gather.5.cloned.1.call-start
  10.6 0.3 copy.97
  10.9 1.3 copy.98
  12.2 0.3 copy.99
  12.5 1.3 copy.100
  13.9 0.7 concatenate.24.src_ref
  14.6 57.6 %shard_map.112 = (bf16[8,8,24,1152]{3,2,1,0:T(8,128)(2,1)}, bf16[4,2,512,96]{3,2,1,0:T(8,128)(2,1)}, bf16[4,2,512,96]{3,2,1,0:T(8,128)(2,1)}) custom-call(bf16[24,1152]{1,0:T(8,128)(2,1)} %concatenate.24.src_ref, bf16[4,2,512,96]{3,2,1,0:T(8,128)(2,1)} %bitcast.74, bf16[4,2,512,96]{3,2,1,0:T(8,128)(2,1)} %bitcast.76), custom_call_target="tpu_custom_call" | custom-call | tf_op jit(solution)/shard_map/pallas_call | solution.py:199
  72.2 1.9 %fusion.29 = (bf16[1536,384]{1,0:T(8,128)(2,1)S(1)}, bf16[1536,384]{1,0:T(8,128)(2,1)S(1)}) fusion(bf16[1536,1152]{1,0:T(8,128)(2,1)} %bitcast.72), kind=kLoop, calls=%fused_computation.31 | loop fusion | bytes 4718592 | tf_op jit(solution)/shard_map/slice | solution.py:351
  74.1 1.2 copy.114
  75.3 1.9 %fusion.28 = (bf16[1536,192]{1,0:T(8,128)(2,1)S(1)}, bf16[1536,192]{1,0:T(8,128)(2,1)S(1)}) fusion(bf16[1536,1152]{1,0:T(8,128)(2,1)} %bitcast.73), kind=kLoop, calls=%fused_computation.30 | loop fusion | bytes 2359296 | tf_op jit(solution)/shard_map/slice | solution.py:353
  77.2 1.1 copy.107
  78.9 0.8 multiply_cosine_fusion
  79.7 0.2 copy.109
  79.9 1.0 copy.110
  80.9 1.5 copy.101
  82.4 0.3 copy.111
  82.7 0.0 all-gather.3.cloned.1.call-done
  82.7 3.1 %fusion.20 = f32[2,1024,96]{2,1,0:T(8,128)S(1)} fusion(bf16[1536,2,96]{0,2,1:T(8,128)(2,1)} %bitcast.88, bf16[1024,1536]{1,0:T(8,128)(2,1)} %all-gather.3.cloned.1.call-done), kind=kOutput, calls=%fused_computation.14 | convolution fusion | flops 603979776 | bytes 4521984 | tf_op jit(solution)/shard_map/td,dch->cth/dot_general | solution.py:377
  85.9 0.5 subtract_convert_fusion
  86.3 0.2 copy.117
  86.5 0.2 copy.118
  86.7 0.8 pad_maximum_fusion.2
  87.5 3.5 %all-to-all-start.1 = ((bf16[2,4,256,96]{2,3,0,1:T(8,128)(2,1)}), bf16[2,4,256,96]{2,3,0,1:T(8,128)(2,1)S(1)}, u32[]{:S(2)}, u32[]{:S(2)}) async-start(bf16[2,4,256,96]{2,3,0,1:T(8,128)(2,1)} %pad_maximum_fusion.2), calls=%async_computation.1 | async-start | bytes 786432 | tf_op jit(solution)/shard_map/all_to_all | solution.py:391
  91.0 3.8 %fusion.17 = f32[2,2,1024,96]{2,3,1,0:T(8,128)S(1)} fusion(bf16[1536,2,2,96]{0,3,2,1:T(8,128)(2,1)} %bitcast.86, bf16[1024,1536]{1,0:T(8,128)(2,1)} %all-gather.3.cloned.1.call-done), kind=kOutput, calls=%fused_computation.13 | convolution fusion | flops 1207959552 | bytes 5898240 | tf_op jit(solution)/shard_map/td,dcgh->cgth/dot_general | solution.py:373
  94.8 1.0 subtract_convert_fusion.1
  95.8 1.2 fusion.23
  97.0 1.1 pad_maximum_fusion.1.kn_ref
  98.1 0.5 copy.105
  98.6 0.5 copy.106
  99.0 0.3 copy.112
  99.3 1.0 copy.119
  100.3 1.6 pad_maximum_fusion.q_ref
  101.9 0.1 all-to-all-done.1
  102.0 4.3 %all-to-all-start.2 = ((bf16[2,4,256,96]{2,3,0,1:T(8,128)(2,1)}), bf16[2,4,256,96]{2,3,0,1:T(8,128)(2,1)S(1)}, u32[]{:S(2)}, u32[]{:S(2)}) async-start(bf16[2,4,256,96]{2,3,0,1:T(8,128)(2,1)} %copy.119), calls=%async_computation.2 | async-start | bytes 786432 | tf_op jit(solution)/shard_map/all_to_all | solution.py:391
  106.2 37.7 %shard_map.113 = bf16[2,2048,96]{2,1,0:T(8,128)(2,1)} custom-call(s32[1]{0:T(128)} %copy.135.len_ref, bf16[2,2048,96]{2,1,0:T(8,128)(2,1)} %pad_maximum_fusion.q_ref, bf16[4,2,512,96]{3,2,1,0:T(8,128)(2,1)} %get-tuple-element.7.kc_ref, bf16[4,2,512,96]{3,2,1,0:T(8,128)(2,1)} %get-tuple-element.8.vc_ref, bf16[2,1024,96]{2,1,0:T(8,128)(2,1)} %pad_maximum_fusion.1.kn_ref, ...), custom_call_target="tpu_custom_call" | custom-call | flops 4831838208 | bytes 3932160 | tf_op jit(solution)/shard_map/pallas_call | solution.py:304
  143.9 2.2 %copy.113 = bf16[2,2,4,256,96]{3,4,1,0,2:T(8,128)(2,1)} copy(bf16[2,2,4,256,96]{4,3,2,1,0:T(8,128)(2,1)} %bitcast.87) | data formatting | bytes 1572864 | tf_op jit(solution)/shard_map/reshape | solution.py:400
  146.1 4.9 %all-to-all-start = ((bf16[2,2,4,256,96]{3,4,1,0,2:T(8,128)(2,1)}), bf16[2,2,4,256,96]{3,4,1,0,2:T(8,128)(2,1)S(1)}, u32[]{:S(2)}, u32[]{:S(2)}) async-start(bf16[2,2,4,256,96]{3,4,1,0,2:T(8,128)(2,1)} %copy.113), calls=%async_computation | async-start | bytes 1572864 | tf_op jit(solution)/shard_map/all_to_all | solution.py:401
  150.9 0.9 copy.120
  151.9 0.9 copy.121
  152.8 10.5 %all-to-all-done = bf16[2,2,4,256,96]{3,4,1,0,2:T(8,128)(2,1)S(1)} async-done(((bf16[2,2,4,256,96]{3,4,1,0,2:T(8,128)(2,1)}), bf16[2,2,4,256,96]{3,4,1,0,2:T(8,128)(2,1)S(1)}, u32[]{:S(2)}, u32[]{:S(2)}) %all-to-all-start) | async-done | bytes 786464 | tf_op jit(solution)/shard_map/all_to_all | solution.py:401
  163.2 4.6 %fusion.14 = bf16[1,256,1536]{2,1,0:T(8,128)(2,1)} fusion(bf16[4,2,2,96,1536]{4,3,2,1,0:T(8,128)(2,1)} %bitcast.89, bf16[2,2,4,256,96]{3,4,1,0,2:T(8,128)(2,1)S(1)} %all-to-all-done), kind=kOutput, calls=%fused_computation.10 | convolution fusion | flops 1208352768 | bytes 6291456 | tf_op jit(solution)/shard_map/cgsth,scghn->tn/dot_general | solution.py:402
  (29 shorter events, 0.1 us)
Async XLA Ops:
  7.2 1.7 copy-start.10
  7.2 75.5 %all-gather.3.cloned.1.call-start = ((), (), s32[]{:S(2)}) async-start(), calls=%async_computation.3 | async-start | bytes 3932160 | tf_op jit(solution)/shard_map/all_gather | solution.py:340
  9.3 1.3 copy-start.4
  10.5 1.7 copy-start.5
  10.5 152.7 %all-gather.5.cloned.1.call-start = ((), (), s32[]{:S(2)}) async-start(), calls=%async_computation.4 | async-start | bytes 5898240 | tf_op jit(solution)/shard_map/all_gather | solution.py:356
  12.2 1.6 copy-start.6
  12.2 1.6 copy-start.7
  12.2 1.6 copy-start.8
  12.2 1.6 copy-start.9
  82.7 3.1 %copy-start.2 = (f32[1024,48]{1,0:T(8,128)S(1)}, f32[1024,48]{1,0:T(8,128)}, u32[]{:S(2)}) copy-start(f32[1024,48]{1,0:T(8,128)} %copy.110) | copy-start | bytes 589828
  87.5 14.4 %all-to-all-start.1 = ((bf16[2,4,256,96]{2,3,0,1:T(8,128)(2,1)}), bf16[2,4,256,96]{2,3,0,1:T(8,128)(2,1)S(1)}, u32[]{:S(2)}, u32[]{:S(2)}) async-start(bf16[2,4,256,96]{2,3,0,1:T(8,128)(2,1)} %pad_maximum_fusion.2), calls=%async_computation.1 | async-start | bytes 786432 | tf_op jit(solution)/shard_map/all_to_all | solution.py:391
  91.0 4.8 %copy-start = (bf16[1024,1536]{1,0:T(8,128)(2,1)S(1)}, bf16[1024,1536]{1,0:T(8,128)(2,1)}, u32[]{:S(2)}) copy-start(bf16[1024,1536]{1,0:T(8,128)(2,1)} %all-gather.3.cloned.1.call-done) | copy-start | bytes 9437188
  97.0 1.6 copy-start.3
  99.3 2.6 %copy-start.1 = (bf16[2,96,1024]{1,2,0:T(8,128)(2,1)}, bf16[2,96,1024]{1,2,0:T(8,128)(2,1)S(1)}, u32[]{:S(2)}) copy-start(bf16[2,96,1024]{1,2,0:T(8,128)(2,1)S(1)} %copy.112) | copy-start | bytes 1179652
  102.0 44.1 %all-to-all-start.2 = ((bf16[2,4,256,96]{2,3,0,1:T(8,128)(2,1)}), bf16[2,4,256,96]{2,3,0,1:T(8,128)(2,1)S(1)}, u32[]{:S(2)}, u32[]{:S(2)}) async-start(bf16[2,4,256,96]{2,3,0,1:T(8,128)(2,1)} %copy.119), calls=%async_computation.2 | async-start | bytes 786432 | tf_op jit(solution)/shard_map/all_to_all | solution.py:391
  146.1 17.1 %all-to-all-start = ((bf16[2,2,4,256,96]{3,4,1,0,2:T(8,128)(2,1)}), bf16[2,2,4,256,96]{3,4,1,0,2:T(8,128)(2,1)S(1)}, u32[]{:S(2)}, u32[]{:S(2)}) async-start(bf16[2,2,4,256,96]{3,4,1,0,2:T(8,128)(2,1)} %copy.113), calls=%async_computation | async-start | bytes 1572864 | tf_op jit(solution)/shard_map/all_to_all | solution.py:401
Sparse Core Ops, SparseCore 0:
  10.7 44.0 all-gather.2
  75.4 50.9 all-gather.4
